TPU v7x, 512 devices: a whole 4x4x16 slice. The times are simulated.
512 devices in a mesh: gx: 32 (over x, y, core), gy: 16 (over z).
Axes of the slice: x: 4, y: 4, z: 16, core: 2. Of those that a mesh axis runs over, the one named last changes fastest.
Arguments:
- conductance: float32 [16, 256, 2048], P(None, 'gx', 'gy'), may hold values from 0.2 to 5
- labels: int32 [16, 256, 2048], P(None, 'gx', 'gy'), may hold values from 0 to 2, as said below
- cotangent: float32 [2, 16, 256, 2048], P(None, None, 'gx', 'gy')
- saved: float32 [2, 16, 256, 2048], P(None, None, 'gx', 'gy'), may hold values from 0 to 1
Outputs:
- adjoint: float32 [2, 16, 256, 2048], P(None, None, 'gx', 'gy')
- gradient: float32 [16, 256, 2048], P(None, 'gx', 'gy')
Inputs may be any that keep to these rules, and one draw needn't show every extreme that they name: `labels`: 0 marks an unseeded voxel, 1 or 2 the class of a seed.
All inputs are finite; a program needn't handle non-finite values.
Results may differ from a plain program's by a relative error of at most 0.0003.
Values sent between devices are 32-bit elements; how exact they have to be, the bound alone decides.
No kernel may reach another device: no remote copies, remote signals or barrier semaphores. Data moves between devices by JAX's collectives and lax.ppermute only.
A program may use at most 64 MiB of HBM per device.

v0:
```python
import jax
import jax.numpy as jnp
from jax import lax
from jax.sharding import PartitionSpec as P

ITERS = 3


prior_strength = 1.0


def extended(x, sides, width):
    for axis, dim in sides:
        size, length = (lax.axis_size(axis), x.shape[dim])
        up = [(i, (i + 1) % size) for i in range(size - 1)]
        down = [(j, i) for i, j in up]
        last = lax.slice_in_dim(x, length - width, length, axis=dim)
        initial = lax.slice_in_dim(x, 0, width, axis=dim)
        before = lax.ppermute(last, axis, up)
        after = lax.ppermute(initial, axis, down)
        x = jnp.concatenate([before, x, after], axis=dim)
    return x


def potentials(labels, saved):
    classes = jnp.arange(1, 3, dtype=jnp.int32)[:, None, None, None]
    tagged = labels[None]
    return jnp.where(tagged == classes, 1.0, jnp.where(tagged > 0, 0.0, saved))


def edge_validity(row_count, col_count, depth):
    row_pos = lax.axis_index("gx") * row_count + jnp.arange(row_count, dtype=jnp.int32)
    col_pos = lax.axis_index("gy") * col_count + jnp.arange(col_count, dtype=jnp.int32)
    depth_pos = jnp.arange(depth, dtype=jnp.int32)
    total_rows = row_count * lax.axis_size("gx")
    total_cols = col_count * lax.axis_size("gy")
    return (
        (row_pos > 0).astype(jnp.float32)[None, :, None],
        (row_pos < total_rows - 1).astype(jnp.float32)[None, :, None],
        (col_pos > 0).astype(jnp.float32)[None, None, :],
        (col_pos < total_cols - 1).astype(jnp.float32)[None, None, :],
        (depth_pos > 0).astype(jnp.float32)[:, None, None],
        (depth_pos < depth - 1).astype(jnp.float32)[:, None, None],
    )


def side_slices(padded):
    return (
        padded[..., :-2, 1:-1],
        padded[..., 2:, 1:-1],
        padded[..., 1:-1, :-2],
        padded[..., 1:-1, 2:],
    )


def depth_neighbours(input_vector):
    depth_axis = input_vector.ndim - 3
    depth = input_vector.shape[depth_axis]
    widths = [(0, 0)] * input_vector.ndim
    widths[depth_axis] = (1, 1)
    padded = jnp.pad(input_vector, widths)
    lower = lax.slice_in_dim(padded, 0, depth, axis=depth_axis)
    upper = lax.slice_in_dim(padded, 2, depth + 2, axis=depth_axis)
    return (lower, upper)


def apply_operator(input_vector, unlabelled_mask, weight_field):
    mask_applied = unlabelled_mask * input_vector
    padded = extended(mask_applied, (("gx", 2), ("gy", 3)), 1)
    neighbours = side_slices(padded) + depth_neighbours(mask_applied)
    graph_laplacian = jnp.zeros_like(mask_applied)
    for weight, neighbour in zip(weight_field, neighbours):
        graph_laplacian = graph_laplacian + weight * (mask_applied - neighbour)
    return (
        unlabelled_mask * (prior_strength * mask_applied + graph_laplacian)
        + (1.0 - unlabelled_mask) * input_vector
    )


def class_sum(first_vec, second_vec):
    return jnp.sum(first_vec * second_vec, axis=(1, 2, 3))


def expand(scalars):
    return scalars[:, None, None, None]


def global_norm(solver_residual):
    return lax.psum(class_sum(solver_residual, solver_residual), ("gx", "gy"))


def per_device(conductance, labels, cotangent, saved):
    depth, row_count, col_count = conductance.shape
    validity = edge_validity(row_count, col_count, depth)
    potential = potentials(labels, saved)
    unlabelled_mask = (labels == 0).astype(jnp.float32)[None]
    solver_residual = unlabelled_mask * cotangent
    cond_pad = extended(conductance, (("gx", 1), ("gy", 2)), 1)
    cond_neighbours = side_slices(cond_pad) + depth_neighbours(conductance)
    weight_field = [
        0.5 * (conductance + neighbour) * valid_edge
        for neighbour, valid_edge in zip(cond_neighbours, validity)
    ]
    adjoint = jnp.zeros_like(solver_residual)
    search_direction = solver_residual
    norm_now = global_norm(solver_residual)
    for iteration in range(ITERS):
        operator_result = apply_operator(search_direction, unlabelled_mask, weight_field)
        step_size = norm_now / lax.psum(class_sum(search_direction, operator_result), ("gx", "gy"))
        adjoint = adjoint + expand(step_size) * search_direction
        solver_residual = solver_residual - expand(step_size) * operator_result
        if iteration + 1 < ITERS:
            norm_next = global_norm(solver_residual)
            search_direction = solver_residual + expand(norm_next / norm_now) * search_direction
            norm_now = norm_next
    joined = extended(jnp.concatenate((adjoint, potential), axis=0), (("gx", 2), ("gy", 3)), 1)
    adj_pad = joined[:2]
    pot_pad = joined[2:]
    adj_neighbours = side_slices(adj_pad) + depth_neighbours(adjoint)
    pot_neighbours = side_slices(pot_pad) + depth_neighbours(potential)
    gradient = jnp.zeros_like(conductance)
    for adj_nb, pot_nb, valid_edge in zip(adj_neighbours, pot_neighbours, validity):
        gradient = (
            gradient - jnp.sum((adjoint - adj_nb) * (potential - pot_nb), axis=0) * valid_edge
        )
    return (adjoint, 0.5 * gradient)


def solution(mesh):
    return jax.shard_map(
        per_device,
        mesh=mesh,
        in_specs=(
            P(None, "gx", "gy"),
            P(None, "gx", "gy"),
            P(None, None, "gx", "gy"),
            P(None, None, "gx", "gy"),
        ),
        out_specs=(P(None, None, "gx", "gy"), P(None, "gx", "gy")),
        check_vma=False,
    )
```

profile of v0, /device:TPU:1, one launch (start us, length us, event | category | flops | bytes accessed | tf_op | source)
XLA Modules:
  0.0 619.8 jit_solution(12101957498100516942)
XLA Ops:
  0.6 0.9 broadcast_compare_fusion
  1.5 0.0 copy-done.1
  1.6 0.0 copy-start.2
  1.6 4.7 collective-permute-start.1
  6.4 5.5 collective-permute-start.3
  11.9 1.9 collective-permute-start
  13.8 2.4 collective-permute-start.2
  16.3 0.1 fusion.83
  16.4 0.0 collective-permute-done
  16.4 2.4 collective-permute-done.2
  18.8 0.1 fusion.102
  18.9 1.7 collective-permute-start.4
  20.6 1.3 collective-permute-start.6
  21.9 0.0 collective-permute-done.1
  21.9 0.1 pad_maximum_fusion.1
  22.0 0.1 fusion.99
  22.1 4.2 collective-permute-start.5
  26.3 1.3 collective-permute-start.7
  27.7 0.2 fusion.89
  27.8 3.5 collective-permute-done.5
  31.4 4.1 collective-permute-done.7
  35.5 0.4 multiply_reduce_fusion.3
  35.9 112.1 %all-reduce.6 = (f32[2]{0:T(128)S(1)}, f32[2]{0:T(128)S(1)}) all-reduce(f32[2]{0:T(128)S(1)} %get-tuple-element.9, f32[2]{0:T(128)S(1)} %get-tuple-element.8), channel_id=1, replica_groups=mesh['gx'=32,'gy'=16] {'gx','gy'}, use_global_device_ids=true, to_apply=%region_1.2 | all-reduce | flops 4 | bytes 32 | tf_op jit(solution)/shard_map/psum | solution.py:89
  148.0 0.2 multiply_reduce_fusion.2
  148.2 98.7 %psum.44 = f32[2]{0:T(128)S(1)} all-reduce(f32[2]{0:T(128)S(1)} %get-tuple-element.18), channel_id=1, replica_groups=mesh['gx'=32,'gy'=16] {'gx','gy'}, use_global_device_ids=true, to_apply=%region_5.6 | all-reduce | flops 2 | bytes 16 | tf_op jit(solution)/shard_map/psum | solution.py:89
  246.8 0.1 broadcast_multiply_fusion.1
  246.9 3.4 collective-permute-start.8
  250.4 1.9 collective-permute-start.9
  252.3 3.1 collective-permute-done.9
  255.5 0.1 fusion.98
  255.6 3.7 collective-permute-start.10
  259.3 1.3 collective-permute-start.11
  260.6 3.3 collective-permute-done.10
  263.9 4.1 collective-permute-done.11
  268.0 0.3 multiply_reduce_fusion.1
  268.4 101.5 %psum.45 = f32[2]{0:T(128)S(1)} all-reduce(f32[2]{0:T(128)S(1)} %get-tuple-element.14), channel_id=1, replica_groups=mesh['gx'=32,'gy'=16] {'gx','gy'}, use_global_device_ids=true, to_apply=%region_7.8 | all-reduce | flops 2 | bytes 16 | tf_op jit(solution)/shard_map/psum | solution.py:109
  369.9 0.2 multiply_reduce_fusion
  370.1 99.5 %psum.46 = f32[2]{0:T(128)S(1)} all-reduce(f32[2]{0:T(128)S(1)} %multiply_reduce_fusion), channel_id=1, replica_groups=mesh['gx'=32,'gy'=16] {'gx','gy'}, use_global_device_ids=true, to_apply=%region_9.10 | all-reduce | flops 2 | bytes 16 | tf_op jit(solution)/shard_map/psum | solution.py:89
  469.6 0.1 broadcast_multiply_fusion
  469.7 3.5 collective-permute-start.12
  473.2 1.9 collective-permute-start.13
  475.2 0.1 select_select_fusion
  475.3 3.0 collective-permute-done.13
  478.4 0.1 fusion.97
  478.5 3.7 collective-permute-start.14
  482.2 1.3 collective-permute-start.15
  483.5 3.3 collective-permute-done.14
  486.8 4.1 collective-permute-done.15
  490.9 0.4 fusion.81
  491.3 101.5 %psum.47 = f32[2]{0:T(128)S(1)} all-reduce(f32[2]{0:T(128)S(1)} %fusion.81), channel_id=1, replica_groups=mesh['gx'=32,'gy'=16] {'gx','gy'}, use_global_device_ids=true, to_apply=%region_11.12 | all-reduce | flops 2 | bytes 16 | tf_op jit(solution)/shard_map/psum | solution.py:109
  592.7 0.1 multiply_add_fusion
  592.8 0.0 copy-start
  592.9 3.7 collective-permute-start.16
  596.6 1.9 collective-permute-start.17
  598.6 3.3 collective-permute-done.17
  601.9 0.1 pad_maximum_fusion
  602.0 0.2 fusion.96
  602.2 2.4 collective-permute-start.18
  604.6 1.3 collective-permute-start.19
  605.9 8.7 %collective-permute-done.18 = f32[4,16,10,1]{3,2,1,0:T(8,128)S(1)} collective-permute-done((f32[4,16,10,1]{3,2,1,0:T(8,128)S(1)}, f32[4,16,10,1]{3,2,1,0:T(8,128)S(1)}, u32[]{:S(2)}, u32[]{:S(2)}) %collective-permute-start.18) | collective-permute-done | bytes 2592 | tf_op jit(solution)/shard_map/ppermute | solution.py:19
  614.6 0.2 fusion.44
  614.8 4.0 collective-permute-done.19
  618.8 0.3 fusion.47
  619.1 0.7 subtract_multiply_fusion
  (36 shorter events, 0.4 us)
Async XLA Ops:
  0.6 0.9 copy-start.1
  1.6 14.7 %copy-start.3 = (s32[16,8,128]{2,1,0:T(8,128)S(1)}, s32[16,8,128]{2,1,0:T(8,128)}, u32[]{:S(2)}) copy-start(s32[16,8,128]{2,1,0:T(8,128)} %param.5) | copy-start | bytes 196612
  1.6 10.3 %copy-start.2 = (f32[16,8,128]{2,1,0:T(8,128)S(1)}, f32[16,8,128]{2,1,0:T(8,128)}, u32[]{:S(2)}) copy-start(f32[16,8,128]{2,1,0:T(8,128)} %param.4) | copy-start | bytes 196612
  1.6 20.3 %collective-permute-start.1 = (f32[2,16,1,128]{3,2,1,0:T(1,128)S(1)}, f32[2,16,1,128]{3,2,1,0:T(1,128)S(1)}, u32[]{:S(2)}, u32[]{:S(2)}) collective-permute-start(f32[2,16,1,128]{3,2,1,0:T(1,128)S(1)} %get-tuple-element.37), channel_id=1, source_target_pairs={{0,16},{16,32},{32,48},{48,64},{64,80},{80,96},{96,112},{112,128},... | collective-permute-start | bytes 49160 | tf_op jit(solution)/shard_map/ppermute | solution.py:19
  6.4 15.6 %collective-permute-start.3 = (f32[2,16,1,128]{3,2,1,0:T(1,128)S(1)}, f32[2,16,1,128]{3,2,1,0:T(1,128)S(1)}, u32[]{:S(2)}, u32[]{:S(2)}) collective-permute-start(f32[2,16,1,128]{3,2,1,0:T(1,128)S(1)} %get-tuple-element.38), channel_id=1, source_target_pairs={{16,0},{32,16},{48,32},{64,48},{80,64},{96,80},{112,96},{128,112},... | collective-permute-start | bytes 49160 | tf_op jit(solution)/shard_map/ppermute | solution.py:20
  11.9 4.5 collective-permute-start
  13.8 5.0 collective-permute-start.2
  18.9 8.7 %collective-permute-start.4 = (f32[16,10,1]{2,1,0:T(8,128)S(1)}, f32[16,10,1]{2,1,0:T(8,128)S(1)}, u32[]{:S(2)}, u32[]{:S(2)}) collective-permute-start(f32[16,10,1]{2,1,0:T(8,128)S(1)} %get-tuple-element.35), channel_id=1, source_target_pairs={{0,1},{1,2},{2,3},{3,4},{4,5},{5,6},{6,7},{7,8},{8,9},{9,10},{10,1... | collective-permute-start | bytes 1928 | tf_op jit(solution)/shard_map/ppermute | solution.py:19
  20.6 7.0 %collective-permute-start.6 = (f32[16,10,1]{2,1,0:T(8,128)S(1)}, f32[16,10,1]{2,1,0:T(8,128)S(1)}, u32[]{:S(2)}, u32[]{:S(2)}) collective-permute-start(f32[16,10,1]{2,1,0:T(8,128)S(1)} %get-tuple-element.36), channel_id=1, source_target_pairs={{1,0},{2,1},{3,2},{4,3},{5,4},{6,5},{7,6},{8,7},{9,8},{10,9},{11,1... | collective-permute-start | bytes 1928 | tf_op jit(solution)/shard_map/ppermute | solution.py:20
  22.1 9.2 %collective-permute-start.5 = (f32[2,16,10,1]{3,2,1,0:T(8,128)S(1)}, f32[2,16,10,1]{3,2,1,0:T(8,128)S(1)}, u32[]{:S(2)}, u32[]{:S(2)}) collective-permute-start(f32[2,16,10,1]{3,2,1,0:T(8,128)S(1)} %get-tuple-element.29), channel_id=1, source_target_pairs={{0,1},{1,2},{2,3},{3,4},{4,5},{5,6},{6,7},{7,8},{8,9},{9,10},{10,1... | collective-permute-start | bytes 3848 | tf_op jit(solution)/shard_map/ppermute | solution.py:19
  26.3 9.2 %collective-permute-start.7 = (f32[2,16,10,1]{3,2,1,0:T(8,128)S(1)}, f32[2,16,10,1]{3,2,1,0:T(8,128)S(1)}, u32[]{:S(2)}, u32[]{:S(2)}) collective-permute-start(f32[2,16,10,1]{3,2,1,0:T(8,128)S(1)} %get-tuple-element.30), channel_id=1, source_target_pairs={{1,0},{2,1},{3,2},{4,3},{5,4},{6,5},{7,6},{8,7},{9,8},{10,9},{11,1... | collective-permute-start | bytes 3848 | tf_op jit(solution)/shard_map/ppermute | solution.py:20
  246.9 5.4 collective-permute-start.8
  250.4 5.1 collective-permute-start.9
  255.6 8.3 %collective-permute-start.10 = (f32[2,16,10,1]{3,2,1,0:T(8,128)S(1)}, f32[2,16,10,1]{3,2,1,0:T(8,128)S(1)}, u32[]{:S(2)}, u32[]{:S(2)}) collective-permute-start(f32[2,16,10,1]{3,2,1,0:T(8,128)S(1)} %get-tuple-element.27), channel_id=1, source_target_pairs={{0,1},{1,2},{2,3},{3,4},{4,5},{5,6},{6,7},{7,8},{8,9},{9,10},{10,1... | collective-permute-start | bytes 3848 | tf_op jit(solution)/shard_map/ppermute | solution.py:19
  259.3 8.7 %collective-permute-start.11 = (f32[2,16,10,1]{3,2,1,0:T(8,128)S(1)}, f32[2,16,10,1]{3,2,1,0:T(8,128)S(1)}, u32[]{:S(2)}, u32[]{:S(2)}) collective-permute-start(f32[2,16,10,1]{3,2,1,0:T(8,128)S(1)} %get-tuple-element.28), channel_id=1, source_target_pairs={{1,0},{2,1},{3,2},{4,3},{5,4},{6,5},{7,6},{8,7},{9,8},{10,9},{11,1... | collective-permute-start | bytes 3848 | tf_op jit(solution)/shard_map/ppermute | solution.py:20
  469.6 5.6 copy-start.4
  469.7 5.5 collective-permute-start.12
  473.2 5.1 collective-permute-start.13
  478.5 8.3 %collective-permute-start.14 = (f32[2,16,10,1]{3,2,1,0:T(8,128)S(1)}, f32[2,16,10,1]{3,2,1,0:T(8,128)S(1)}, u32[]{:S(2)}, u32[]{:S(2)}) collective-permute-start(f32[2,16,10,1]{3,2,1,0:T(8,128)S(1)} %get-tuple-element.25), channel_id=1, source_target_pairs={{0,1},{1,2},{2,3},{3,4},{4,5},{5,6},{6,7},{7,8},{8,9},{9,10},{10,1... | collective-permute-start | bytes 3848 | tf_op jit(solution)/shard_map/ppermute | solution.py:19
  482.2 8.7 %collective-permute-start.15 = (f32[2,16,10,1]{3,2,1,0:T(8,128)S(1)}, f32[2,16,10,1]{3,2,1,0:T(8,128)S(1)}, u32[]{:S(2)}, u32[]{:S(2)}) collective-permute-start(f32[2,16,10,1]{3,2,1,0:T(8,128)S(1)} %get-tuple-element.26), channel_id=1, source_target_pairs={{1,0},{2,1},{3,2},{4,3},{5,4},{6,5},{7,6},{8,7},{9,8},{10,9},{11,1... | collective-permute-start | bytes 3848 | tf_op jit(solution)/shard_map/ppermute | solution.py:20
  592.8 26.0 %copy-start = (f32[2,16,8,128]{3,2,1,0:T(8,128)}, f32[2,16,8,128]{3,2,1,0:T(8,128)S(1)}, u32[]{:S(2)}) copy-start(f32[2,16,8,128]{3,2,1,0:T(8,128)S(1)} %multiply_add_fusion) | copy-start | bytes 393220
  592.9 5.7 collective-permute-start.16
  596.6 5.2 collective-permute-start.17
  602.2 12.5 %collective-permute-start.18 = (f32[4,16,10,1]{3,2,1,0:T(8,128)S(1)}, f32[4,16,10,1]{3,2,1,0:T(8,128)S(1)}, u32[]{:S(2)}, u32[]{:S(2)}) collective-permute-start(f32[4,16,10,1]{3,2,1,0:T(8,128)S(1)} %get-tuple-element.21), channel_id=1, source_target_pairs={{0,1},{1,2},{2,3},{3,4},{4,5},{5,6},{6,7},{7,8},{8,9},{9,10},{10,1... | collective-permute-start | bytes 7688 | tf_op jit(solution)/shard_map/ppermute | solution.py:19
  604.6 14.2 %collective-permute-start.19 = (f32[4,16,10,1]{3,2,1,0:T(8,128)S(1)}, f32[4,16,10,1]{3,2,1,0:T(8,128)S(1)}, u32[]{:S(2)}, u32[]{:S(2)}) collective-permute-start(f32[4,16,10,1]{3,2,1,0:T(8,128)S(1)} %get-tuple-element.22), channel_id=1, source_target_pairs={{1,0},{2,1},{3,2},{4,3},{5,4},{6,5},{7,6},{8,7},{9,8},{10,9},{11,1... | collective-permute-start | bytes 7688 | tf_op jit(solution)/shard_map/ppermute | solution.py:20
where the time goes:
time: 621 us; the launch traced here: 620 us
  blocking collectives  513 us (83%)
  starting transfers between devices  53.1 us (9%)
  waiting for transfers between devices  46.9 us (8%)
    psum x3, blocking collectives, global_norm(): return lax.psum(class_sum(solver_residual, solver_residual), ('gx', 'gy'))  310 us
    psum x2, blocking collectives, per_device(): lax.psum(class_sum(search_direction, operator_result), ('gx', 'gy'))  203 us
    ppermute x10, starting transfers between devices, extended(): before = lax.ppermute(last, axis, up)  33 us
    ppermute x10, waiting for transfers between devices, extended(): after = lax.ppermute(initial, axis, down)  28.1 us
    ppermute x10, starting transfers between devices, extended(): after = lax.ppermute(initial, axis, down)  20.1 us
    ppermute x10, waiting for transfers between devices, extended(): before = lax.ppermute(last, axis, up)  18.8 us
  transfers between devices with their start and end apart: 20, of which 12 were waited for; matrix products, arithmetic and copies ran while one was open for 0% of the time, Pallas kernels for 0%

commit v1 on v0

v1 whole, which is shorter than its diff:
```python
import jax
import jax.numpy as jnp
from jax import lax
from jax.sharding import PartitionSpec as P

SHIFT = 2.0
SPAN = 32.0
ALPHA_LOW = 1.0 / 61.0


def extended(x, axis, dim, width):
    size, length = lax.axis_size(axis), x.shape[dim]
    up = [(i, i + 1) for i in range(size - 1)]
    down = [(j, i) for i, j in up]
    last = lax.slice_in_dim(x, length - width, length, axis=dim)
    first = lax.slice_in_dim(x, 0, width, axis=dim)
    before = lax.ppermute(last, axis, up)
    after = lax.ppermute(first, axis, down)
    return jnp.concatenate([before, x, after], axis=dim)


def global_sum(row):
    for axis in ("gx", "gy"):
        size = lax.axis_size(axis)
        sent = jnp.broadcast_to(row[None, None], (size, 1, row.shape[0]))
        row = jnp.sum(lax.all_to_all(sent, axis, 0, 0), axis=(0, 1))
    return row


def edge(c, dim):
    n = c.shape[dim]
    a = lax.slice_in_dim(c, 0, n - 1, axis=dim)
    b = lax.slice_in_dim(c, 1, n, axis=dim)
    return jnp.where(jnp.minimum(a, b) > 0, 0.5 * (a + b), 0.0)


def diff(v, dim):
    n = v.shape[dim]
    return lax.slice_in_dim(v, 0, n - 1, axis=dim) - lax.slice_in_dim(v, 1, n, axis=dim)


def spread(flux, dim, sign):
    low = [(0, 0)] * flux.ndim
    high = [(0, 0)] * flux.ndim
    low[dim], high[dim] = (0, 1), (1, 0)
    return jnp.pad(flux, low) + sign * jnp.pad(flux, high)


def shifted_operator(v, mask, weights):
    total = v
    for dim, w in zip((1, 2, 3), weights):
        total = total + spread(w[None] * diff(v, dim), dim, -1.0)
    return (mask * total - SHIFT * v) * (1.0 / SPAN)


def coefficients(nu):
    def inner(a, b, lift):
        total = 0.0
        for i, x in enumerate(a):
            for j, y in enumerate(b):
                total = total + (x * y) * nu[i + j + lift]
        return total

    residual = [jnp.ones_like(nu[0])]
    direction = residual
    answer = []
    norm = nu[0]
    for iteration in range(3):
        energy = SHIFT * inner(direction, direction, 0) + SPAN * inner(direction, direction, 1)
        step = jnp.clip(norm / energy, ALPHA_LOW, 1.0)
        answer = answer + [0.0]
        answer = [a + step * d for a, d in zip(answer, direction)]
        if iteration == 2:
            return answer
        image = [SHIFT * d for d in direction] + [0.0]
        image = [i + SPAN * d for i, d in zip(image, [0.0] + direction)]
        residual = [r - step * i for r, i in zip(residual + [0.0], image)]
        new = jnp.maximum(inner(residual, residual, 0), 0.0)
        ratio = new / norm
        direction = [r + ratio * d for r, d in zip(residual, direction + [0.0])]
        norm = new


def per_device(conductance, labels, cotangent, saved):
    classes = jnp.arange(1, 3, dtype=jnp.int32)[:, None, None, None]
    potential = jnp.where(labels[None] == classes, 1.0, jnp.where(labels[None] > 0, 0.0, saved))
    mask = (labels == 0).astype(jnp.float32)[None]
    fields = jnp.concatenate([conductance[None], mask, mask * cotangent, potential], axis=0)
    fields = extended(fields, "gx", 2, 3)
    fields = extended(fields, "gy", 3, 3)
    cond, mask, v0, potential = fields[0], fields[1:2], fields[2:4], fields[4:6]
    weights = [edge(cond, dim) for dim in range(3)]
    v1 = shifted_operator(v0, mask, weights)
    v2 = shifted_operator(v1, mask, weights)
    v3 = shifted_operator(v2, mask, weights)
    own = lambda v: v[:, :, 3:-3, 3:-3]
    o = [own(v) for v in (v0, v1, v2, v3)]
    moments = [jnp.sum(o[k // 2] * o[k - k // 2], axis=(1, 2, 3)) for k in range(6)]
    row = jnp.pad(jnp.concatenate(moments), (0, 116))
    row = global_sum(row)
    nu = [row[2 * k : 2 * k + 2] for k in range(6)]
    c = [x[:, None, None, None] for x in coefficients(nu)]
    adjoint = c[0] * v0 + c[1] * v1 + c[2] * v2
    adjoint = adjoint[:, :, 2:-2, 2:-2]
    potential = potential[:, :, 2:-2, 2:-2]
    valid = [(w > 0).astype(jnp.float32) for w in weights]
    gradient = 0.0
    for dim in (1, 2, 3):
        flux = jnp.sum(diff(adjoint, dim) * diff(potential, dim), axis=0)
        ok = valid[dim - 1][:, 2:-2, 2:-2]
        gradient = gradient + spread(flux * ok, dim - 1, 1.0)
    return adjoint[:, :, 1:-1, 1:-1], -0.5 * gradient[:, 1:-1, 1:-1]


def solution(mesh):
    return jax.shard_map(
        per_device,
        mesh=mesh,
        in_specs=(
            P(None, "gx", "gy"),
            P(None, "gx", "gy"),
            P(None, None, "gx", "gy"),
            P(None, None, "gx", "gy"),
        ),
        out_specs=(P(None, None, "gx", "gy"), P(None, "gx", "gy")),
        check_vma=False,
    )
```

time: 621 us -> 85.8 us (0.14)
  blocking collectives: 513 us -> 14.9 us
  waiting for transfers between devices: 46.9 us -> 18 us
  starting transfers between devices: 53.1 us -> 28 us
  other arithmetic: 4.61 us -> 14.5 us
  local copies, waits for them, and re-layouts: 0.82 us -> 8.72 us
    psum x5 -> x0, blocking collectives: 513 us -> none  [the longest x3 310 us: global_norm(): return lax.psum(class_sum(solver_residual, solver_residual), ('gx', 'gy'))]
    ppermute x10 -> x2, starting transfers between devices: 33 us -> 3.21 us  [extended(): before = lax.ppermute(last, axis, up)]
    ppermute x10 -> x2, waiting for transfers between devices: 28.1 us -> 4.28 us  [extended(): after = lax.ppermute(first, axis, down)]
    ppermute x10 -> x2, waiting for transfers between devices: 18.8 us -> 3.18 us  [extended(): before = lax.ppermute(last, axis, up)]
    all_to_all x0 -> x1, blocking collectives: none -> 14.9 us  [global_sum(): row = jnp.sum(lax.all_to_all(sent, axis, 0, 0), axis=(0, 1))]
    all_to_all x0 -> x1, starting transfers between devices: none -> 14.8 us  [global_sum(): row = jnp.sum(lax.all_to_all(sent, axis, 0, 0), axis=(0, 1))]
    all_to_all x0 -> x1, waiting for transfers between devices: none -> 10.5 us  [global_sum(): row = jnp.sum(lax.all_to_all(sent, axis, 0, 0), axis=(0, 1))]
    ppermute x10 -> x2, starting transfers between devices: 20.1 us -> 10.1 us  [extended(): after = lax.ppermute(first, axis, down)]
  transfers between devices with their start and end apart: 20 -> 5, of which waited for: 12 -> 4; matrix products, arithmetic and copies ran while one was open for 0% -> 3% of each run, Pallas kernels for 0% -> 0%
where the time goes in v1:
time: 85.8 us; the launch traced here: 85.3 us
  starting transfers between devices  28 us (33%)
  waiting for transfers between devices  18 us (21%)
  blocking collectives  14.9 us (17%)
  other arithmetic  14.5 us (17%)
  local copies, waits for them, and re-layouts  8.72 us (10%)
  between operations  1.12 us (1%)
    all_to_all x1, blocking collectives, global_sum(): row = jnp.sum(lax.all_to_all(sent, axis, 0, 0), axis=(0, 1))  14.9 us
    all_to_all x1, starting transfers between devices, global_sum(): row = jnp.sum(lax.all_to_all(sent, axis, 0, 0), axis=(0, 1))  14.8 us
    all_to_all x1, waiting for transfers between devices, global_sum(): row = jnp.sum(lax.all_to_all(sent, axis, 0, 0), axis=(0, 1))  10.5 us
    ppermute x2, starting transfers between devices, extended(): after = lax.ppermute(first, axis, down)  10.1 us
    ppermute x2, waiting for transfers between devices, extended(): after = lax.ppermute(first, axis, down)  4.28 us
    ppermute x2, starting transfers between devices, extended(): before = lax.ppermute(last, axis, up)  3.21 us
    ppermute x2, waiting for transfers between devices, extended(): before = lax.ppermute(last, axis, up)  3.18 us
    concatenate x2, other arithmetic, extended(): return jnp.concatenate([before, x, after], axis=dim)  2.25 us
  transfers between devices with their start and end apart: 5, of which 4 were waited for; matrix products, arithmetic and copies ran while one was open for 3% of the time, Pallas kernels for 0%

profile of v1, /device:TPU:1, one launch (start us, length us, event | category | flops | bytes accessed | tf_op | source)
XLA Modules:
  0.0 85.3 jit_solution(8137515332779096511)
XLA Ops:
  0.6 0.9 %fusion.37 = (f32[1,16,8,128]{3,2,1,0:T(8,128)S(1)}, f32[16,8,128]{2,1,0:T(8,128)S(1)}, pred[16,8,128]{2,1,0:T(8,128)(4,1)S(1)}) fusion(s32[16,8,128]{2,1,0:T(8,128)} %param.5), kind=kLoop, calls=%fused_computation.123 | loop fusion | flops 49152 | bytes 212992 | tf_op jit(solution)/shard_map/broadcast_in_dim | solution.py:87
  1.5 0.0 copy-start.10
  1.5 1.1 %select_select_fusion = (f32[2,16,8,128]{3,2,1,0:T(8,128)S(1)}, f32[2,16,8,128]{3,2,1,0:T(8,128)S(1)}) fusion(f32[2,16,8,128]{3,2,1,0:T(8,128)} %param.7, s32[16,8,128]{2,1,0:T(8,128)} %param.5, s32[2]{0:T(128)S(1)} %iota_add_fusion, pred[16,8,128]{2,1,0:T(8,128)(4,1)S(1)} %get-tuple-element.32, f32[2,16,8,128]{3,2,1,0:T(8,128)} %param.6, ...), kind=kLoop, calls=%fused_computation.82 | loop fusion | flops 131072 | bytes 671752 | tf_op jit(solution)/shard_map/jit(_where)/select_n | solution.py:86
  2.6 0.0 copy-start.3
  2.6 0.0 copy-start.12
  2.6 0.9 %pad_maximum_fusion.14 = f32[6,16,8,128]{3,2,1,0:T(8,128)S(1)} fusion(f32[2,16,8,128]{3,2,1,0:T(8,128)S(1)} %get-tuple-element.35, f32[2,16,8,128]{3,2,1,0:T(8,128)S(1)} %get-tuple-element.36, f32[1,16,8,128]{3,2,1,0:T(8,128)S(1)} %get-tuple-element.30, f32[1,16,8,128]{3,2,1,0:T(8,128)} %bitcast.13), kind=kLoop, calls=%fused_computation.49 | loop fusion | flops 294912 | bytes 786432 | tf_op jit(solution)/shard_map/concatenate | solution.py:88
  3.6 0.1 fusion.43
  3.7 8.8 %collective-permute-start.1 = (f32[6,16,3,128]{3,1,2,0:T(8,128)S(1)}, f32[6,16,3,128]{3,1,2,0:T(8,128)S(1)}, u32[]{:S(2)}, u32[]{:S(2)}) collective-permute-start(f32[6,16,3,128]{3,1,2,0:T(8,128)S(1)} %copy.97), channel_id=1, source_target_pairs={{16,0},{32,16},{48,32},{64,48},{80,64},{96,80},{112,96},{128,112},... | collective-permute-start | bytes 442376 | tf_op jit(solution)/shard_map/ppermute | solution.py:18
  12.5 1.9 %collective-permute-start = (f32[6,16,3,128]{3,1,2,0:T(8,128)S(1)}, f32[6,16,3,128]{3,1,2,0:T(8,128)S(1)}, u32[]{:S(2)}, u32[]{:S(2)}) collective-permute-start(f32[6,16,3,128]{3,1,2,0:T(8,128)S(1)} %copy.96), channel_id=1, source_target_pairs={{0,16},{16,32},{32,48},{48,64},{64,80},{80,96},{96,112},{112,128},... | collective-permute-start | bytes 442376 | tf_op jit(solution)/shard_map/ppermute | solution.py:17
  14.4 0.1 copy.87
  14.5 2.0 %collective-permute-done = f32[6,16,3,128]{3,1,2,0:T(8,128)S(1)} collective-permute-done((f32[6,16,3,128]{3,1,2,0:T(8,128)S(1)}, f32[6,16,3,128]{3,1,2,0:T(8,128)S(1)}, u32[]{:S(2)}, u32[]{:S(2)}) %collective-permute-start) | collective-permute-done | bytes 147488 | tf_op jit(solution)/shard_map/ppermute | solution.py:17
  16.5 0.1 copy.86
  16.6 0.1 pad_maximum_fusion.1
  16.7 0.3 fusion.42
  17.0 0.2 copy-done.7
  17.2 0.7 copy.88
  18.0 1.3 %collective-permute-start.2 = (f32[6,16,14,3]{2,1,3,0:T(8,128)S(1)}, f32[6,16,14,3]{2,1,3,0:T(8,128)S(1)}, u32[]{:S(2)}, u32[]{:S(2)}) collective-permute-start(f32[6,16,14,3]{2,1,3,0:T(8,128)S(1)} %copy.88), channel_id=1, source_target_pairs={{0,1},{1,2},{2,3},{3,4},{4,5},{5,6},{6,7},{7,8},{8,9},{9,10},{10,1... | collective-permute-start | bytes 48392 | tf_op jit(solution)/shard_map/ppermute | solution.py:17
  19.3 0.7 copy.89
  20.0 1.3 %collective-permute-start.3 = (f32[6,16,14,3]{2,1,3,0:T(8,128)S(1)}, f32[6,16,14,3]{2,1,3,0:T(8,128)S(1)}, u32[]{:S(2)}, u32[]{:S(2)}) collective-permute-start(f32[6,16,14,3]{2,1,3,0:T(8,128)S(1)} %copy.89), channel_id=1, source_target_pairs={{1,0},{2,1},{3,2},{4,3},{5,4},{6,5},{7,6},{8,7},{9,8},{10,9},{11,1... | collective-permute-start | bytes 48392 | tf_op jit(solution)/shard_map/ppermute | solution.py:18
  21.3 1.2 %collective-permute-done.2 = f32[6,16,14,3]{2,1,3,0:T(8,128)S(1)} collective-permute-done((f32[6,16,14,3]{2,1,3,0:T(8,128)S(1)}, f32[6,16,14,3]{2,1,3,0:T(8,128)S(1)}, u32[]{:S(2)}, u32[]{:S(2)}) %collective-permute-start.2) | collective-permute-done | bytes 16160 | tf_op jit(solution)/shard_map/ppermute | solution.py:17
  22.5 0.7 copy.90
  23.2 4.3 %collective-permute-done.3 = f32[6,16,14,3]{2,1,3,0:T(8,128)S(1)} collective-permute-done((f32[6,16,14,3]{2,1,3,0:T(8,128)S(1)}, f32[6,16,14,3]{2,1,3,0:T(8,128)S(1)}, u32[]{:S(2)}, u32[]{:S(2)}) %collective-permute-start.3) | collective-permute-done | bytes 16160 | tf_op jit(solution)/shard_map/ppermute | solution.py:18
  27.5 0.7 copy.91
  28.2 2.1 %pad_maximum_fusion = f32[6,16,14,134]{3,2,1,0:T(8,128)S(1)} fusion(f32[6,16,14,3]{3,2,1,0:T(8,128)S(1)} %copy.91, f32[6,16,3,128]{3,2,1,0:T(4,128)} %copy-done.5, f32[2,16,8,128]{3,2,1,0:T(8,128)S(1)} %get-tuple-element.35, f32[2,16,8,128]{3,2,1,0:T(8,128)S(1)} %get-tuple-element.36, f32[1,16,8,128]{3,2,1,0:T(8,128)S(1)} %get-tuple-element.30, ...), kind=kLoop, calls=%fused_computation | loop fusion | flops 1260672 | bytes 1440768 | tf_op jit(solution)/shard_map/concatenate | solution.py:19
  30.4 0.1 multiply_select_fusion.1
  30.5 0.1 multiply_select_fusion
  30.6 0.1 fusion.15
  30.7 0.1 slice.300
  30.8 0.2 fusion.9
  31.0 0.1 fusion.10
  31.1 0.4 broadcast_multiply_fusion.1
  31.5 0.1 fusion.14
  31.6 0.2 fusion.7
  31.8 0.1 fusion.8
  31.9 0.4 copy-done.2
  32.3 0.4 broadcast_multiply_fusion
  32.7 0.1 fusion.13
  32.8 0.1 fusion.6
  32.9 0.2 fusion.5
  33.1 0.1 multiply_add_fusion.1
  33.2 0.1 pad_multiply_fusion
  33.3 0.2 copy-done.9
  33.5 1.1 %fusion.21 = (f32[2]{0:T(128)S(1)}, f32[2]{0:T(128)S(1)}, f32[2]{0:T(128)S(1)}, f32[2]{0:T(128)S(1)}, f32[2]{0:T(128)}, /*index=5*/f32[2]{0:T(128)}) fusion(f32[2,16,14,134]{3,2,1,0:T(8,128)S(1)} %get-tuple-element.21, f32[2,16,14,133]{3,2,1,0:T(8,128)S(1)} %fusion.5, f32[2,16,14,134]{3,2,1,0:T(8,128)S(1)} %pad_multiply_fusion, ...), kind=kLoop, calls=%fused_computation.70 | loop fusion | flops 720884 | bytes 1313328 | tf_op jit(solution)/shard_map/reduce_sum | solution.py:98
  34.6 1.3 %concatenate.21 = f32[12]{0:T(128)} concatenate(f32[2]{0:T(128)} %get-tuple-element.11, f32[2]{0:T(128)} %get-tuple-element.10, f32[2]{0:T(128)S(1)} %get-tuple-element.9, f32[2]{0:T(128)S(1)} %get-tuple-element.8, f32[2]{0:T(128)S(1)} %get-tuple-element.7, f32[2]{0:T(128)S(1)} %get-tuple-element.6), dimensions={0} | concatenate | bytes 96 | tf_op jit(solution)/shard_map/concatenate | solution.py:99
  35.9 0.7 pad.106
  36.6 14.9 %all_to_all.10 = f32[32,1,128]{2,1,0:T(1,128)S(1)} all-to-all(f32[32,1,128]{2,1,0:T(1,128)S(1)} %broadcast_in_dim.35), channel_id=1, replica_groups=mesh['gx'=32,'gy'=16] {'gx'}, dimensions={0} | all-to-all | bytes 32768 | tf_op jit(solution)/shard_map/all_to_all | solution.py:26
  51.5 0.6 reduce_sum.105
  52.0 1.2 %broadcast_in_dim.36 = f32[16,1,128]{2,1,0:T(1,128)} broadcast(f32[128]{0:T(128)} %reduce_sum.105), dimensions={2} | broadcast | bytes 8704 | tf_op jit(solution)/shard_map/broadcast_in_dim | solution.py:25
  53.3 14.8 %all-to-all-start.1 = ((f32[16,1,128]{2,1,0:T(1,128)}), f32[16,1,128]{2,1,0:T(1,128)S(1)}, u32[]{:S(2)}, u32[]{:S(2)}) async-start(f32[16,1,128]{2,1,0:T(1,128)} %broadcast_in_dim.36), calls=%async_computation.1 | async-start | bytes 16384 | tf_op jit(solution)/shard_map/all_to_all | solution.py:26
  68.0 0.7 compare_bitcast_fusion
  68.7 10.5 %all-to-all-done.1 = f32[16,1,128]{2,1,0:T(1,128)S(1)} async-done(((f32[16,1,128]{2,1,0:T(1,128)}), f32[16,1,128]{2,1,0:T(1,128)S(1)}, u32[]{:S(2)}, u32[]{:S(2)}) %all-to-all-start.1) | async-done | bytes 8224 | tf_op jit(solution)/shard_map/all_to_all | solution.py:26
  79.3 0.0 copy-start.11
  79.3 0.1 add_maximum_fusion
  79.5 0.1 multiply_add_fusion.2
  79.6 1.4 %multiply_add_fusion = f32[2,16,14,134]{3,2,1,0:T(8,128)S(1)} fusion(f32[2,16,14,134]{3,2,1,0:T(8,128)} %copy-done.9, f32[2,16,14,134]{3,2,1,0:T(8,128)} %copy-done.2, f32[6,16,14,134]{3,2,1,0:T(8,128)S(1)} %pad_maximum_fusion, f32[2]{0:T(128)S(1)} %get-tuple-element.34, f32[2]{0:T(128)S(1)} %get-tuple-element.33, f32[2]{0:T(128)S(1)} %get-tuple-element.12), kind=kLoop, calls=%fused_computation.34 | loop fusion | flops 300160 | bytes 960536 | tf_op jit(solution)/shard_map/add | solution.py:103
  81.1 0.7 fusion.2
  81.8 0.8 slice.302
  82.5 0.6 fusion.12
  83.1 0.6 fusion.4
  83.7 0.3 copy-done.1
  84.1 0.1 fusion.17
  84.2 0.1 fusion.16
  84.3 0.1 slice_select_fusion
  84.5 0.8 fusion.26
  (31 shorter events, 0.2 us)
Async XLA Ops:
  1.5 26.7 %copy-start.10 = (f32[1,16,8,128]{3,2,1,0:T(8,128)}, f32[1,16,8,128]{3,2,1,0:T(8,128)S(1)}, u32[]{:S(2)}) copy-start(f32[1,16,8,128]{3,2,1,0:T(8,128)S(1)} %get-tuple-element.30) | copy-start | bytes 196612
  2.6 25.6 %copy-start.3 = (f32[2,16,8,128]{3,2,1,0:T(8,128)}, f32[2,16,8,128]{3,2,1,0:T(8,128)S(1)}, u32[]{:S(2)}) copy-start(f32[2,16,8,128]{3,2,1,0:T(8,128)S(1)} %get-tuple-element.35) | copy-start | bytes 393220
  2.6 13.9 %copy-start.12 = (f32[16,8,128]{2,1,0:T(8,128)S(1)}, f32[16,8,128]{2,1,0:T(8,128)}, u32[]{:S(2)}) copy-start(f32[16,8,128]{2,1,0:T(8,128)} %param.4) | copy-start | bytes 196612
  3.7 10.7 %collective-permute-start.1 = (f32[6,16,3,128]{3,1,2,0:T(8,128)S(1)}, f32[6,16,3,128]{3,1,2,0:T(8,128)S(1)}, u32[]{:S(2)}, u32[]{:S(2)}) collective-permute-start(f32[6,16,3,128]{3,1,2,0:T(8,128)S(1)} %copy.97), channel_id=1, source_target_pairs={{16,0},{32,16},{48,32},{64,48},{80,64},{96,80},{112,96},{128,112},... | collective-permute-start | bytes 442376 | tf_op jit(solution)/shard_map/ppermute | solution.py:18
  12.5 4.0 %collective-permute-start = (f32[6,16,3,128]{3,1,2,0:T(8,128)S(1)}, f32[6,16,3,128]{3,1,2,0:T(8,128)S(1)}, u32[]{:S(2)}, u32[]{:S(2)}) collective-permute-start(f32[6,16,3,128]{3,1,2,0:T(8,128)S(1)} %copy.96), channel_id=1, source_target_pairs={{0,16},{16,32},{32,48},{48,64},{64,80},{80,96},{96,112},{112,128},... | collective-permute-start | bytes 442376 | tf_op jit(solution)/shard_map/ppermute | solution.py:17
  14.5 2.5 %copy-start.5 = (f32[6,16,3,128]{3,2,1,0:T(4,128)}, f32[6,16,3,128]{3,2,1,0:T(4,128)S(1)}, u32[]{:S(2)}) copy-start(f32[6,16,3,128]{3,2,1,0:T(4,128)S(1)} %copy.87) | copy-start | bytes 442372
  16.6 0.7 copy-start.7
  18.0 4.5 %collective-permute-start.2 = (f32[6,16,14,3]{2,1,3,0:T(8,128)S(1)}, f32[6,16,14,3]{2,1,3,0:T(8,128)S(1)}, u32[]{:S(2)}, u32[]{:S(2)}) collective-permute-start(f32[6,16,14,3]{2,1,3,0:T(8,128)S(1)} %copy.88), channel_id=1, source_target_pairs={{0,1},{1,2},{2,3},{3,4},{4,5},{5,6},{6,7},{7,8},{8,9},{9,10},{10,1... | collective-permute-start | bytes 48392 | tf_op jit(solution)/shard_map/ppermute | solution.py:17
  20.0 7.5 %collective-permute-start.3 = (f32[6,16,14,3]{2,1,3,0:T(8,128)S(1)}, f32[6,16,14,3]{2,1,3,0:T(8,128)S(1)}, u32[]{:S(2)}, u32[]{:S(2)}) collective-permute-start(f32[6,16,14,3]{2,1,3,0:T(8,128)S(1)} %copy.89), channel_id=1, source_target_pairs={{1,0},{2,1},{3,2},{4,3},{5,4},{6,5},{7,6},{8,7},{9,8},{10,9},{11,1... | collective-permute-start | bytes 48392 | tf_op jit(solution)/shard_map/ppermute | solution.py:18
  30.6 2.3 %copy-start = (f32[16,14,133]{2,1,0:T(8,128)}, f32[16,14,133]{2,1,0:T(8,128)S(1)}, u32[]{:S(2)}) copy-start(f32[16,14,133]{2,1,0:T(8,128)S(1)} %multiply_select_fusion) | copy-start | bytes 357508
  31.5 0.8 copy-start.2
  32.7 0.8 copy-start.9
  53.3 26.0 %all-to-all-start.1 = ((f32[16,1,128]{2,1,0:T(1,128)}), f32[16,1,128]{2,1,0:T(1,128)S(1)}, u32[]{:S(2)}, u32[]{:S(2)}) async-start(f32[16,1,128]{2,1,0:T(1,128)} %broadcast_in_dim.36), calls=%async_computation.1 | async-start | bytes 16384 | tf_op jit(solution)/shard_map/all_to_all | solution.py:26
  79.3 1.7 %copy-start.4 = (f32[2,16,8,128]{3,2,1,0:T(8,128)S(1)}, f32[2,16,8,128]{3,2,1,0:T(8,128)}, u32[]{:S(2)}) copy-start(f32[2,16,8,128]{3,2,1,0:T(8,128)} %copy-done.3) | copy-start | bytes 393220
  79.3 1.7 %copy-start.6 = (f32[6,16,3,128]{3,2,1,0:T(4,128)S(1)}, f32[6,16,3,128]{3,2,1,0:T(4,128)}, u32[]{:S(2)}) copy-start(f32[6,16,3,128]{3,2,1,0:T(4,128)} %copy-done.5) | copy-start | bytes 442372
  79.3 1.7 %copy-start.8 = (f32[6,16,3,128]{3,2,1,0:T(4,128)S(1)}, f32[6,16,3,128]{3,2,1,0:T(4,128)}, u32[]{:S(2)}) copy-start(f32[6,16,3,128]{3,2,1,0:T(4,128)} %copy-done.7) | copy-start | bytes 442372
  79.3 1.7 %copy-start.11 = (f32[1,16,8,128]{3,2,1,0:T(8,128)S(1)}, f32[1,16,8,128]{3,2,1,0:T(8,128)}, u32[]{:S(2)}) copy-start(f32[1,16,8,128]{3,2,1,0:T(8,128)} %copy-done.10) | copy-start | bytes 196612
  79.3 1.7 %copy-start.13 = (f32[16,8,128]{2,1,0:T(8,128)S(1)}, f32[16,8,128]{2,1,0:T(8,128)}, u32[]{:S(2)}) copy-start(f32[16,8,128]{2,1,0:T(8,128)} %param.4) | copy-start | bytes 196612
  83.1 1.0 %copy-start.1 = (f32[16,14,133]{2,1,0:T(8,128)S(1)}, f32[16,14,133]{2,1,0:T(8,128)}, u32[]{:S(2)}) copy-start(f32[16,14,133]{2,1,0:T(8,128)} %copy-done) | copy-start | bytes 357508
  83.1 1.2 %copy-start.14 = (pred[15,14,134]{2,1,0:T(8,128)(4,1)S(1)}, pred[15,14,134]{2,1,0:T(8,128)(4,1)}, u32[]{:S(2)}) copy-start(pred[15,14,134]{2,1,0:T(8,128)(4,1)} %compare_bitcast_fusion) | copy-start | bytes 84424

commit v2 on v1

v2 whole, which is shorter than its diff:
```python
import jax
import jax.numpy as jnp
from jax import lax
from jax.experimental import pallas as pl
from jax.experimental.pallas import tpu as pltpu
from jax.sharding import PartitionSpec as P

SHIFT = 2.0
SPAN = 32.0
STEP_LOW = 1.0 / 61.0
SECOND = 64
COND, MASK, RES1, RES2, POT1, POT2 = range(6)
WIDTH = (3, 2, 3, 3, 1, 1)
LANE = (0, 9, 3, 6, 11, 12)
SLOT = (0, 6, 3, 8, 11, 12)
GROUP = 16


def roll(x, amount, axis):
    amount = amount % x.shape[axis]
    return x if amount == 0 else pltpu.roll(x, amount, axis)


def fields_at(cond, labels, cot, saved, z):
    tag = labels[z]
    free = tag == 0
    mask = jnp.where(free, 1.0, 0.0)
    pots = [jnp.where(tag == k + 1, 1.0, jnp.where(free, saved[k, z], 0.0)) for k in range(2)]
    return [cond[z], mask] + [jnp.where(free, cot[k, z], 0.0) for k in range(2)] + pots


def lanes_of(shape=(8, 128)):
    return lax.broadcasted_iota(jnp.int32, shape, 1)


def within(index, low, count):
    return (index >= low) & (index < low + count)


def pack_columns(cond, labels, cot, saved, left, right):
    lane = lanes_of()
    place = [within(lane, LANE[f], WIDTH[f]) for f in range(6)]
    depth = cond.shape[0]
    per = 128 // GROUP
    for tile in range(depth // per):
        left_tile = jnp.zeros((8, 128), jnp.float32)
        right_tile = left_tile
        for j in range(per):
            fields = fields_at(cond, labels, cot, saved, tile * per + j)
            low = jnp.zeros((8, 128), jnp.float32)
            high = low
            for f, x in enumerate(fields):
                low = jnp.where(place[f], roll(x, LANE[f], 1), low)
                high = jnp.where(place[f], roll(x, LANE[f] + WIDTH[f], 1), high)
            here = within(lane, j * GROUP, GROUP)
            left_tile = jnp.where(here, roll(low, j * GROUP, 1), left_tile)
            right_tile = jnp.where(here, roll(high, j * GROUP, 1), right_tile)
        left[tile] = left_tile
        right[tile] = right_tile


def widen(cond, labels, cot, saved, from_left, from_right, wide, top, bottom):
    lane = lanes_of()
    lane16 = lanes_of((16, 128))
    depth = cond.shape[0]
    per = 128 // GROUP
    zero = jnp.zeros((8, 128), jnp.float32)
    ends = [jnp.zeros((16, 128), jnp.float32) for _ in range(2)]
    for z in range(depth):
        fields = fields_at(cond, labels, cot, saved, z)
        tile, base = z // per, (z % per) * GROUP
        low = roll(from_left[tile], -base, 1)
        high = roll(from_right[tile], -base, 1)
        halos = []
        for f in range(6):
            w = WIDTH[f]
            before = roll(low, 128 - w - LANE[f], 1)
            after = roll(high, -LANE[f], 1)
            halos.append(jnp.where(lane < w, after, jnp.where(lane >= 128 - w, before, zero)))
        outside = (halos[COND] == 0.0) & ((lane == 0) | (lane == 127))

        def edge_value(x):
            return jnp.where(lane == 0, roll(x, 1, 1), roll(x, -1, 1))

        halos[COND] = jnp.where(outside, -edge_value(fields[COND]), halos[COND])
        for f in (POT1, POT2):
            halos[f] = jnp.where(outside, edge_value(fields[f]), halos[f])
        for f in range(6):
            wide[f, z, :, 0:128] = fields[f]
            wide[f, z, :, 128:256] = halos[f]
        for side, out in enumerate((top, bottom)):
            out[z, 13:16, :] = jnp.zeros((3, 128), jnp.float32)
            rows = []
            for f in (COND, RES1, MASK, RES2, POT1, POT2):
                w = WIDTH[f]
                start = 0 if side == 0 else 8 - w
                out[z, SLOT[f] : SLOT[f] + w, :] = fields[f][start : start + w]
                rows.append(halos[f][start : start + w])
            rows = jnp.concatenate(rows + [jnp.zeros((3, 128), jnp.float32)], axis=0)
            where = (lane16 + (128 - 8 * z + 3)) % 128 < 6
            ends[side] = jnp.where(where, roll(rows, 8 * z, 1), ends[side])
    top[depth] = ends[0]
    bottom[depth] = ends[1]


def moments(wide, from_top, from_bottom, sent, basis, pots, field, weight):
    depth = wide.shape[1]
    lane16 = lanes_of((16, 128))
    keep = (lane16 < 3) | (lane16 >= 125)
    row8 = lax.broadcasted_iota(jnp.int32, (8, 256), 0)
    for z in range(depth):
        halo = []
        for source in (from_top, from_bottom):
            end = jnp.where(keep, roll(source[depth], -8 * z, 1), 0.0)
            halo.append(jnp.concatenate([source[z], end], axis=1))
        top, bottom = halo
        parts = []
        for f in range(6):
            w, s = WIDTH[f], SLOT[f]
            own = wide[f, z]
            gap = jnp.zeros((8 - 2 * w, 256), jnp.float32)
            parts.append((own, jnp.concatenate([bottom[s : s + w], gap, top[s : s + w]], axis=0)))
        own, other = parts[COND]
        outside = (other == 0.0) & ((row8 == 0) | (row8 == 7))

        def edge_value(x):
            return jnp.where(row8 == 0, roll(x, 1, 0), roll(x, -1, 0))

        parts[COND] = (own, jnp.where(outside, -edge_value(own), other))
        for f in (POT1, POT2):
            own, other = parts[f]
            parts[f] = (own, jnp.where(outside, edge_value(own), other))
        field[0, z, 0:8], field[0, z, 8:16] = parts[COND]
        weight[3, z, 0:8] = parts[MASK][0] * (1.0 / SPAN)
        weight[3, z, 8:16] = parts[MASK][1] * (1.0 / SPAN)
        for k in range(2):
            basis[0, k, z, 0:8], basis[0, k, z, 8:16] = parts[RES1 + k]
            pots[k, z, 0:8], pots[k, z, 8:16] = parts[POT1 + k]
    for z in range(depth):
        c = field[0, z]
        weight[0, z] = 0.5 * (c + roll(c, -1, 0))
        weight[1, z] = 0.5 * (c + roll(c, -1, 1))
        if z + 1 < depth:
            weight[2, z] = 0.5 * (c + field[0, z + 1])

    def image(read, k, z, carry):
        u = read(k, z)
        fx = weight[0, z] * (u - roll(u, -1, 0))
        fy = weight[1, z] * (u - roll(u, -1, 1))
        total = (fx - roll(fx, 1, 0)) + (fy - roll(fy, 1, 1)) - u
        if carry is not None:
            total = total - carry
        carry = None
        if z + 1 < depth:
            carry = weight[2, z] * (u - read(k, z + 1))
            total = total + carry
        return weight[3, z] * total, carry

    for power in range(2):
        for k in range(2):
            carry = None
            for z in range(depth):
                value, carry = image(lambda k, z: basis[power, k, z], k, z, carry)
                basis[power + 1, k, z] = value
    totals = []
    for k in range(2):
        sums = [jnp.zeros((8, 128), jnp.float32) for _ in range(6)]
        carry = None
        for z in range(depth):
            last, carry = image(lambda k, z: basis[2, k, z], k, z, carry)
            v = [basis[i, k, z, 0:8, 0:128] for i in range(3)] + [last[0:8, 0:128]]
            sums = [s + v[i // 2] * v[i - i // 2] for i, s in enumerate(sums)]
        totals += sums
    sub = lax.broadcasted_iota(jnp.int32, (16, 128), 0)
    packed = jnp.zeros((16, 128), jnp.float32)
    for i, s in enumerate(totals):
        packed = jnp.where(sub == i, jnp.sum(s, axis=0, keepdims=True), packed)
    packed = jnp.sum(packed, axis=1, keepdims=True)
    target = jnp.where(sub < 6, sub, sub - 6 + SECOND)
    row = jnp.sum(jnp.where((lane16 == target) & (sub < 12), packed, 0.0), axis=0, keepdims=True)
    sent[...] = jnp.broadcast_to(row, sent.shape)


def relay(received, sent):
    sent[...] = jnp.broadcast_to(jnp.sum(received[...], axis=0, keepdims=True), sent.shape)


def coefficients(nu):
    def inner(a, b, lift):
        total = None
        for i, x in enumerate(a):
            for j, y in enumerate(b):
                term = (x * y) * nu[i + j + lift]
                total = term if total is None else total + term
        return total

    residual = [jnp.ones_like(nu[0])]
    direction = residual
    answer = []
    norm = nu[0]
    for iteration in range(3):
        energy = SHIFT * inner(direction, direction, 0) + SPAN * inner(direction, direction, 1)
        step = jnp.clip(norm / energy, STEP_LOW, 1.0)
        answer = [a + step * d for a, d in zip(answer + [0.0], direction)]
        if iteration == 2:
            return answer
        image = [SHIFT * d for d in direction] + [0.0]
        image = [i + SPAN * d for i, d in zip(image, [0.0] + direction)]
        residual = [r - step * i for r, i in zip(residual + [0.0], image)]
        new = jnp.maximum(inner(residual, residual, 0), 0.0)
        ratio = new / norm
        direction = [r + ratio * d for r, d in zip(residual, direction + [0.0])]
        norm = new


def finish(received, basis, pots, adjoint, gradient, field):
    depth = basis.shape[2]
    row = jnp.sum(received[...], axis=0, keepdims=True)
    row = jnp.broadcast_to(row, (8, 128))
    combined = coefficients([roll(row, -i, 1) for i in range(6)])
    lane = lanes_of()
    scale = [
        [
            jnp.sum(jnp.where(lane == k * SECOND, c, 0.0), axis=1, keepdims=True)[0:1, 0:1]
            for c in combined
        ]
        for k in range(2)
    ]
    for k in range(2):
        c = [jnp.broadcast_to(x, (16, 256)) for x in scale[k]]
        for z in range(depth):
            value = c[0] * basis[0, k, z] + c[1] * basis[1, k, z] + c[2] * basis[2, k, z]
            field[k, z] = value
            adjoint[k, z] = value[0:8, 0:128]
    carry = None
    for z in range(depth):
        gx = gy = gz = None
        for k in range(2):
            a, p = field[k, z], pots[k, z]
            tx = (a - roll(a, -1, 0)) * (p - roll(p, -1, 0))
            ty = (a - roll(a, -1, 1)) * (p - roll(p, -1, 1))
            gx = tx if gx is None else gx + tx
            gy = ty if gy is None else gy + ty
            if z + 1 < depth:
                tz = (a[0:8, 0:128] - field[k, z + 1, 0:8, 0:128]) * (
                    p[0:8, 0:128] - pots[k, z + 1, 0:8, 0:128]
                )
                gz = tz if gz is None else gz + tz
        total = (gx + roll(gx, 1, 0) + gy + roll(gy, 1, 1))[0:8, 0:128]
        if carry is not None:
            total = total + carry
        if gz is not None:
            total = total + gz
        carry = gz
        gradient[z] = -0.5 * total


def local(body, outs, scratch=()):
    vmem = pl.BlockSpec(memory_space=pltpu.VMEM)
    shapes = [jax.ShapeDtypeStruct(s, jnp.float32) for s in outs]

    def call(*args):
        return pl.pallas_call(
            body,
            out_shape=shapes,
            in_specs=[vmem] * len(args),
            out_specs=[vmem] * len(outs),
            scratch_shapes=[pltpu.VMEM(s, jnp.float32) for s in scratch],
            compiler_params=pltpu.CompilerParams(vmem_limit_bytes=32 * 1024 * 1024),
        )(*args)

    return call


def swap(low, high, axis):
    size = lax.axis_size(axis)
    up = [(i, i + 1) for i in range(size - 1)]
    down = [(j, i) for i, j in up]
    return lax.ppermute(high, axis, up), lax.ppermute(low, axis, down)


def per_device(conductance, labels, cotangent, saved):
    depth = conductance.shape[0]
    args = (conductance, labels, cotangent, saved)
    tiles = depth * GROUP // 128
    left, right = local(pack_columns, [(tiles, 8, 128)] * 2)(*args)
    from_left, from_right = swap(left, right, "gy")
    wide, top, bottom = local(widen, [(6, depth, 8, 256)] + [(depth + 1, 16, 128)] * 2)(
        *args, from_left, from_right
    )
    from_top, from_bottom = swap(top, bottom, "gx")
    rows, cols = lax.axis_size("gx"), lax.axis_size("gy")
    sent, basis, pots = local(
        moments,
        [(rows, 128), (3, 2, depth, 16, 256), (2, depth, 16, 256)],
        [(1, depth, 16, 256), (4, depth, 16, 256)],
    )(wide, from_top, from_bottom)
    received = lax.all_to_all(sent, "gx", 0, 0, tiled=True)
    (sent,) = local(relay, [(cols, 128)])(received)
    received = lax.all_to_all(sent, "gy", 0, 0, tiled=True)
    adjoint, gradient = local(finish, [cotangent.shape, conductance.shape], [(2, depth, 16, 256)])(
        received, basis, pots
    )
    return adjoint, gradient


def solution(mesh):
    return jax.shard_map(
        per_device,
        mesh=mesh,
        in_specs=(
            P(None, "gx", "gy"),
            P(None, "gx", "gy"),
            P(None, None, "gx", "gy"),
            P(None, None, "gx", "gy"),
        ),
        out_specs=(P(None, None, "gx", "gy"), P(None, "gx", "gy")),
        check_vma=False,
    )
```

time: 85.8 us -> 74.3 us (0.87)
  blocking collectives: 14.9 us -> 41 us
  other arithmetic: 14.5 us -> 0 us
  starting transfers between devices: 28 us -> 13.6 us
  waiting for transfers between devices: 18 us -> 6.68 us
  Pallas kernels: 0 us -> 8.43 us
  local copies, waits for them, and re-layouts: 8.72 us -> 3.48 us
    all_to_all x1 -> x2, blocking collectives: 14.9 us -> 41 us  [the longest x1 25.9 us: per_device(): received = lax.all_to_all(sent, 'gy', 0, 0, tiled=True)]
    all_to_all x1 -> x0, starting transfers between devices: 14.8 us -> none  [global_sum(): row = jnp.sum(lax.all_to_all(sent, axis, 0, 0), axis=(0, 1))]
    all_to_all x1 -> x0, waiting for transfers between devices: 10.5 us -> none  [global_sum(): row = jnp.sum(lax.all_to_all(sent, axis, 0, 0), axis=(0, 1))]
    pallas_call x0 -> x5, Pallas kernels: none -> 8.43 us  [call(): pl.pallas_call(body, out_shape=shapes, in_specs=[vmem] * len(args), out_s...]
    reduce_sum x6 -> x0, other arithmetic: 3.5 us -> none  [the longest x3 1.87 us: per_device(): flux = jnp.sum(diff(adjoint, dim) * diff(potential, dim), axis=0)]
    mul x18 -> x0, other arithmetic: 3.23 us -> none  [the longest x10 1.12 us: shifted_operator(): total = total + spread(w[None] * diff(v, dim), dim, -1.0)]
    concatenate x3 -> x0, other arithmetic: 3.18 us -> none  [the longest x2 2.25 us: extended(): return jnp.concatenate([before, x, after], axis=dim)]
    slice x6 -> x0, local copies, waits for them, and re-layouts: 2.63 us -> none  [the longest x3 1.06 us: extended(): last = lax.slice_in_dim(x, length - width, length, axis=dim)]
  transfers between devices with their start and end apart: 5 -> 4, of which waited for: 4 -> 2; matrix products, arithmetic and copies ran while one was open for 3% -> 0% of each run, Pallas kernels for 0% -> 0%
where the time goes in v2:
time: 74.3 us; the launch traced here: 73.9 us
  blocking collectives  41 us (55%)
  starting transfers between devices  13.6 us (18%)
  Pallas kernels  8.43 us (11%)
  waiting for transfers between devices  6.68 us (9%)
  local copies, waits for them, and re-layouts  3.48 us (5%)
    all_to_all x1, blocking collectives, per_device(): received = lax.all_to_all(sent, 'gy', 0, 0, tiled=True)  25.9 us
    all_to_all x1, blocking collectives, per_device(): received = lax.all_to_all(sent, 'gx', 0, 0, tiled=True)  15.1 us
    ppermute x4, starting transfers between devices, swap(): return (lax.ppermute(high, axis, up), lax.ppermute(low, axis, down))  13.6 us
    pallas_call x5, Pallas kernels, call(): pl.pallas_call(body, out_shape=shapes, in_specs=[vmem] * len(args), out_s...  8.43 us
    ppermute x4, waiting for transfers between devices, swap(): return (lax.ppermute(high, axis, up), lax.ppermute(low, axis, down))  6.68 us
    unnamed x8, local copies, waits for them, and re-layouts  3.48 us
  transfers between devices with their start and end apart: 4, of which 2 were waited for; matrix products, arithmetic and copies ran while one was open for 0% of the time, Pallas kernels for 0%

profile of v2, /device:TPU:1, one launch (start us, length us, event | category | flops | bytes accessed | tf_op | source)
XLA Modules:
  0.0 73.9 jit_solution(15087556689063182562)
XLA Ops:
  0.6 0.0 copy-start
  0.6 0.9 %copy-done = f32[2,16,8,128]{3,2,1,0:T(8,128)S(1)} copy-done((f32[2,16,8,128]{3,2,1,0:T(8,128)S(1)}, f32[2,16,8,128]{3,2,1,0:T(8,128)}, u32[]{:S(2)}) %copy-start) | copy-done | bytes 131096
  1.5 0.0 copy-start.1
  1.5 0.9 %copy-done.1 = f32[2,16,8,128]{3,2,1,0:T(8,128)S(1)} copy-done((f32[2,16,8,128]{3,2,1,0:T(8,128)S(1)}, f32[2,16,8,128]{3,2,1,0:T(8,128)}, u32[]{:S(2)}) %copy-start.1) | copy-done | bytes 131096
  2.4 0.0 copy-start.2
  2.4 0.8 %copy-done.2 = f32[16,8,128]{2,1,0:T(8,128)S(1)} copy-done((f32[16,8,128]{2,1,0:T(8,128)S(1)}, f32[16,8,128]{2,1,0:T(8,128)}, u32[]{:S(2)}) %copy-start.2) | copy-done | bytes 65560
  3.3 0.0 copy-start.3
  3.3 0.8 %copy-done.3 = s32[16,8,128]{2,1,0:T(8,128)S(1)} copy-done((s32[16,8,128]{2,1,0:T(8,128)S(1)}, s32[16,8,128]{2,1,0:T(8,128)}, u32[]{:S(2)}) %copy-start.3) | copy-done | bytes 65560
  4.1 0.6 shard_map.59
  4.7 4.4 %collective-permute-start = (f32[2,8,128]{2,1,0:T(8,128)S(1)}, f32[2,8,128]{2,1,0:T(8,128)S(1)}, u32[]{:S(2)}, u32[]{:S(2)}) collective-permute-start(f32[2,8,128]{2,1,0:T(8,128)S(1)} %get-tuple-element.10), channel_id=1, source_target_pairs={{0,1},{1,2},{2,3},{3,4},{4,5},{5,6},{6,7},{7,8},{8,9},{9,10},{10,1... | collective-permute-start | bytes 24584 | tf_op jit(solution)/shard_map/ppermute | solution.py:279
  9.1 1.3 %collective-permute-start.1 = (f32[2,8,128]{2,1,0:T(8,128)S(1)}, f32[2,8,128]{2,1,0:T(8,128)S(1)}, u32[]{:S(2)}, u32[]{:S(2)}) collective-permute-start(f32[2,8,128]{2,1,0:T(8,128)S(1)} %get-tuple-element.11), channel_id=1, source_target_pairs={{1,0},{2,1},{3,2},{4,3},{5,4},{6,5},{7,6},{8,7},{9,8},{10,9},{11,1... | collective-permute-start | bytes 24584 | tf_op jit(solution)/shard_map/ppermute | solution.py:279
  10.4 0.0 collective-permute-done.from_left
  10.4 3.3 %collective-permute-done.1.from_right = f32[2,8,128]{2,1,0:T(8,128)S(1)} collective-permute-done((f32[2,8,128]{2,1,0:T(8,128)S(1)}, f32[2,8,128]{2,1,0:T(8,128)S(1)}, u32[]{:S(2)}, u32[]{:S(2)}) %collective-permute-start.1) | collective-permute-done | bytes 8224 | tf_op jit(solution)/shard_map/ppermute | solution.py:279
  13.7 1.4 %shard_map.60 = (f32[6,16,8,256]{3,2,1,0:T(8,128)S(1)}, f32[17,16,128]{2,1,0:T(8,128)S(1)}, f32[17,16,128]{2,1,0:T(8,128)S(1)}) custom-call(f32[16,8,128]{2,1,0:T(8,128)S(1)} %copy-done.2, s32[16,8,128]{2,1,0:T(8,128)S(1)} %copy-done.3, f32[2,16,8,128]{3,2,1,0:T(8,128)S(1)} %copy-done, f32[2,16,8,128]{3,2,1,0:T(8,128)S(1)} %copy-done.1, ...), custom_call_target="tpu_custom_call" | custom-call | tf_op jit(solution)/shard_map/pallas_call | solution.py:263
  15.1 5.0 %collective-permute-start.2 = (f32[17,16,128]{2,1,0:T(8,128)S(1)}, f32[17,16,128]{2,1,0:T(8,128)S(1)}, u32[]{:S(2)}, u32[]{:S(2)}) collective-permute-start(f32[17,16,128]{2,1,0:T(8,128)S(1)} %get-tuple-element.13), channel_id=1, source_target_pairs={{0,16},{16,32},{32,48},{48,64},{64,80},{80,96},{96,112},{112,128},... | collective-permute-start | bytes 417800 | tf_op jit(solution)/shard_map/ppermute | solution.py:279
  20.1 3.0 %collective-permute-start.3 = (f32[17,16,128]{2,1,0:T(8,128)S(1)}, f32[17,16,128]{2,1,0:T(8,128)S(1)}, u32[]{:S(2)}, u32[]{:S(2)}) collective-permute-start(f32[17,16,128]{2,1,0:T(8,128)S(1)} %get-tuple-element.14), channel_id=1, source_target_pairs={{16,0},{32,16},{48,32},{64,48},{80,64},{96,80},{112,96},{128,112},... | collective-permute-start | bytes 417800 | tf_op jit(solution)/shard_map/ppermute | solution.py:279
  23.0 0.0 collective-permute-done.2.from_top
  23.0 3.4 %collective-permute-done.3.from_bottom = f32[17,16,128]{2,1,0:T(8,128)S(1)} collective-permute-done((f32[17,16,128]{2,1,0:T(8,128)S(1)}, f32[17,16,128]{2,1,0:T(8,128)S(1)}, u32[]{:S(2)}, u32[]{:S(2)}) %collective-permute-start.3) | collective-permute-done | bytes 139296 | tf_op jit(solution)/shard_map/ppermute | solution.py:279
  26.4 5.3 %shard_map.61 = (f32[32,128]{1,0:T(8,128)S(1)}, f32[3,2,16,16,256]{4,3,2,1,0:T(8,128)S(1)}, f32[2,16,16,256]{3,2,1,0:T(8,128)S(1)}) custom-call(f32[6,16,8,256]{3,2,1,0:T(8,128)S(1)} %get-tuple-element.12.wide, f32[17,16,128]{2,1,0:T(8,128)S(1)} %collective-permute-done.2.from_top, f32[17,16,128]{2,1,0:T(8,128)S(1)} %collective-permute-done.3.from_bottom), custom_call_target="tpu_custom_call" | custom-call | tf_op jit(solution)/shard_map/pallas_call | solution.py:263
  31.8 15.1 %all_to_all.22 = f32[32,1,128]{2,1,0:T(1,128)S(1)} all-to-all(f32[32,1,128]{2,1,0:T(1,128)S(1)} %bitcast.11), channel_id=1, replica_groups=mesh['gx'=32,'gy'=16] {'gx'}, dimensions={0} | all-to-all | bytes 32768 | tf_op jit(solution)/shard_map/all_to_all | solution.py:298
  46.9 25.9 %all_to_all.23 = f32[16,1,128]{2,1,0:T(1,128)S(1)} all-to-all(f32[16,1,128]{2,1,0:T(1,128)S(1)} %bitcast.10), channel_id=1, replica_groups=mesh['gx'=32,'gy'=16] {'gy'}, dimensions={0} | all-to-all | bytes 16384 | tf_op jit(solution)/shard_map/all_to_all | solution.py:300
  72.8 1.1 %shard_map.63 = (f32[2,16,8,128]{3,2,1,0:T(8,128)}, f32[16,8,128]{2,1,0:T(8,128)}) custom-call(f32[16,128]{1,0:T(8,128)S(1)} %bitcast.9, f32[3,2,16,16,256]{4,3,2,1,0:T(8,128)S(1)} %get-tuple-element.16.basis, f32[2,16,16,256]{3,2,1,0:T(8,128)S(1)} %get-tuple-element.17.pots), custom_call_target="tpu_custom_call" | custom-call | tf_op jit(solution)/shard_map/pallas_call | solution.py:263
  (1 shorter events, 0.0 us)
Async XLA Ops:
  0.6 0.9 %copy-start = (f32[2,16,8,128]{3,2,1,0:T(8,128)S(1)}, f32[2,16,8,128]{3,2,1,0:T(8,128)}, u32[]{:S(2)}) copy-start(f32[2,16,8,128]{3,2,1,0:T(8,128)} %cot.3) | copy-start | bytes 393220
  1.5 0.9 %copy-start.1 = (f32[2,16,8,128]{3,2,1,0:T(8,128)S(1)}, f32[2,16,8,128]{3,2,1,0:T(8,128)}, u32[]{:S(2)}) copy-start(f32[2,16,8,128]{3,2,1,0:T(8,128)} %saved.3) | copy-start | bytes 393220
  2.4 0.8 %copy-start.2 = (f32[16,8,128]{2,1,0:T(8,128)S(1)}, f32[16,8,128]{2,1,0:T(8,128)}, u32[]{:S(2)}) copy-start(f32[16,8,128]{2,1,0:T(8,128)} %cond.3) | copy-start | bytes 196612
  3.3 0.8 %copy-start.3 = (s32[16,8,128]{2,1,0:T(8,128)S(1)}, s32[16,8,128]{2,1,0:T(8,128)}, u32[]{:S(2)}) copy-start(s32[16,8,128]{2,1,0:T(8,128)} %labels.3) | copy-start | bytes 196612
  4.7 5.7 %collective-permute-start = (f32[2,8,128]{2,1,0:T(8,128)S(1)}, f32[2,8,128]{2,1,0:T(8,128)S(1)}, u32[]{:S(2)}, u32[]{:S(2)}) collective-permute-start(f32[2,8,128]{2,1,0:T(8,128)S(1)} %get-tuple-element.10), channel_id=1, source_target_pairs={{0,1},{1,2},{2,3},{3,4},{4,5},{5,6},{6,7},{7,8},{8,9},{9,10},{10,1... | collective-permute-start | bytes 24584 | tf_op jit(solution)/shard_map/ppermute | solution.py:279
  9.1 4.6 %collective-permute-start.1 = (f32[2,8,128]{2,1,0:T(8,128)S(1)}, f32[2,8,128]{2,1,0:T(8,128)S(1)}, u32[]{:S(2)}, u32[]{:S(2)}) collective-permute-start(f32[2,8,128]{2,1,0:T(8,128)S(1)} %get-tuple-element.11), channel_id=1, source_target_pairs={{1,0},{2,1},{3,2},{4,3},{5,4},{6,5},{7,6},{8,7},{9,8},{10,9},{11,1... | collective-permute-start | bytes 24584 | tf_op jit(solution)/shard_map/ppermute | solution.py:279
  15.1 8.0 %collective-permute-start.2 = (f32[17,16,128]{2,1,0:T(8,128)S(1)}, f32[17,16,128]{2,1,0:T(8,128)S(1)}, u32[]{:S(2)}, u32[]{:S(2)}) collective-permute-start(f32[17,16,128]{2,1,0:T(8,128)S(1)} %get-tuple-element.13), channel_id=1, source_target_pairs={{0,16},{16,32},{32,48},{48,64},{64,80},{80,96},{96,112},{112,128},... | collective-permute-start | bytes 417800 | tf_op jit(solution)/shard_map/ppermute | solution.py:279
  20.1 6.4 %collective-permute-start.3 = (f32[17,16,128]{2,1,0:T(8,128)S(1)}, f32[17,16,128]{2,1,0:T(8,128)S(1)}, u32[]{:S(2)}, u32[]{:S(2)}) collective-permute-start(f32[17,16,128]{2,1,0:T(8,128)S(1)} %get-tuple-element.14), channel_id=1, source_target_pairs={{16,0},{32,16},{48,32},{64,48},{80,64},{96,80},{112,96},{128,112},... | collective-permute-start | bytes 417800 | tf_op jit(solution)/shard_map/ppermute | solution.py:279

commit v3 on v2

--- a/solution.py
+++ b/solution.py
@@ -37,7 +37,18 @@
     return (index >= low) & (index < low + count)
 
 
-def pack_columns(cond, labels, cot, saved, left, right):
+def pack_columns(cond_in, labels_in, cot_in, saved_in, first, second, field, cond, labels, cot, saved, sems):
+    copies = [
+        pltpu.make_async_copy(source, target, sems.at[i])
+        for i, (source, target) in enumerate(
+            ((cond_in, cond), (labels_in, labels), (cot_in, cot), (saved_in, saved))
+        )
+    ]
+    for copy in copies:
+        copy.start()
+    for copy in copies:
+        copy.wait()
+    even = lax.axis_index("gy") % 2 == 0
     lane = lanes_of()
     place = [within(lane, LANE[f], WIDTH[f]) for f in range(6)]
     depth = cond.shape[0]
@@ -46,31 +57,35 @@
         left_tile = jnp.zeros((8, 128), jnp.float32)
         right_tile = left_tile
         for j in range(per):
-            fields = fields_at(cond, labels, cot, saved, tile * per + j)
+            z = tile * per + j
+            fields = fields_at(cond, labels, cot, saved, z)
             low = jnp.zeros((8, 128), jnp.float32)
             high = low
             for f, x in enumerate(fields):
+                field[f, z] = x
                 low = jnp.where(place[f], roll(x, LANE[f], 1), low)
                 high = jnp.where(place[f], roll(x, LANE[f] + WIDTH[f], 1), high)
             here = within(lane, j * GROUP, GROUP)
             left_tile = jnp.where(here, roll(low, j * GROUP, 1), left_tile)
             right_tile = jnp.where(here, roll(high, j * GROUP, 1), right_tile)
-        left[tile] = left_tile
-        right[tile] = right_tile
-
-
-def widen(cond, labels, cot, saved, from_left, from_right, wide, top, bottom):
+        first[tile] = jnp.where(even, right_tile, left_tile)
+        second[tile] = jnp.where(even, left_tile, right_tile)
+
+
+def widen(field, from_first, from_second, wide, near, far):
+    even = lax.axis_index("gy") % 2 == 0
+    upper = lax.axis_index("gx") % 2 == 0
     lane = lanes_of()
     lane16 = lanes_of((16, 128))
-    depth = cond.shape[0]
+    depth = field.shape[1]
     per = 128 // GROUP
     zero = jnp.zeros((8, 128), jnp.float32)
     ends = [jnp.zeros((16, 128), jnp.float32) for _ in range(2)]
     for z in range(depth):
-        fields = fields_at(cond, labels, cot, saved, z)
+        fields = [field[f, z] for f in range(6)]
         tile, base = z // per, (z % per) * GROUP
-        low = roll(from_left[tile], -base, 1)
-        high = roll(from_right[tile], -base, 1)
+        low = roll(jnp.where(even, from_second[tile], from_first[tile]), -base, 1)
+        high = roll(jnp.where(even, from_first[tile], from_second[tile]), -base, 1)
         halos = []
         for f in range(6):
             w = WIDTH[f]
@@ -88,32 +103,39 @@
         for f in range(6):
             wide[f, z, :, 0:128] = fields[f]
             wide[f, z, :, 128:256] = halos[f]
-        for side, out in enumerate((top, bottom)):
-            out[z, 13:16, :] = jnp.zeros((3, 128), jnp.float32)
-            rows = []
+        own, end = [], []
+        for side in range(2):
+            rows, tips = [], []
             for f in (COND, RES1, MASK, RES2, POT1, POT2):
                 w = WIDTH[f]
                 start = 0 if side == 0 else 8 - w
-                out[z, SLOT[f] : SLOT[f] + w, :] = fields[f][start : start + w]
-                rows.append(halos[f][start : start + w])
-            rows = jnp.concatenate(rows + [jnp.zeros((3, 128), jnp.float32)], axis=0)
-            where = (lane16 + (128 - 8 * z + 3)) % 128 < 6
-            ends[side] = jnp.where(where, roll(rows, 8 * z, 1), ends[side])
-    top[depth] = ends[0]
-    bottom[depth] = ends[1]
-
-
-def moments(wide, from_top, from_bottom, sent, basis, pots, field, weight):
+                rows.append(fields[f][start : start + w])
+                tips.append(halos[f][start : start + w])
+            blank = [jnp.zeros((3, 128), jnp.float32)]
+            own.append(jnp.concatenate(rows + blank, axis=0))
+            end.append(jnp.concatenate(tips + blank, axis=0))
+        where = (lane16 + (128 - 8 * z + 3)) % 128 < 6
+        near[z] = jnp.where(upper, own[1], own[0])
+        far[z] = jnp.where(upper, own[0], own[1])
+        for side in range(2):
+            ends[side] = jnp.where(where, roll(end[side], 8 * z, 1), ends[side])
+    near[depth] = jnp.where(upper, ends[1], ends[0])
+    far[depth] = jnp.where(upper, ends[0], ends[1])
+
+
+def moments(wide, from_near, from_far, sent, basis, pots, field, weight):
     depth = wide.shape[1]
+    core = lax.axis_index("gx") % 2
     lane16 = lanes_of((16, 128))
     keep = (lane16 < 3) | (lane16 >= 125)
     row8 = lax.broadcasted_iota(jnp.int32, (8, 256), 0)
     for z in range(depth):
         halo = []
-        for source in (from_top, from_bottom):
-            end = jnp.where(keep, roll(source[depth], -8 * z, 1), 0.0)
-            halo.append(jnp.concatenate([source[z], end], axis=1))
-        top, bottom = halo
+        for source in (lambda i: from_near[1 - core, i], lambda i: from_far[i]):
+            end = jnp.where(keep, roll(source(depth), -8 * z, 1), 0.0)
+            halo.append(jnp.concatenate([source(z), end], axis=1))
+        top = jnp.where(core == 0, halo[1], halo[0])
+        bottom = jnp.where(core == 0, halo[0], halo[1])
         parts = []
         for f in range(6):
             w, s = WIDTH[f], SLOT[f]
@@ -162,13 +184,29 @@
             for z in range(depth):
                 value, carry = image(lambda k, z: basis[power, k, z], k, z, carry)
                 basis[power + 1, k, z] = value
+    def own_image(k, z, carry):
+        u = basis[2, k, z]
+        fx = weight[0, z, :, 0:128] * (u[:, 0:128] - roll(u[:, 0:128], -1, 0))
+        fx = (fx - roll(fx, 1, 0))[0:8]
+        u = u[0:8]
+        fy = weight[1, z, 0:8] * (u - roll(u, -1, 1))
+        own = (slice(0, 8), slice(0, 128))
+        total = fx + (fy - roll(fy, 1, 1))[own] - u[own]
+        if carry is not None:
+            total = total - carry
+        carry = None
+        if z + 1 < depth:
+            carry = weight[2, z, 0:8, 0:128] * (u[own] - basis[2, k, z + 1, 0:8, 0:128])
+            total = total + carry
+        return weight[3, z, 0:8, 0:128] * total, carry
+
     totals = []
     for k in range(2):
         sums = [jnp.zeros((8, 128), jnp.float32) for _ in range(6)]
         carry = None
         for z in range(depth):
-            last, carry = image(lambda k, z: basis[2, k, z], k, z, carry)
-            v = [basis[i, k, z, 0:8, 0:128] for i in range(3)] + [last[0:8, 0:128]]
+            last, carry = own_image(k, z, carry)
+            v = [basis[i, k, z, 0:8, 0:128] for i in range(3)] + [last]
             sums = [s + v[i // 2] * v[i - i // 2] for i, s in enumerate(sums)]
         totals += sums
     sub = lax.broadcasted_iota(jnp.int32, (16, 128), 0)
@@ -255,52 +293,62 @@
         gradient[z] = -0.5 * total
 
 
-def local(body, outs, scratch=()):
+def local(body, outs, scratch=(), space=pltpu.VMEM, limit=32 * 2**20, kind=pltpu.VMEM):
     vmem = pl.BlockSpec(memory_space=pltpu.VMEM)
-    shapes = [jax.ShapeDtypeStruct(s, jnp.float32) for s in outs]
+    shapes = [kind(s, jnp.float32) for s in outs]
 
     def call(*args):
         return pl.pallas_call(
             body,
             out_shape=shapes,
-            in_specs=[vmem] * len(args),
+            in_specs=[pl.BlockSpec(memory_space=space)] * len(args),
             out_specs=[vmem] * len(outs),
-            scratch_shapes=[pltpu.VMEM(s, jnp.float32) for s in scratch],
-            compiler_params=pltpu.CompilerParams(vmem_limit_bytes=32 * 1024 * 1024),
+            scratch_shapes=list(scratch),
+            compiler_params=pltpu.CompilerParams(vmem_limit_bytes=limit),
         )(*args)
 
     return call
 
 
-def swap(low, high, axis):
-    size = lax.axis_size(axis)
-    up = [(i, i + 1) for i in range(size - 1)]
-    down = [(j, i) for i, j in up]
-    return lax.ppermute(high, axis, up), lax.ppermute(low, axis, down)
+def scratch(*shape, dtype=jnp.float32):
+    return pltpu.VMEM(shape, dtype)
+
+
+def trade(x, axis, start):
+    pairs = [(i, i + 1) for i in range(start, lax.axis_size(axis) - 1, 2)]
+    return lax.ppermute(x, axis, pairs + [(j, i) for i, j in pairs])
 
 
 def per_device(conductance, labels, cotangent, saved):
     depth = conductance.shape[0]
+    rows, cols = lax.axis_size("gx"), lax.axis_size("gy")
     args = (conductance, labels, cotangent, saved)
     tiles = depth * GROUP // 128
-    left, right = local(pack_columns, [(tiles, 8, 128)] * 2)(*args)
-    from_left, from_right = swap(left, right, "gy")
-    wide, top, bottom = local(widen, [(6, depth, 8, 256)] + [(depth + 1, 16, 128)] * 2)(
-        *args, from_left, from_right
+    first, second, field = local(
+        pack_columns,
+        [(tiles, 8, 128)] * 2 + [(6, depth, 8, 128)],
+        [scratch(*x.shape, dtype=x.dtype) for x in args] + [pltpu.SemaphoreType.DMA((4,))],
+        pltpu.HBM,
+        56 * 2**20,
+    )(*args)
+    first, second = trade(first, "gy", 0), trade(second, "gy", 1)
+    wide, near, far = local(widen, [(6, depth, 8, 256)] + [(depth + 1, 16, 128)] * 2)(
+        field, first, second
     )
-    from_top, from_bottom = swap(top, bottom, "gx")
-    rows, cols = lax.axis_size("gx"), lax.axis_size("gy")
+    far = trade(far, "gx", 1)
+    near = lax.all_gather(near, "gx", axis_index_groups=[[i, i + 1] for i in range(0, rows, 2)])
     sent, basis, pots = local(
         moments,
         [(rows, 128), (3, 2, depth, 16, 256), (2, depth, 16, 256)],
-        [(1, depth, 16, 256), (4, depth, 16, 256)],
-    )(wide, from_top, from_bottom)
+        [scratch(1, depth, 16, 256), scratch(4, depth, 16, 256)],
+    )(wide, near, far)
     received = lax.all_to_all(sent, "gx", 0, 0, tiled=True)
     (sent,) = local(relay, [(cols, 128)])(received)
     received = lax.all_to_all(sent, "gy", 0, 0, tiled=True)
-    adjoint, gradient = local(finish, [cotangent.shape, conductance.shape], [(2, depth, 16, 256)])(
-        received, basis, pots
-    )
+    adjoint, gradient = local(
+        finish, [cotangent.shape, conductance.shape], [scratch(2, depth, 16, 256)],
+        kind=jax.ShapeDtypeStruct,
+    )(received, basis, pots)
     return adjoint, gradient
 
 

time: 74.3 us -> 67.8 us (0.913)
  waiting for transfers between devices: 6.68 us -> 0.36 us
  blocking collectives: 41 us -> 47.2 us
  starting transfers between devices: 13.6 us -> 9.77 us
  local copies, waits for them, and re-layouts: 3.48 us -> 0 us
  Pallas kernels: 8.43 us -> 9.48 us
    ppermute x4 -> x3, waiting for transfers between devices: 6.68 us -> 0.36 us  [trade(): return lax.ppermute(x, axis, pairs + [(j, i) for i, j in pairs])]
    all_gather x0 -> x1, blocking collectives: none -> 4.6 us  [per_device(): lax.all_gather(near, 'gx', axis_index_groups=[[i, i + 1] for i in range(0...]
    all_to_all x1, blocking collectives: 25.9 us -> 29.7 us  [per_device(): received = lax.all_to_all(sent, 'gy', 0, 0, tiled=True)]
    ppermute x4 -> x3, starting transfers between devices: 13.6 us -> 9.77 us  [trade(): return lax.ppermute(x, axis, pairs + [(j, i) for i, j in pairs])]
    unnamed x8 -> x0, local copies, waits for them, and re-layouts: 3.48 us -> none
    all_to_all x1, blocking collectives: 15.1 us -> 12.9 us  [per_device(): received = lax.all_to_all(sent, 'gx', 0, 0, tiled=True)]
    pallas_call x5, Pallas kernels: 8.43 us -> 9.48 us  [call(): pl.pallas_call(body, out_shape=shapes, in_specs=[pl.BlockSpec(memory_spac...]
  transfers between devices with their start and end apart: 4 -> 3, of which waited for: 2 -> 1; matrix products, arithmetic and copies ran while one was open for 0% -> 0% of each run, Pallas kernels for 0% -> 0%
where the time goes in v3:
time: 67.8 us; the launch traced here: 67.5 us
  blocking collectives  47.2 us (70%)
  starting transfers between devices  9.77 us (14%)
  Pallas kernels  9.48 us (14%)
    all_to_all x1, blocking collectives, per_device(): received = lax.all_to_all(sent, 'gy', 0, 0, tiled=True)  29.7 us
    all_to_all x1, blocking collectives, per_device(): received = lax.all_to_all(sent, 'gx', 0, 0, tiled=True)  12.9 us
    ppermute x3, starting transfers between devices, trade(): return lax.ppermute(x, axis, pairs + [(j, i) for i, j in pairs])  9.77 us
    pallas_call x5, Pallas kernels, call(): pl.pallas_call(body, out_shape=shapes, in_specs=[pl.BlockSpec(memory_spac...  9.48 us
    all_gather x1, blocking collectives, per_device(): lax.all_gather(near, 'gx', axis_index_groups=[[i, i + 1] for i in range(0...  4.6 us
  transfers between devices with their start and end apart: 3, of which 1 were waited for; matrix products, arithmetic and copies ran while one was open for 0% of the time, Pallas kernels for 0%

profile of v3, /device:TPU:1, one launch (start us, length us, event | category | flops | bytes accessed | tf_op | source)
XLA Modules:
  0.0 67.5 jit_solution(10096429080863090617)
XLA Ops:
  0.6 1.6 %shard_map.59 = (f32[2,8,128]{2,1,0:T(8,128)S(1)}, f32[2,8,128]{2,1,0:T(8,128)S(1)}, f32[6,16,8,128]{3,2,1,0:T(8,128)S(1)}) custom-call(f32[16,8,128]{2,1,0:T(8,128)} %cond_in.1, s32[16,8,128]{2,1,0:T(8,128)} %labels_in.1, f32[2,16,8,128]{3,2,1,0:T(8,128)} %cot_in.1, f32[2,16,8,128]{3,2,1,0:T(8,128)} %saved_in.1), custom_call_target="tpu_custom_call" | custom-call | tf_op jit(solution)/shard_map/pallas_call | solution.py:301
  2.3 4.4 %collective-permute-start = (f32[2,8,128]{2,1,0:T(8,128)S(1)}, f32[2,8,128]{2,1,0:T(8,128)S(1)}, u32[]{:S(2)}, u32[]{:S(2)}) collective-permute-start(f32[2,8,128]{2,1,0:T(8,128)S(1)} %get-tuple-element.12), channel_id=1, source_target_pairs={{0,1},{2,3},{4,5},{6,7},{8,9},{10,11},{12,13},{14,15},{1,0},{3,2},... | collective-permute-start | bytes 24584 | tf_op jit(solution)/shard_map/ppermute | solution.py:319
  6.7 0.7 collective-permute-start.1
  7.3 0.4 collective-permute-done.from_first
  7.7 0.0 collective-permute-done.1.from_second
  7.7 1.3 %shard_map.60 = (f32[6,16,8,256]{3,2,1,0:T(8,128)S(1)}, f32[17,16,128]{2,1,0:T(8,128)S(1)}, f32[17,16,128]{2,1,0:T(8,128)S(1)}) custom-call(f32[6,16,8,128]{3,2,1,0:T(8,128)S(1)} %get-tuple-element.11.field, f32[2,8,128]{2,1,0:T(8,128)S(1)} %collective-permute-done.from_first, f32[2,8,128]{2,1,0:T(8,128)S(1)} %collective-permute-done.1.from_second), custom_call_target="tpu_custom_call" | custom-call | tf_op jit(solution)/shard_map/pallas_call | solution.py:301
  9.0 4.7 %collective-permute-start.2 = (f32[17,16,128]{2,1,0:T(8,128)S(1)}, f32[17,16,128]{2,1,0:T(8,128)S(1)}, u32[]{:S(2)}, u32[]{:S(2)}) collective-permute-start(f32[17,16,128]{2,1,0:T(8,128)S(1)} %get-tuple-element.16), channel_id=1, source_target_pairs={{16,32},{48,64},{80,96},{112,128},{144,160},{176,192},{208,224},{2... | collective-permute-start | bytes 417800 | tf_op jit(solution)/shard_map/ppermute | solution.py:319
  13.8 4.6 %all-gather = f32[34,16,128]{2,1,0:T(8,128)S(1)} all-gather(f32[17,16,128]{2,1,0:T(8,128)S(1)} %get-tuple-element.15), channel_id=2, replica_groups={{0,16},{32,48},{64,80},{96,112},{128,144},{160,176},{192,208},{224,240}..., dimensions={0}, use_global_device_ids=true | all-gather | bytes 417792 | tf_op jit(solution)/shard_map/all_gather | solution.py:339
  18.4 0.0 collective-permute-done.2.from_far
  18.4 5.3 %shard_map.61 = (f32[32,128]{1,0:T(8,128)S(1)}, f32[3,2,16,16,256]{4,3,2,1,0:T(8,128)S(1)}, f32[2,16,16,256]{3,2,1,0:T(8,128)S(1)}) custom-call(f32[6,16,8,256]{3,2,1,0:T(8,128)S(1)} %get-tuple-element.14.wide, f32[2,17,16,128]{3,2,1,0:T(8,128)S(1)} %bitcast.9, f32[17,16,128]{2,1,0:T(8,128)S(1)} %collective-permute-done.2.from_far), custom_call_target="tpu_custom_call" | custom-call | tf_op jit(solution)/shard_map/pallas_call | solution.py:301
  23.7 12.9 %all_to_all.22 = f32[32,1,128]{2,1,0:T(1,128)S(1)} all-to-all(f32[32,1,128]{2,1,0:T(1,128)S(1)} %bitcast.13), channel_id=1, replica_groups=mesh['gx'=32,'gy'=16] {'gx'}, dimensions={0} | all-to-all | bytes 32768 | tf_op jit(solution)/shard_map/all_to_all | solution.py:345
  36.6 29.7 %all_to_all.23 = f32[16,1,128]{2,1,0:T(1,128)S(1)} all-to-all(f32[16,1,128]{2,1,0:T(1,128)S(1)} %bitcast.12), channel_id=1, replica_groups=mesh['gx'=32,'gy'=16] {'gy'}, dimensions={0} | all-to-all | bytes 16384 | tf_op jit(solution)/shard_map/all_to_all | solution.py:347
  66.4 1.1 %shard_map.63 = (f32[2,16,8,128]{3,2,1,0:T(8,128)}, f32[16,8,128]{2,1,0:T(8,128)}) custom-call(f32[16,128]{1,0:T(8,128)S(1)} %bitcast.11, f32[3,2,16,16,256]{4,3,2,1,0:T(8,128)S(1)} %get-tuple-element.18.basis, f32[2,16,16,256]{3,2,1,0:T(8,128)S(1)} %get-tuple-element.19.pots), custom_call_target="tpu_custom_call" | custom-call | tf_op jit(solution)/shard_map/pallas_call | solution.py:301
  (1 shorter events, 0.0 us)
Async XLA Ops:
  2.3 5.4 %collective-permute-start = (f32[2,8,128]{2,1,0:T(8,128)S(1)}, f32[2,8,128]{2,1,0:T(8,128)S(1)}, u32[]{:S(2)}, u32[]{:S(2)}) collective-permute-start(f32[2,8,128]{2,1,0:T(8,128)S(1)} %get-tuple-element.12), channel_id=1, source_target_pairs={{0,1},{2,3},{4,5},{6,7},{8,9},{10,11},{12,13},{14,15},{1,0},{3,2},... | collective-permute-start | bytes 24584 | tf_op jit(solution)/shard_map/ppermute | solution.py:319
  6.7 1.0 %collective-permute-start.1 = (f32[2,8,128]{2,1,0:T(8,128)S(1)}, f32[2,8,128]{2,1,0:T(8,128)S(1)}, u32[]{:S(2)}, u32[]{:S(2)}) collective-permute-start(f32[2,8,128]{2,1,0:T(8,128)S(1)} %get-tuple-element.13), channel_id=1, source_target_pairs={{1,2},{3,4},{5,6},{7,8},{9,10},{11,12},{13,14},{2,1},{4,3},{6,5},{... | collective-permute-start | bytes 24584 | tf_op jit(solution)/shard_map/ppermute | solution.py:319
  9.0 9.3 %collective-permute-start.2 = (f32[17,16,128]{2,1,0:T(8,128)S(1)}, f32[17,16,128]{2,1,0:T(8,128)S(1)}, u32[]{:S(2)}, u32[]{:S(2)}) collective-permute-start(f32[17,16,128]{2,1,0:T(8,128)S(1)} %get-tuple-element.16), channel_id=1, source_target_pairs={{16,32},{48,64},{80,96},{112,128},{144,160},{176,192},{208,224},{2... | collective-permute-start | bytes 417800 | tf_op jit(solution)/shard_map/ppermute | solution.py:319

commit v4 on v3

--- a/solution.py
+++ b/solution.py
@@ -339,12 +339,12 @@
     near = lax.all_gather(near, "gx", axis_index_groups=[[i, i + 1] for i in range(0, rows, 2)])
     sent, basis, pots = local(
         moments,
-        [(rows, 128), (3, 2, depth, 16, 256), (2, depth, 16, 256)],
+        [(cols, 128), (3, 2, depth, 16, 256), (2, depth, 16, 256)],
         [scratch(1, depth, 16, 256), scratch(4, depth, 16, 256)],
     )(wide, near, far)
+    received = lax.all_to_all(sent, "gy", 0, 0, tiled=True)
+    (sent,) = local(relay, [(rows, 128)])(received)
     received = lax.all_to_all(sent, "gx", 0, 0, tiled=True)
-    (sent,) = local(relay, [(cols, 128)])(received)
-    received = lax.all_to_all(sent, "gy", 0, 0, tiled=True)
     adjoint, gradient = local(
         finish, [cotangent.shape, conductance.shape], [scratch(2, depth, 16, 256)],
         kind=jax.ShapeDtypeStruct,

time: 67.8 us -> 69.1 us (1.019)
  blocking collectives: 47.2 us -> 48.7 us
    all_to_all x1, blocking collectives: 12.9 us -> 15.8 us  [per_device(): received = lax.all_to_all(sent, 'gx', 0, 0, tiled=True)]
    all_to_all x1, blocking collectives: 29.7 us -> 28.3 us  [per_device(): received = lax.all_to_all(sent, 'gy', 0, 0, tiled=True)]
where the time goes in v4:
time: 69.1 us; the launch traced here: 68.9 us
  blocking collectives  48.7 us (70%)
  starting transfers between devices  9.77 us (14%)
  Pallas kernels  9.44 us (14%)
    all_to_all x1, blocking collectives, per_device(): received = lax.all_to_all(sent, 'gy', 0, 0, tiled=True)  28.3 us
    all_to_all x1, blocking collectives, per_device(): received = lax.all_to_all(sent, 'gx', 0, 0, tiled=True)  15.8 us
    ppermute x3, starting transfers between devices, trade(): return lax.ppermute(x, axis, pairs + [(j, i) for i, j in pairs])  9.77 us
    pallas_call x5, Pallas kernels, call(): pl.pallas_call(body, out_shape=shapes, in_specs=[pl.BlockSpec(memory_spac...  9.44 us
    all_gather x1, blocking collectives, per_device(): lax.all_gather(near, 'gx', axis_index_groups=[[i, i + 1] for i in range(0...  4.6 us
  transfers between devices with their start and end apart: 3, of which 1 were waited for; matrix products, arithmetic and copies ran while one was open for 0% of the time, Pallas kernels for 0%

profile of v4, /device:TPU:1, one launch (start us, length us, event | category | flops | bytes accessed | tf_op | source)
XLA Modules:
  0.0 68.9 jit_solution(5901140943644788512)
XLA Ops:
  0.6 1.6 %shard_map.59 = (f32[2,8,128]{2,1,0:T(8,128)S(1)}, f32[2,8,128]{2,1,0:T(8,128)S(1)}, f32[6,16,8,128]{3,2,1,0:T(8,128)S(1)}) custom-call(f32[16,8,128]{2,1,0:T(8,128)} %cond_in.1, s32[16,8,128]{2,1,0:T(8,128)} %labels_in.1, f32[2,16,8,128]{3,2,1,0:T(8,128)} %cot_in.1, f32[2,16,8,128]{3,2,1,0:T(8,128)} %saved_in.1), custom_call_target="tpu_custom_call" | custom-call | tf_op jit(solution)/shard_map/pallas_call | solution.py:301
  2.3 4.4 %collective-permute-start = (f32[2,8,128]{2,1,0:T(8,128)S(1)}, f32[2,8,128]{2,1,0:T(8,128)S(1)}, u32[]{:S(2)}, u32[]{:S(2)}) collective-permute-start(f32[2,8,128]{2,1,0:T(8,128)S(1)} %get-tuple-element.12), channel_id=1, source_target_pairs={{0,1},{2,3},{4,5},{6,7},{8,9},{10,11},{12,13},{14,15},{1,0},{3,2},... | collective-permute-start | bytes 24584 | tf_op jit(solution)/shard_map/ppermute | solution.py:319
  6.7 0.7 collective-permute-start.1
  7.3 0.4 collective-permute-done.from_first
  7.7 0.0 collective-permute-done.1.from_second
  7.7 1.3 %shard_map.60 = (f32[6,16,8,256]{3,2,1,0:T(8,128)S(1)}, f32[17,16,128]{2,1,0:T(8,128)S(1)}, f32[17,16,128]{2,1,0:T(8,128)S(1)}) custom-call(f32[6,16,8,128]{3,2,1,0:T(8,128)S(1)} %get-tuple-element.11.field, f32[2,8,128]{2,1,0:T(8,128)S(1)} %collective-permute-done.from_first, f32[2,8,128]{2,1,0:T(8,128)S(1)} %collective-permute-done.1.from_second), custom_call_target="tpu_custom_call" | custom-call | tf_op jit(solution)/shard_map/pallas_call | solution.py:301
  9.0 4.7 %collective-permute-start.2 = (f32[17,16,128]{2,1,0:T(8,128)S(1)}, f32[17,16,128]{2,1,0:T(8,128)S(1)}, u32[]{:S(2)}, u32[]{:S(2)}) collective-permute-start(f32[17,16,128]{2,1,0:T(8,128)S(1)} %get-tuple-element.16), channel_id=1, source_target_pairs={{16,32},{48,64},{80,96},{112,128},{144,160},{176,192},{208,224},{2... | collective-permute-start | bytes 417800 | tf_op jit(solution)/shard_map/ppermute | solution.py:319
  13.8 4.6 %all-gather = f32[34,16,128]{2,1,0:T(8,128)S(1)} all-gather(f32[17,16,128]{2,1,0:T(8,128)S(1)} %get-tuple-element.15), channel_id=2, replica_groups={{0,16},{32,48},{64,80},{96,112},{128,144},{160,176},{192,208},{224,240}..., dimensions={0}, use_global_device_ids=true | all-gather | bytes 417792 | tf_op jit(solution)/shard_map/all_gather | solution.py:339
  18.4 0.0 collective-permute-done.2.from_far
  18.4 5.3 %shard_map.61 = (f32[16,128]{1,0:T(8,128)S(1)}, f32[3,2,16,16,256]{4,3,2,1,0:T(8,128)S(1)}, f32[2,16,16,256]{3,2,1,0:T(8,128)S(1)}) custom-call(f32[6,16,8,256]{3,2,1,0:T(8,128)S(1)} %get-tuple-element.14.wide, f32[2,17,16,128]{3,2,1,0:T(8,128)S(1)} %bitcast.9, f32[17,16,128]{2,1,0:T(8,128)S(1)} %collective-permute-done.2.from_far), custom_call_target="tpu_custom_call" | custom-call | tf_op jit(solution)/shard_map/pallas_call | solution.py:301
  23.7 28.3 %all_to_all.22 = f32[16,1,128]{2,1,0:T(1,128)S(1)} all-to-all(f32[16,1,128]{2,1,0:T(1,128)S(1)} %bitcast.13), channel_id=1, replica_groups=mesh['gx'=32,'gy'=16] {'gy'}, dimensions={0} | all-to-all | bytes 16384 | tf_op jit(solution)/shard_map/all_to_all | solution.py:345
  52.0 15.8 %all_to_all.23 = f32[32,1,128]{2,1,0:T(1,128)S(1)} all-to-all(f32[32,1,128]{2,1,0:T(1,128)S(1)} %bitcast.11), channel_id=1, replica_groups=mesh['gx'=32,'gy'=16] {'gx'}, dimensions={0} | all-to-all | bytes 32768 | tf_op jit(solution)/shard_map/all_to_all | solution.py:347
  67.8 1.1 %shard_map.63 = (f32[2,16,8,128]{3,2,1,0:T(8,128)}, f32[16,8,128]{2,1,0:T(8,128)}) custom-call(f32[32,128]{1,0:T(8,128)S(1)} %bitcast.10, f32[3,2,16,16,256]{4,3,2,1,0:T(8,128)S(1)} %get-tuple-element.18.basis, f32[2,16,16,256]{3,2,1,0:T(8,128)S(1)} %get-tuple-element.19.pots), custom_call_target="tpu_custom_call" | custom-call | tf_op jit(solution)/shard_map/pallas_call | solution.py:301
  (1 shorter events, 0.0 us)
Async XLA Ops:
  2.3 5.4 %collective-permute-start = (f32[2,8,128]{2,1,0:T(8,128)S(1)}, f32[2,8,128]{2,1,0:T(8,128)S(1)}, u32[]{:S(2)}, u32[]{:S(2)}) collective-permute-start(f32[2,8,128]{2,1,0:T(8,128)S(1)} %get-tuple-element.12), channel_id=1, source_target_pairs={{0,1},{2,3},{4,5},{6,7},{8,9},{10,11},{12,13},{14,15},{1,0},{3,2},... | collective-permute-start | bytes 24584 | tf_op jit(solution)/shard_map/ppermute | solution.py:319
  6.7 1.0 %collective-permute-start.1 = (f32[2,8,128]{2,1,0:T(8,128)S(1)}, f32[2,8,128]{2,1,0:T(8,128)S(1)}, u32[]{:S(2)}, u32[]{:S(2)}) collective-permute-start(f32[2,8,128]{2,1,0:T(8,128)S(1)} %get-tuple-element.13), channel_id=1, source_target_pairs={{1,2},{3,4},{5,6},{7,8},{9,10},{11,12},{13,14},{2,1},{4,3},{6,5},{... | collective-permute-start | bytes 24584 | tf_op jit(solution)/shard_map/ppermute | solution.py:319
  9.0 9.3 %collective-permute-start.2 = (f32[17,16,128]{2,1,0:T(8,128)S(1)}, f32[17,16,128]{2,1,0:T(8,128)S(1)}, u32[]{:S(2)}, u32[]{:S(2)}) collective-permute-start(f32[17,16,128]{2,1,0:T(8,128)S(1)} %get-tuple-element.16), channel_id=1, source_target_pairs={{16,32},{48,64},{80,96},{112,128},{144,160},{176,192},{208,224},{2... | collective-permute-start | bytes 417800 | tf_op jit(solution)/shard_map/ppermute | solution.py:319

commit v5 on v3

--- a/solution.py
+++ b/solution.py
@@ -123,7 +123,26 @@
     far[depth] = jnp.where(upper, ends[0], ends[1])
 
 
-def moments(wide, from_near, from_far, sent, basis, pots, field, weight):
+def exact_dot(x, matrix):
+    total = None
+    for _ in range(3):
+        term = x.astype(jnp.bfloat16)
+        x = x - term.astype(jnp.float32)
+        part = jnp.dot(term, matrix, preferred_element_type=jnp.float32)
+        total = part if total is None else total + part
+    return total
+
+
+def difference_matrices():
+    i = lax.broadcasted_iota(jnp.int32, (256, 256), 0)
+    j = lax.broadcasted_iota(jnp.int32, (256, 256), 1)
+    here = jnp.where(i == j, 1.0, 0.0)
+    forward = here - jnp.where(i == (j + 1) % 256, 1.0, 0.0)
+    backward = here - jnp.where((i + 1) % 256 == j, 1.0, 0.0)
+    return forward.astype(jnp.bfloat16), backward.astype(jnp.bfloat16)
+
+
+def moments(wide, from_near, from_far, sent, basis, pots, field, weight, flux):
     depth = wide.shape[1]
     core = lax.axis_index("gx") % 2
     lane16 = lanes_of((16, 128))
@@ -165,41 +184,49 @@
         if z + 1 < depth:
             weight[2, z] = 0.5 * (c + field[0, z + 1])
 
-    def image(read, k, z, carry):
-        u = read(k, z)
+    forward, backward = difference_matrices()
+
+    def image(k, z, source, carry):
+        u = basis[source, k, z]
         fx = weight[0, z] * (u - roll(u, -1, 0))
-        fy = weight[1, z] * (u - roll(u, -1, 1))
-        total = (fx - roll(fx, 1, 0)) + (fy - roll(fy, 1, 1)) - u
+        total = (fx - roll(fx, 1, 0)) + flux[k, z] - u
         if carry is not None:
             total = total - carry
         carry = None
         if z + 1 < depth:
-            carry = weight[2, z] * (u - read(k, z + 1))
+            carry = weight[2, z] * (u - basis[source, k, z + 1])
             total = total + carry
         return weight[3, z] * total, carry
 
+    def lane_fluxes(source, rows):
+        for k in range(2):
+            u = basis[source, k, :, 0:rows].reshape(depth * rows, 256)
+            f = weight[1, :, 0:rows].reshape(depth * rows, 256) * exact_dot(u, forward)
+            flux[k, :, 0:rows] = exact_dot(f, backward).reshape(depth, rows, 256)
+
     for power in range(2):
+        lane_fluxes(power, 16)
         for k in range(2):
             carry = None
             for z in range(depth):
-                value, carry = image(lambda k, z: basis[power, k, z], k, z, carry)
+                value, carry = image(k, z, power, carry)
                 basis[power + 1, k, z] = value
+    own = (slice(0, 8), slice(0, 128))
+
     def own_image(k, z, carry):
-        u = basis[2, k, z]
-        fx = weight[0, z, :, 0:128] * (u[:, 0:128] - roll(u[:, 0:128], -1, 0))
-        fx = (fx - roll(fx, 1, 0))[0:8]
+        u = basis[2, k, z, :, 0:128]
+        fx = weight[0, z, :, 0:128] * (u - roll(u, -1, 0))
         u = u[0:8]
-        fy = weight[1, z, 0:8] * (u - roll(u, -1, 1))
-        own = (slice(0, 8), slice(0, 128))
-        total = fx + (fy - roll(fy, 1, 1))[own] - u[own]
+        total = (fx - roll(fx, 1, 0))[0:8] + flux[k, z, 0:8, 0:128] - u
         if carry is not None:
             total = total - carry
         carry = None
         if z + 1 < depth:
-            carry = weight[2, z, 0:8, 0:128] * (u[own] - basis[2, k, z + 1, 0:8, 0:128])
+            carry = weight[2, z, 0:8, 0:128] * (u - basis[2, k, z + 1, 0:8, 0:128])
             total = total + carry
         return weight[3, z, 0:8, 0:128] * total, carry
 
+    lane_fluxes(2, 8)
     totals = []
     for k in range(2):
         sums = [jnp.zeros((8, 128), jnp.float32) for _ in range(6)]
@@ -340,7 +367,7 @@
     sent, basis, pots = local(
         moments,
         [(rows, 128), (3, 2, depth, 16, 256), (2, depth, 16, 256)],
-        [scratch(1, depth, 16, 256), scratch(4, depth, 16, 256)],
+        [scratch(1, depth, 16, 256), scratch(4, depth, 16, 256), scratch(2, depth, 16, 256)],
     )(wide, near, far)
     received = lax.all_to_all(sent, "gx", 0, 0, tiled=True)
     (sent,) = local(relay, [(cols, 128)])(received)

time: 67.8 us -> 64.8 us (0.956)
  Pallas kernels: 9.48 us -> 6.47 us
    pallas_call x5, Pallas kernels: 9.48 us -> 6.47 us  [call(): pl.pallas_call(body, out_shape=shapes, in_specs=[pl.BlockSpec(memory_spac...]
where the time goes in v5:
time: 64.8 us; the launch traced here: 64.5 us
  blocking collectives  47.2 us (73%)
  starting transfers between devices  9.77 us (15%)
  Pallas kernels  6.47 us (10%)
  between operations  0.67 us (1%)
    all_to_all x1, blocking collectives, per_device(): received = lax.all_to_all(sent, 'gy', 0, 0, tiled=True)  29.7 us
    all_to_all x1, blocking collectives, per_device(): received = lax.all_to_all(sent, 'gx', 0, 0, tiled=True)  12.9 us
    ppermute x3, starting transfers between devices, trade(): return lax.ppermute(x, axis, pairs + [(j, i) for i, j in pairs])  9.77 us
    pallas_call x5, Pallas kernels, call(): pl.pallas_call(body, out_shape=shapes, in_specs=[pl.BlockSpec(memory_spac...  6.47 us
    all_gather x1, blocking collectives, per_device(): lax.all_gather(near, 'gx', axis_index_groups=[[i, i + 1] for i in range(0...  4.6 us
  transfers between devices with their start and end apart: 3, of which 1 were waited for; matrix products, arithmetic and copies ran while one was open for 0% of the time, Pallas kernels for 0%

profile of v5, /device:TPU:1, one launch (start us, length us, event | category | flops | bytes accessed | tf_op | source)
XLA Modules:
  0.0 64.5 jit_solution(12181105435207954480)
XLA Ops:
  0.6 1.6 %shard_map.59 = (f32[2,8,128]{2,1,0:T(8,128)S(1)}, f32[2,8,128]{2,1,0:T(8,128)S(1)}, f32[6,16,8,128]{3,2,1,0:T(8,128)S(1)}) custom-call(f32[16,8,128]{2,1,0:T(8,128)} %cond_in.1, s32[16,8,128]{2,1,0:T(8,128)} %labels_in.1, f32[2,16,8,128]{3,2,1,0:T(8,128)} %cot_in.1, f32[2,16,8,128]{3,2,1,0:T(8,128)} %saved_in.1), custom_call_target="tpu_custom_call" | custom-call | tf_op jit(solution)/shard_map/pallas_call | solution.py:328
  2.3 4.4 %collective-permute-start = (f32[2,8,128]{2,1,0:T(8,128)S(1)}, f32[2,8,128]{2,1,0:T(8,128)S(1)}, u32[]{:S(2)}, u32[]{:S(2)}) collective-permute-start(f32[2,8,128]{2,1,0:T(8,128)S(1)} %get-tuple-element.12), channel_id=1, source_target_pairs={{0,1},{2,3},{4,5},{6,7},{8,9},{10,11},{12,13},{14,15},{1,0},{3,2},... | collective-permute-start | bytes 24584 | tf_op jit(solution)/shard_map/ppermute | solution.py:346
  6.7 0.7 %collective-permute-start.1 = (f32[2,8,128]{2,1,0:T(8,128)S(1)}, f32[2,8,128]{2,1,0:T(8,128)S(1)}, u32[]{:S(2)}, u32[]{:S(2)}) collective-permute-start(f32[2,8,128]{2,1,0:T(8,128)S(1)} %get-tuple-element.13), channel_id=1, source_target_pairs={{1,2},{3,4},{5,6},{7,8},{9,10},{11,12},{13,14},{2,1},{4,3},{6,5},{... | collective-permute-start | bytes 24584 | tf_op jit(solution)/shard_map/ppermute | solution.py:346
  7.3 0.4 collective-permute-done.from_first
  7.7 0.0 collective-permute-done.1.from_second
  7.7 1.3 %shard_map.60 = (f32[6,16,8,256]{3,2,1,0:T(8,128)S(1)}, f32[17,16,128]{2,1,0:T(8,128)S(1)}, f32[17,16,128]{2,1,0:T(8,128)S(1)}) custom-call(f32[6,16,8,128]{3,2,1,0:T(8,128)S(1)} %get-tuple-element.11.field, f32[2,8,128]{2,1,0:T(8,128)S(1)} %collective-permute-done.from_first, f32[2,8,128]{2,1,0:T(8,128)S(1)} %collective-permute-done.1.from_second), custom_call_target="tpu_custom_call" | custom-call | tf_op jit(solution)/shard_map/pallas_call | solution.py:328
  9.0 4.7 %collective-permute-start.2 = (f32[17,16,128]{2,1,0:T(8,128)S(1)}, f32[17,16,128]{2,1,0:T(8,128)S(1)}, u32[]{:S(2)}, u32[]{:S(2)}) collective-permute-start(f32[17,16,128]{2,1,0:T(8,128)S(1)} %get-tuple-element.16), channel_id=1, source_target_pairs={{16,32},{48,64},{80,96},{112,128},{144,160},{176,192},{208,224},{2... | collective-permute-start | bytes 417800 | tf_op jit(solution)/shard_map/ppermute | solution.py:346
  13.8 4.6 %all-gather = f32[34,16,128]{2,1,0:T(8,128)S(1)} all-gather(f32[17,16,128]{2,1,0:T(8,128)S(1)} %get-tuple-element.15), channel_id=2, replica_groups={{0,16},{32,48},{64,80},{96,112},{128,144},{160,176},{192,208},{224,240}..., dimensions={0}, use_global_device_ids=true | all-gather | bytes 417792 | tf_op jit(solution)/shard_map/all_gather | solution.py:366
  18.4 0.0 collective-permute-done.2.from_far
  18.4 2.3 %shard_map.61 = (f32[32,128]{1,0:T(8,128)S(1)}, f32[3,2,16,16,256]{4,3,2,1,0:T(8,128)S(1)}, f32[2,16,16,256]{3,2,1,0:T(8,128)S(1)}) custom-call(f32[6,16,8,256]{3,2,1,0:T(8,128)S(1)} %get-tuple-element.14.wide, f32[2,17,16,128]{3,2,1,0:T(8,128)S(1)} %bitcast.9, f32[17,16,128]{2,1,0:T(8,128)S(1)} %collective-permute-done.2.from_far), custom_call_target="tpu_custom_call" | custom-call | tf_op jit(solution)/shard_map/pallas_call | solution.py:328
  20.7 12.9 %all_to_all.22 = f32[32,1,128]{2,1,0:T(1,128)S(1)} all-to-all(f32[32,1,128]{2,1,0:T(1,128)S(1)} %bitcast.13), channel_id=1, replica_groups=mesh['gx'=32,'gy'=16] {'gx'}, dimensions={0} | all-to-all | bytes 32768 | tf_op jit(solution)/shard_map/all_to_all | solution.py:372
  33.6 29.7 %all_to_all.23 = f32[16,1,128]{2,1,0:T(1,128)S(1)} all-to-all(f32[16,1,128]{2,1,0:T(1,128)S(1)} %bitcast.12), channel_id=1, replica_groups=mesh['gx'=32,'gy'=16] {'gy'}, dimensions={0} | all-to-all | bytes 16384 | tf_op jit(solution)/shard_map/all_to_all | solution.py:374
  63.4 1.1 %shard_map.63 = (f32[2,16,8,128]{3,2,1,0:T(8,128)}, f32[16,8,128]{2,1,0:T(8,128)}) custom-call(f32[16,128]{1,0:T(8,128)S(1)} %bitcast.11, f32[3,2,16,16,256]{4,3,2,1,0:T(8,128)S(1)} %get-tuple-element.18.basis, f32[2,16,16,256]{3,2,1,0:T(8,128)S(1)} %get-tuple-element.19.pots), custom_call_target="tpu_custom_call" | custom-call | tf_op jit(solution)/shard_map/pallas_call | solution.py:328
  (1 shorter events, 0.0 us)
Async XLA Ops:
  2.3 5.4 %collective-permute-start = (f32[2,8,128]{2,1,0:T(8,128)S(1)}, f32[2,8,128]{2,1,0:T(8,128)S(1)}, u32[]{:S(2)}, u32[]{:S(2)}) collective-permute-start(f32[2,8,128]{2,1,0:T(8,128)S(1)} %get-tuple-element.12), channel_id=1, source_target_pairs={{0,1},{2,3},{4,5},{6,7},{8,9},{10,11},{12,13},{14,15},{1,0},{3,2},... | collective-permute-start | bytes 24584 | tf_op jit(solution)/shard_map/ppermute | solution.py:346
  6.7 1.0 %collective-permute-start.1 = (f32[2,8,128]{2,1,0:T(8,128)S(1)}, f32[2,8,128]{2,1,0:T(8,128)S(1)}, u32[]{:S(2)}, u32[]{:S(2)}) collective-permute-start(f32[2,8,128]{2,1,0:T(8,128)S(1)} %get-tuple-element.13), channel_id=1, source_target_pairs={{1,2},{3,4},{5,6},{7,8},{9,10},{11,12},{13,14},{2,1},{4,3},{6,5},{... | collective-permute-start | bytes 24584 | tf_op jit(solution)/shard_map/ppermute | solution.py:346
  9.0 9.3 %collective-permute-start.2 = (f32[17,16,128]{2,1,0:T(8,128)S(1)}, f32[17,16,128]{2,1,0:T(8,128)S(1)}, u32[]{:S(2)}, u32[]{:S(2)}) collective-permute-start(f32[17,16,128]{2,1,0:T(8,128)S(1)} %get-tuple-element.16), channel_id=1, source_target_pairs={{16,32},{48,64},{80,96},{112,128},{144,160},{176,192},{208,224},{2... | collective-permute-start | bytes 417800 | tf_op jit(solution)/shard_map/ppermute | solution.py:346

commit v6 on v3

--- a/solution.py
+++ b/solution.py
@@ -37,6 +37,34 @@
     return (index >= low) & (index < low + count)
 
 
+def exact_dot(x, matrix):
+    total = None
+    for _ in range(3):
+        term = x.astype(jnp.bfloat16)
+        x = x - term.astype(jnp.float32)
+        part = jnp.dot(term, matrix, preferred_element_type=jnp.float32)
+        total = part if total is None else total + part
+    return total
+
+
+def difference_matrices():
+    i = lax.broadcasted_iota(jnp.int32, (256, 256), 0)
+    j = lax.broadcasted_iota(jnp.int32, (256, 256), 1)
+    here = jnp.where(i == j, 1.0, 0.0)
+    forward = here - jnp.where(i == (j + 1) % 256, 1.0, 0.0)
+    backward = here - jnp.where((i + 1) % 256 == j, 1.0, 0.0)
+    return forward.astype(jnp.bfloat16), backward.astype(jnp.bfloat16)
+
+
+def place(shape, rows, cols, pairs):
+    i = lax.broadcasted_iota(jnp.int32, shape, rows)
+    j = lax.broadcasted_iota(jnp.int32, shape, cols)
+    hit = i < 0
+    for row, col, count in pairs:
+        hit |= within(i, row, count) & (j - i == col - row)
+    return jnp.where(hit, 1.0, 0.0).astype(jnp.bfloat16)
+
+
 def pack_columns(cond_in, labels_in, cot_in, saved_in, first, second, field, cond, labels, cot, saved, sems):
     copies = [
         pltpu.make_async_copy(source, target, sems.at[i])
@@ -46,102 +74,110 @@
     ]
     for copy in copies:
         copy.start()
+    picks = [
+        place(
+            (128, 128),
+            0,
+            1,
+            [(0, LANE[f], WIDTH[f]), (128 - WIDTH[f], GROUP + LANE[f], WIDTH[f])],
+        )
+        for f in range(6)
+    ]
     for copy in copies:
         copy.wait()
     even = lax.axis_index("gy") % 2 == 0
-    lane = lanes_of()
-    place = [within(lane, LANE[f], WIDTH[f]) for f in range(6)]
     depth = cond.shape[0]
-    per = 128 // GROUP
-    for tile in range(depth // per):
-        left_tile = jnp.zeros((8, 128), jnp.float32)
-        right_tile = left_tile
-        for j in range(per):
-            z = tile * per + j
-            fields = fields_at(cond, labels, cot, saved, z)
-            low = jnp.zeros((8, 128), jnp.float32)
-            high = low
-            for f, x in enumerate(fields):
-                field[f, z] = x
-                low = jnp.where(place[f], roll(x, LANE[f], 1), low)
-                high = jnp.where(place[f], roll(x, LANE[f] + WIDTH[f], 1), high)
-            here = within(lane, j * GROUP, GROUP)
-            left_tile = jnp.where(here, roll(low, j * GROUP, 1), left_tile)
-            right_tile = jnp.where(here, roll(high, j * GROUP, 1), right_tile)
-        first[tile] = jnp.where(even, right_tile, left_tile)
-        second[tile] = jnp.where(even, left_tile, right_tile)
-
-
-def widen(field, from_first, from_second, wide, near, far):
+    for z in range(depth):
+        for f, x in enumerate(fields_at(cond, labels, cot, saved, z)):
+            field[f, z] = x
+    total = None
+    for f in range(6):
+        part = exact_dot(field[f].reshape(depth * 8, 128), picks[f])
+        total = part if total is None else total + part
+    columns = total.T
+    left, right = columns[0:GROUP], columns[GROUP : 2 * GROUP]
+    first[...] = jnp.where(even, right, left)
+    second[...] = jnp.where(even, left, right)
+
+
+def unpack_columns(left, right, out):
+    packed = jnp.concatenate([left, right], axis=0).T
+    for f in range(6):
+        w = WIDTH[f]
+        matrix = place(
+            (2 * GROUP, 128), 0, 1, [(LANE[f], 128 - w, w), (GROUP + LANE[f], 0, w)]
+        )
+        out[:, f * 128 : (f + 1) * 128] = exact_dot(packed, matrix)
+
+
+def widen(field, sent_first, sent_second, from_first, from_second, wide, near, far, halo):
     even = lax.axis_index("gy") % 2 == 0
     upper = lax.axis_index("gx") % 2 == 0
-    lane = lanes_of()
-    lane16 = lanes_of((16, 128))
     depth = field.shape[1]
-    per = 128 // GROUP
-    zero = jnp.zeros((8, 128), jnp.float32)
-    ends = [jnp.zeros((16, 128), jnp.float32) for _ in range(2)]
+    slot = lax.broadcasted_iota(jnp.int32, (GROUP, 128), 0)
+    c = LANE[COND]
+
+    def choose(a, b):
+        return jnp.where(even, a[...], b[...])
+
+    left, right = choose(from_second, from_first), choose(from_first, from_second)
+    own_left, own_right = choose(sent_second, sent_first), choose(sent_first, sent_second)
+    pot = (slot == LANE[POT1]) | (slot == LANE[POT2])
+    outside = right[c : c + 1] == 0.0
+    right = jnp.where(outside & (slot == c), -roll(own_right, -2, 0), right)
+    right = jnp.where(outside & pot, own_right, right)
+    outside = left[c + 2 : c + 3] == 0.0
+    left = jnp.where(outside & (slot == c + 2), -roll(own_left, 2, 0), left)
+    left = jnp.where(outside & pot, own_left, left)
+    near[depth] = left
+    near[depth + 1] = right
+    far[depth] = left
+    far[depth + 1] = right
+    unpack_columns(left, right, halo)
     for z in range(depth):
         fields = [field[f, z] for f in range(6)]
-        tile, base = z // per, (z % per) * GROUP
-        low = roll(jnp.where(even, from_second[tile], from_first[tile]), -base, 1)
-        high = roll(jnp.where(even, from_first[tile], from_second[tile]), -base, 1)
-        halos = []
-        for f in range(6):
-            w = WIDTH[f]
-            before = roll(low, 128 - w - LANE[f], 1)
-            after = roll(high, -LANE[f], 1)
-            halos.append(jnp.where(lane < w, after, jnp.where(lane >= 128 - w, before, zero)))
-        outside = (halos[COND] == 0.0) & ((lane == 0) | (lane == 127))
-
-        def edge_value(x):
-            return jnp.where(lane == 0, roll(x, 1, 1), roll(x, -1, 1))
-
-        halos[COND] = jnp.where(outside, -edge_value(fields[COND]), halos[COND])
-        for f in (POT1, POT2):
-            halos[f] = jnp.where(outside, edge_value(fields[f]), halos[f])
         for f in range(6):
             wide[f, z, :, 0:128] = fields[f]
-            wide[f, z, :, 128:256] = halos[f]
-        own, end = [], []
+            wide[f, z, :, 128:256] = halo[8 * z : 8 * z + 8, f * 128 : (f + 1) * 128]
+        own = []
         for side in range(2):
-            rows, tips = [], []
+            rows = []
             for f in (COND, RES1, MASK, RES2, POT1, POT2):
                 w = WIDTH[f]
                 start = 0 if side == 0 else 8 - w
                 rows.append(fields[f][start : start + w])
-                tips.append(halos[f][start : start + w])
-            blank = [jnp.zeros((3, 128), jnp.float32)]
-            own.append(jnp.concatenate(rows + blank, axis=0))
-            end.append(jnp.concatenate(tips + blank, axis=0))
-        where = (lane16 + (128 - 8 * z + 3)) % 128 < 6
+            own.append(jnp.concatenate(rows + [jnp.zeros((3, 128), jnp.float32)], axis=0))
         near[z] = jnp.where(upper, own[1], own[0])
         far[z] = jnp.where(upper, own[0], own[1])
-        for side in range(2):
-            ends[side] = jnp.where(where, roll(end[side], 8 * z, 1), ends[side])
-    near[depth] = jnp.where(upper, ends[1], ends[0])
-    far[depth] = jnp.where(upper, ends[0], ends[1])
-
-
-def moments(wide, from_near, from_far, sent, basis, pots, field, weight):
+
+
+def moments(wide, from_near, from_far, sent, basis, pots, field, weight, flux, corner):
     depth = wide.shape[1]
     core = lax.axis_index("gx") % 2
     lane16 = lanes_of((16, 128))
-    keep = (lane16 < 3) | (lane16 >= 125)
     row8 = lax.broadcasted_iota(jnp.int32, (8, 256), 0)
+
+    def above(i):
+        return jnp.where(core == 0, from_far[i], from_near[1 - core, i])
+
+    def below(i):
+        return jnp.where(core == 0, from_near[1 - core, i], from_far[i])
+
+    for side, source in enumerate((above, below)):
+        unpack_columns(source(depth), source(depth + 1), corner.at[side])
     for z in range(depth):
-        halo = []
-        for source in (lambda i: from_near[1 - core, i], lambda i: from_far[i]):
-            end = jnp.where(keep, roll(source(depth), -8 * z, 1), 0.0)
-            halo.append(jnp.concatenate([source(z), end], axis=1))
-        top = jnp.where(core == 0, halo[1], halo[0])
-        bottom = jnp.where(core == 0, halo[0], halo[1])
+        top, bottom = above(z), below(z)
         parts = []
         for f in range(6):
             w, s = WIDTH[f], SLOT[f]
             own = wide[f, z]
-            gap = jnp.zeros((8 - 2 * w, 256), jnp.float32)
-            parts.append((own, jnp.concatenate([bottom[s : s + w], gap, top[s : s + w]], axis=0)))
+            gap = jnp.zeros((8 - 2 * w, 128), jnp.float32)
+            low = jnp.concatenate([bottom[s : s + w], gap, top[s : s + w]], axis=0)
+            tips = [
+                corner[side, 8 * z : 8 * z + 8, f * 128 : (f + 1) * 128] for side in range(2)
+            ]
+            high = jnp.concatenate([tips[1][0:w], gap, tips[0][8 - w : 8]], axis=0)
+            parts.append((own, jnp.concatenate([low, high], axis=1)))
         own, other = parts[COND]
         outside = (other == 0.0) & ((row8 == 0) | (row8 == 7))
 
@@ -165,41 +201,49 @@
         if z + 1 < depth:
             weight[2, z] = 0.5 * (c + field[0, z + 1])
 
-    def image(read, k, z, carry):
-        u = read(k, z)
+    forward, backward = difference_matrices()
+
+    def image(k, z, source, carry):
+        u = basis[source, k, z]
         fx = weight[0, z] * (u - roll(u, -1, 0))
-        fy = weight[1, z] * (u - roll(u, -1, 1))
-        total = (fx - roll(fx, 1, 0)) + (fy - roll(fy, 1, 1)) - u
+        total = (fx - roll(fx, 1, 0)) + flux[k, z] - u
         if carry is not None:
             total = total - carry
         carry = None
         if z + 1 < depth:
-            carry = weight[2, z] * (u - read(k, z + 1))
+            carry = weight[2, z] * (u - basis[source, k, z + 1])
             total = total + carry
         return weight[3, z] * total, carry
 
+    def lane_fluxes(source, rows):
+        for k in range(2):
+            u = basis[source, k, :, 0:rows].reshape(depth * rows, 256)
+            f = weight[1, :, 0:rows].reshape(depth * rows, 256) * exact_dot(u, forward)
+            flux[k, :, 0:rows] = exact_dot(f, backward).reshape(depth, rows, 256)
+
     for power in range(2):
+        lane_fluxes(power, 16)
         for k in range(2):
             carry = None
             for z in range(depth):
-                value, carry = image(lambda k, z: basis[power, k, z], k, z, carry)
+                value, carry = image(k, z, power, carry)
                 basis[power + 1, k, z] = value
+    own = (slice(0, 8), slice(0, 128))
+
     def own_image(k, z, carry):
-        u = basis[2, k, z]
-        fx = weight[0, z, :, 0:128] * (u[:, 0:128] - roll(u[:, 0:128], -1, 0))
-        fx = (fx - roll(fx, 1, 0))[0:8]
+        u = basis[2, k, z, :, 0:128]
+        fx = weight[0, z, :, 0:128] * (u - roll(u, -1, 0))
         u = u[0:8]
-        fy = weight[1, z, 0:8] * (u - roll(u, -1, 1))
-        own = (slice(0, 8), slice(0, 128))
-        total = fx + (fy - roll(fy, 1, 1))[own] - u[own]
+        total = (fx - roll(fx, 1, 0))[0:8] + flux[k, z, 0:8, 0:128] - u
         if carry is not None:
             total = total - carry
         carry = None
         if z + 1 < depth:
-            carry = weight[2, z, 0:8, 0:128] * (u[own] - basis[2, k, z + 1, 0:8, 0:128])
+            carry = weight[2, z, 0:8, 0:128] * (u - basis[2, k, z + 1, 0:8, 0:128])
             total = total + carry
         return weight[3, z, 0:8, 0:128] * total, carry
 
+    lane_fluxes(2, 8)
     totals = []
     for k in range(2):
         sums = [jnp.zeros((8, 128), jnp.float32) for _ in range(6)]
@@ -251,7 +295,7 @@
         norm = new
 
 
-def finish(received, basis, pots, adjoint, gradient, field):
+def finish(received, basis, pots, adjoint, gradient, field, lanes):
     depth = basis.shape[2]
     row = jnp.sum(received[...], axis=0, keepdims=True)
     row = jnp.broadcast_to(row, (8, 128))
@@ -270,21 +314,29 @@
             value = c[0] * basis[0, k, z] + c[1] * basis[1, k, z] + c[2] * basis[2, k, z]
             field[k, z] = value
             adjoint[k, z] = value[0:8, 0:128]
+    forward, _ = difference_matrices()
+    i = lax.broadcasted_iota(jnp.int32, (256, 256), 0)
+    j = lax.broadcasted_iota(jnp.int32, (256, 256), 1)
+    both = jnp.where((i == j) | ((i + 1) % 256 == j), 1.0, 0.0).astype(jnp.bfloat16)
+    gy = None
+    for k in range(2):
+        a, p = (x[k, :, 0:8].reshape(depth * 8, 256) for x in (field, pots))
+        term = exact_dot(a, forward) * exact_dot(p, forward)
+        gy = term if gy is None else gy + term
+    lanes[...] = exact_dot(gy, both[:, 0:128])
     carry = None
     for z in range(depth):
-        gx = gy = gz = None
+        gx = gz = None
         for k in range(2):
-            a, p = field[k, z], pots[k, z]
+            a, p = field[k, z, :, 0:128], pots[k, z, :, 0:128]
             tx = (a - roll(a, -1, 0)) * (p - roll(p, -1, 0))
-            ty = (a - roll(a, -1, 1)) * (p - roll(p, -1, 1))
             gx = tx if gx is None else gx + tx
-            gy = ty if gy is None else gy + ty
             if z + 1 < depth:
-                tz = (a[0:8, 0:128] - field[k, z + 1, 0:8, 0:128]) * (
-                    p[0:8, 0:128] - pots[k, z + 1, 0:8, 0:128]
+                tz = (a[0:8] - field[k, z + 1, 0:8, 0:128]) * (
+                    p[0:8] - pots[k, z + 1, 0:8, 0:128]
                 )
                 gz = tz if gz is None else gz + tz
-        total = (gx + roll(gx, 1, 0) + gy + roll(gy, 1, 1))[0:8, 0:128]
+        total = (gx + roll(gx, 1, 0))[0:8] + lanes[8 * z : 8 * z + 8]
         if carry is not None:
             total = total + carry
         if gz is not None:
@@ -323,30 +375,33 @@
     depth = conductance.shape[0]
     rows, cols = lax.axis_size("gx"), lax.axis_size("gy")
     args = (conductance, labels, cotangent, saved)
-    tiles = depth * GROUP // 128
     first, second, field = local(
         pack_columns,
-        [(tiles, 8, 128)] * 2 + [(6, depth, 8, 128)],
+        [(GROUP, depth * 8)] * 2 + [(6, depth, 8, 128)],
         [scratch(*x.shape, dtype=x.dtype) for x in args] + [pltpu.SemaphoreType.DMA((4,))],
         pltpu.HBM,
         56 * 2**20,
     )(*args)
-    first, second = trade(first, "gy", 0), trade(second, "gy", 1)
-    wide, near, far = local(widen, [(6, depth, 8, 256)] + [(depth + 1, 16, 128)] * 2)(
-        field, first, second
-    )
+    from_first, from_second = trade(first, "gy", 0), trade(second, "gy", 1)
+    wide, near, far = local(
+        widen,
+        [(6, depth, 8, 256)] + [(depth + 2, 16, 128)] * 2,
+        [scratch(depth * 8, 768)],
+    )(field, first, second, from_first, from_second)
     far = trade(far, "gx", 1)
     near = lax.all_gather(near, "gx", axis_index_groups=[[i, i + 1] for i in range(0, rows, 2)])
     sent, basis, pots = local(
         moments,
         [(rows, 128), (3, 2, depth, 16, 256), (2, depth, 16, 256)],
-        [scratch(1, depth, 16, 256), scratch(4, depth, 16, 256)],
+        [scratch(1, depth, 16, 256), scratch(4, depth, 16, 256), scratch(2, depth, 16, 256), scratch(2, depth * 8, 768)],
     )(wide, near, far)
     received = lax.all_to_all(sent, "gx", 0, 0, tiled=True)
     (sent,) = local(relay, [(cols, 128)])(received)
     received = lax.all_to_all(sent, "gy", 0, 0, tiled=True)
     adjoint, gradient = local(
-        finish, [cotangent.shape, conductance.shape], [scratch(2, depth, 16, 256)],
+        finish,
+        [cotangent.shape, conductance.shape],
+        [scratch(2, depth, 16, 256), scratch(depth * 8, 128)],
         kind=jax.ShapeDtypeStruct,
     )(received, basis, pots)
     return adjoint, gradient

time: 67.8 us -> 64.3 us (0.948)
  Pallas kernels: 9.48 us -> 5.92 us
    pallas_call x5, Pallas kernels: 9.48 us -> 5.92 us  [call(): pl.pallas_call(body, out_shape=shapes, in_specs=[pl.BlockSpec(memory_spac...]
where the time goes in v6:
time: 64.3 us; the launch traced here: 64.1 us
  blocking collectives  47.3 us (74%)
  starting transfers between devices  9.77 us (15%)
  Pallas kernels  5.92 us (9%)
  between operations  0.67 us (1%)
    all_to_all x1, blocking collectives, per_device(): received = lax.all_to_all(sent, 'gy', 0, 0, tiled=True)  29.7 us
    all_to_all x1, blocking collectives, per_device(): received = lax.all_to_all(sent, 'gx', 0, 0, tiled=True)  13 us
    ppermute x3, starting transfers between devices, trade(): return lax.ppermute(x, axis, pairs + [(j, i) for i, j in pairs])  9.77 us
    pallas_call x5, Pallas kernels, call(): pl.pallas_call(body, out_shape=shapes, in_specs=[pl.BlockSpec(memory_spac...  5.92 us
    all_gather x1, blocking collectives, per_device(): lax.all_gather(near, 'gx', axis_index_groups=[[i, i + 1] for i in range(0...  4.6 us
  transfers between devices with their start and end apart: 3, of which 1 were waited for; matrix products, arithmetic and copies ran while one was open for 0% of the time, Pallas kernels for 0%

profile of v6, /device:TPU:1, one launch (start us, length us, event | category | flops | bytes accessed | tf_op | source)
XLA Modules:
  0.0 64.1 jit_solution(125402294380431278)
XLA Ops:
  0.6 1.5 %shard_map.59 = (f32[16,128]{1,0:T(8,128)S(1)}, f32[16,128]{1,0:T(8,128)S(1)}, f32[6,16,8,128]{3,2,1,0:T(8,128)S(1)}) custom-call(f32[16,8,128]{2,1,0:T(8,128)} %cond_in.1, s32[16,8,128]{2,1,0:T(8,128)} %labels_in.1, f32[2,16,8,128]{3,2,1,0:T(8,128)} %cot_in.1, f32[2,16,8,128]{3,2,1,0:T(8,128)} %saved_in.1), custom_call_target="tpu_custom_call" | custom-call | tf_op jit(solution)/shard_map/pallas_call | solution.py:353
  2.1 4.4 %collective-permute-start = (f32[16,128]{1,0:T(8,128)S(1)}, f32[16,128]{1,0:T(8,128)S(1)}, u32[]{:S(2)}, u32[]{:S(2)}) collective-permute-start(f32[16,128]{1,0:T(8,128)S(1)} %get-tuple-element.12.sent_first), channel_id=1, source_target_pairs={{0,1},{2,3},{4,5},{6,7},{8,9},{10,11},{12,13},{14,15},{1,0},{3,2},... | collective-permute-start | bytes 24584 | tf_op jit(solution)/shard_map/ppermute | solution.py:371
  6.5 0.7 %collective-permute-start.1 = (f32[16,128]{1,0:T(8,128)S(1)}, f32[16,128]{1,0:T(8,128)S(1)}, u32[]{:S(2)}, u32[]{:S(2)}) collective-permute-start(f32[16,128]{1,0:T(8,128)S(1)} %get-tuple-element.13.sent_second), channel_id=1, source_target_pairs={{1,2},{3,4},{5,6},{7,8},{9,10},{11,12},{13,14},{2,1},{4,3},{6,5},{... | collective-permute-start | bytes 24584 | tf_op jit(solution)/shard_map/ppermute | solution.py:371
  7.1 0.4 collective-permute-done.from_first
  7.5 0.0 collective-permute-done.1.from_second
  7.5 0.4 shard_map.60
  7.9 4.7 %collective-permute-start.2 = (f32[18,16,128]{2,1,0:T(8,128)S(1)}, f32[18,16,128]{2,1,0:T(8,128)S(1)}, u32[]{:S(2)}, u32[]{:S(2)}) collective-permute-start(f32[18,16,128]{2,1,0:T(8,128)S(1)} %get-tuple-element.16), channel_id=1, source_target_pairs={{16,32},{48,64},{80,96},{112,128},{144,160},{176,192},{208,224},{2... | collective-permute-start | bytes 442376 | tf_op jit(solution)/shard_map/ppermute | solution.py:371
  12.7 4.6 %all-gather = f32[36,16,128]{2,1,0:T(8,128)S(1)} all-gather(f32[18,16,128]{2,1,0:T(8,128)S(1)} %get-tuple-element.15), channel_id=2, replica_groups={{0,16},{32,48},{64,80},{96,112},{128,144},{160,176},{192,208},{224,240}..., dimensions={0}, use_global_device_ids=true | all-gather | bytes 442368 | tf_op jit(solution)/shard_map/all_gather | solution.py:392
  17.3 0.0 collective-permute-done.2.from_far
  17.3 2.6 %shard_map.61 = (f32[32,128]{1,0:T(8,128)S(1)}, f32[3,2,16,16,256]{4,3,2,1,0:T(8,128)S(1)}, f32[2,16,16,256]{3,2,1,0:T(8,128)S(1)}) custom-call(f32[6,16,8,256]{3,2,1,0:T(8,128)S(1)} %get-tuple-element.14.wide, f32[2,18,16,128]{3,2,1,0:T(8,128)S(1)} %bitcast.9, f32[18,16,128]{2,1,0:T(8,128)S(1)} %collective-permute-done.2.from_far), custom_call_target="tpu_custom_call" | custom-call | tf_op jit(solution)/shard_map/pallas_call | solution.py:353
  19.9 13.0 %all_to_all.22 = f32[32,1,128]{2,1,0:T(1,128)S(1)} all-to-all(f32[32,1,128]{2,1,0:T(1,128)S(1)} %bitcast.13), channel_id=1, replica_groups=mesh['gx'=32,'gy'=16] {'gx'}, dimensions={0} | all-to-all | bytes 32768 | tf_op jit(solution)/shard_map/all_to_all | solution.py:398
  32.9 29.7 %all_to_all.23 = f32[16,1,128]{2,1,0:T(1,128)S(1)} all-to-all(f32[16,1,128]{2,1,0:T(1,128)S(1)} %bitcast.12), channel_id=1, replica_groups=mesh['gx'=32,'gy'=16] {'gy'}, dimensions={0} | all-to-all | bytes 16384 | tf_op jit(solution)/shard_map/all_to_all | solution.py:400
  62.7 1.4 %shard_map.63 = (f32[2,16,8,128]{3,2,1,0:T(8,128)}, f32[16,8,128]{2,1,0:T(8,128)}) custom-call(f32[16,128]{1,0:T(8,128)S(1)} %bitcast.11, f32[3,2,16,16,256]{4,3,2,1,0:T(8,128)S(1)} %get-tuple-element.18.basis, f32[2,16,16,256]{3,2,1,0:T(8,128)S(1)} %get-tuple-element.19.pots), custom_call_target="tpu_custom_call" | custom-call | tf_op jit(solution)/shard_map/pallas_call | solution.py:353
  (1 shorter events, 0.0 us)
Async XLA Ops:
  2.1 5.4 %collective-permute-start = (f32[16,128]{1,0:T(8,128)S(1)}, f32[16,128]{1,0:T(8,128)S(1)}, u32[]{:S(2)}, u32[]{:S(2)}) collective-permute-start(f32[16,128]{1,0:T(8,128)S(1)} %get-tuple-element.12.sent_first), channel_id=1, source_target_pairs={{0,1},{2,3},{4,5},{6,7},{8,9},{10,11},{12,13},{14,15},{1,0},{3,2},... | collective-permute-start | bytes 24584 | tf_op jit(solution)/shard_map/ppermute | solution.py:371
  6.5 1.0 %collective-permute-start.1 = (f32[16,128]{1,0:T(8,128)S(1)}, f32[16,128]{1,0:T(8,128)S(1)}, u32[]{:S(2)}, u32[]{:S(2)}) collective-permute-start(f32[16,128]{1,0:T(8,128)S(1)} %get-tuple-element.13.sent_second), channel_id=1, source_target_pairs={{1,2},{3,4},{5,6},{7,8},{9,10},{11,12},{13,14},{2,1},{4,3},{6,5},{... | collective-permute-start | bytes 24584 | tf_op jit(solution)/shard_map/ppermute | solution.py:371
  7.9 9.3 %collective-permute-start.2 = (f32[18,16,128]{2,1,0:T(8,128)S(1)}, f32[18,16,128]{2,1,0:T(8,128)S(1)}, u32[]{:S(2)}, u32[]{:S(2)}) collective-permute-start(f32[18,16,128]{2,1,0:T(8,128)S(1)} %get-tuple-element.16), channel_id=1, source_target_pairs={{16,32},{48,64},{80,96},{112,128},{144,160},{176,192},{208,224},{2... | collective-permute-start | bytes 442376 | tf_op jit(solution)/shard_map/ppermute | solution.py:371

commit v7 on v6

--- a/solution.py
+++ b/solution.py
@@ -110,7 +110,7 @@
         out[:, f * 128 : (f + 1) * 128] = exact_dot(packed, matrix)
 
 
-def widen(field, sent_first, sent_second, from_first, from_second, wide, near, far, halo):
+def widen(field, sent_first, sent_second, from_second, from_first, wide, near, far, halo):
     even = lax.axis_index("gy") % 2 == 0
     upper = lax.axis_index("gx") % 2 == 0
     depth = field.shape[1]
@@ -295,7 +295,7 @@
         norm = new
 
 
-def finish(received, basis, pots, adjoint, gradient, field, lanes):
+def finish(received, basis, pots, adjoint, gradient, field):
     depth = basis.shape[2]
     row = jnp.sum(received[...], axis=0, keepdims=True)
     row = jnp.broadcast_to(row, (8, 128))
@@ -314,29 +314,21 @@
             value = c[0] * basis[0, k, z] + c[1] * basis[1, k, z] + c[2] * basis[2, k, z]
             field[k, z] = value
             adjoint[k, z] = value[0:8, 0:128]
-    forward, _ = difference_matrices()
-    i = lax.broadcasted_iota(jnp.int32, (256, 256), 0)
-    j = lax.broadcasted_iota(jnp.int32, (256, 256), 1)
-    both = jnp.where((i == j) | ((i + 1) % 256 == j), 1.0, 0.0).astype(jnp.bfloat16)
-    gy = None
-    for k in range(2):
-        a, p = (x[k, :, 0:8].reshape(depth * 8, 256) for x in (field, pots))
-        term = exact_dot(a, forward) * exact_dot(p, forward)
-        gy = term if gy is None else gy + term
-    lanes[...] = exact_dot(gy, both[:, 0:128])
     carry = None
     for z in range(depth):
-        gx = gz = None
+        gx = gy = gz = None
         for k in range(2):
-            a, p = field[k, z, :, 0:128], pots[k, z, :, 0:128]
+            a, p = field[k, z], pots[k, z]
             tx = (a - roll(a, -1, 0)) * (p - roll(p, -1, 0))
+            ty = (a - roll(a, -1, 1)) * (p - roll(p, -1, 1))
             gx = tx if gx is None else gx + tx
+            gy = ty if gy is None else gy + ty
             if z + 1 < depth:
-                tz = (a[0:8] - field[k, z + 1, 0:8, 0:128]) * (
-                    p[0:8] - pots[k, z + 1, 0:8, 0:128]
+                tz = (a[0:8, 0:128] - field[k, z + 1, 0:8, 0:128]) * (
+                    p[0:8, 0:128] - pots[k, z + 1, 0:8, 0:128]
                 )
                 gz = tz if gz is None else gz + tz
-        total = (gx + roll(gx, 1, 0))[0:8] + lanes[8 * z : 8 * z + 8]
+        total = (gx + roll(gx, 1, 0) + gy + roll(gy, 1, 1))[0:8, 0:128]
         if carry is not None:
             total = total + carry
         if gz is not None:
@@ -382,12 +374,13 @@
         pltpu.HBM,
         56 * 2**20,
     )(*args)
-    from_first, from_second = trade(first, "gy", 0), trade(second, "gy", 1)
+    from_second = trade(second, "gy", 1)
+    from_first = trade(first, "gy", 0)
     wide, near, far = local(
         widen,
         [(6, depth, 8, 256)] + [(depth + 2, 16, 128)] * 2,
         [scratch(depth * 8, 768)],
-    )(field, first, second, from_first, from_second)
+    )(field, first, second, from_second, from_first)
     far = trade(far, "gx", 1)
     near = lax.all_gather(near, "gx", axis_index_groups=[[i, i + 1] for i in range(0, rows, 2)])
     sent, basis, pots = local(
@@ -401,7 +394,7 @@
     adjoint, gradient = local(
         finish,
         [cotangent.shape, conductance.shape],
-        [scratch(2, depth, 16, 256), scratch(depth * 8, 128)],
+        [scratch(2, depth, 16, 256)],
         kind=jax.ShapeDtypeStruct,
     )(received, basis, pots)
     return adjoint, gradient

time: 64.3 us -> 64.1 us (level)
  no operation moved by 1% of the time
where the time goes in v7:
time: 64.1 us; the launch traced here: 63.8 us
  blocking collectives  47.3 us (74%)
  starting transfers between devices  9.77 us (15%)
  Pallas kernels  5.66 us (9%)
  between operations  0.67 us (1%)
    all_to_all x1, blocking collectives, per_device(): received = lax.all_to_all(sent, 'gy', 0, 0, tiled=True)  29.7 us
    all_to_all x1, blocking collectives, per_device(): received = lax.all_to_all(sent, 'gx', 0, 0, tiled=True)  13 us
    ppermute x3, starting transfers between devices, trade(): return lax.ppermute(x, axis, pairs + [(j, i) for i, j in pairs])  9.77 us
    pallas_call x5, Pallas kernels, call(): pl.pallas_call(body, out_shape=shapes, in_specs=[pl.BlockSpec(memory_spac...  5.66 us
    all_gather x1, blocking collectives, per_device(): lax.all_gather(near, 'gx', axis_index_groups=[[i, i + 1] for i in range(0...  4.6 us
  transfers between devices with their start and end apart: 3, of which 1 were waited for; matrix products, arithmetic and copies ran while one was open for 0% of the time, Pallas kernels for 0%

profile of v7, /device:TPU:1, one launch (start us, length us, event | category | flops | bytes accessed | tf_op | source)
XLA Modules:
  0.0 63.8 jit_solution(3122963954772326277)
XLA Ops:
  0.6 1.5 %shard_map.59 = (f32[16,128]{1,0:T(8,128)S(1)}, f32[16,128]{1,0:T(8,128)S(1)}, f32[6,16,8,128]{3,2,1,0:T(8,128)S(1)}) custom-call(f32[16,8,128]{2,1,0:T(8,128)} %cond_in.1, s32[16,8,128]{2,1,0:T(8,128)} %labels_in.1, f32[2,16,8,128]{3,2,1,0:T(8,128)} %cot_in.1, f32[2,16,8,128]{3,2,1,0:T(8,128)} %saved_in.1), custom_call_target="tpu_custom_call" | custom-call | tf_op jit(solution)/shard_map/pallas_call | solution.py:345
  2.1 4.4 %collective-permute-start.1 = (f32[16,128]{1,0:T(8,128)S(1)}, f32[16,128]{1,0:T(8,128)S(1)}, u32[]{:S(2)}, u32[]{:S(2)}) collective-permute-start(f32[16,128]{1,0:T(8,128)S(1)} %get-tuple-element.12.sent_first), channel_id=1, source_target_pairs={{0,1},{2,3},{4,5},{6,7},{8,9},{10,11},{12,13},{14,15},{1,0},{3,2},... | collective-permute-start | bytes 24584 | tf_op jit(solution)/shard_map/ppermute | solution.py:363
  6.5 0.7 %collective-permute-start = (f32[16,128]{1,0:T(8,128)S(1)}, f32[16,128]{1,0:T(8,128)S(1)}, u32[]{:S(2)}, u32[]{:S(2)}) collective-permute-start(f32[16,128]{1,0:T(8,128)S(1)} %get-tuple-element.13.sent_second), channel_id=1, source_target_pairs={{1,2},{3,4},{5,6},{7,8},{9,10},{11,12},{13,14},{2,1},{4,3},{6,5},{... | collective-permute-start | bytes 24584 | tf_op jit(solution)/shard_map/ppermute | solution.py:363
  7.1 0.4 collective-permute-done.1.from_first
  7.5 0.0 collective-permute-done.from_second
  7.5 0.4 shard_map.60
  7.9 4.7 %collective-permute-start.2 = (f32[18,16,128]{2,1,0:T(8,128)S(1)}, f32[18,16,128]{2,1,0:T(8,128)S(1)}, u32[]{:S(2)}, u32[]{:S(2)}) collective-permute-start(f32[18,16,128]{2,1,0:T(8,128)S(1)} %get-tuple-element.16), channel_id=1, source_target_pairs={{16,32},{48,64},{80,96},{112,128},{144,160},{176,192},{208,224},{2... | collective-permute-start | bytes 442376 | tf_op jit(solution)/shard_map/ppermute | solution.py:363
  12.7 4.6 %all-gather = f32[36,16,128]{2,1,0:T(8,128)S(1)} all-gather(f32[18,16,128]{2,1,0:T(8,128)S(1)} %get-tuple-element.15), channel_id=2, replica_groups={{0,16},{32,48},{64,80},{96,112},{128,144},{160,176},{192,208},{224,240}..., dimensions={0}, use_global_device_ids=true | all-gather | bytes 442368 | tf_op jit(solution)/shard_map/all_gather | solution.py:385
  17.3 0.0 collective-permute-done.2.from_far
  17.3 2.6 %shard_map.61 = (f32[32,128]{1,0:T(8,128)S(1)}, f32[3,2,16,16,256]{4,3,2,1,0:T(8,128)S(1)}, f32[2,16,16,256]{3,2,1,0:T(8,128)S(1)}) custom-call(f32[6,16,8,256]{3,2,1,0:T(8,128)S(1)} %get-tuple-element.14.wide, f32[2,18,16,128]{3,2,1,0:T(8,128)S(1)} %bitcast.9, f32[18,16,128]{2,1,0:T(8,128)S(1)} %collective-permute-done.2.from_far), custom_call_target="tpu_custom_call" | custom-call | tf_op jit(solution)/shard_map/pallas_call | solution.py:345
  19.9 13.0 %all_to_all.22 = f32[32,1,128]{2,1,0:T(1,128)S(1)} all-to-all(f32[32,1,128]{2,1,0:T(1,128)S(1)} %bitcast.13), channel_id=1, replica_groups=mesh['gx'=32,'gy'=16] {'gx'}, dimensions={0} | all-to-all | bytes 32768 | tf_op jit(solution)/shard_map/all_to_all | solution.py:391
  32.9 29.7 %all_to_all.23 = f32[16,1,128]{2,1,0:T(1,128)S(1)} all-to-all(f32[16,1,128]{2,1,0:T(1,128)S(1)} %bitcast.12), channel_id=1, replica_groups=mesh['gx'=32,'gy'=16] {'gy'}, dimensions={0} | all-to-all | bytes 16384 | tf_op jit(solution)/shard_map/all_to_all | solution.py:393
  62.7 1.1 %shard_map.63 = (f32[2,16,8,128]{3,2,1,0:T(8,128)}, f32[16,8,128]{2,1,0:T(8,128)}) custom-call(f32[16,128]{1,0:T(8,128)S(1)} %bitcast.11, f32[3,2,16,16,256]{4,3,2,1,0:T(8,128)S(1)} %get-tuple-element.18.basis, f32[2,16,16,256]{3,2,1,0:T(8,128)S(1)} %get-tuple-element.19.pots), custom_call_target="tpu_custom_call" | custom-call | tf_op jit(solution)/shard_map/pallas_call | solution.py:345
  (1 shorter events, 0.0 us)
Async XLA Ops:
  2.1 5.4 %collective-permute-start.1 = (f32[16,128]{1,0:T(8,128)S(1)}, f32[16,128]{1,0:T(8,128)S(1)}, u32[]{:S(2)}, u32[]{:S(2)}) collective-permute-start(f32[16,128]{1,0:T(8,128)S(1)} %get-tuple-element.12.sent_first), channel_id=1, source_target_pairs={{0,1},{2,3},{4,5},{6,7},{8,9},{10,11},{12,13},{14,15},{1,0},{3,2},... | collective-permute-start | bytes 24584 | tf_op jit(solution)/shard_map/ppermute | solution.py:363
  6.5 1.0 %collective-permute-start = (f32[16,128]{1,0:T(8,128)S(1)}, f32[16,128]{1,0:T(8,128)S(1)}, u32[]{:S(2)}, u32[]{:S(2)}) collective-permute-start(f32[16,128]{1,0:T(8,128)S(1)} %get-tuple-element.13.sent_second), channel_id=1, source_target_pairs={{1,2},{3,4},{5,6},{7,8},{9,10},{11,12},{13,14},{2,1},{4,3},{6,5},{... | collective-permute-start | bytes 24584 | tf_op jit(solution)/shard_map/ppermute | solution.py:363
  7.9 9.3 %collective-permute-start.2 = (f32[18,16,128]{2,1,0:T(8,128)S(1)}, f32[18,16,128]{2,1,0:T(8,128)S(1)}, u32[]{:S(2)}, u32[]{:S(2)}) collective-permute-start(f32[18,16,128]{2,1,0:T(8,128)S(1)} %get-tuple-element.16), channel_id=1, source_target_pairs={{16,32},{48,64},{80,96},{112,128},{144,160},{176,192},{208,224},{2... | collective-permute-start | bytes 442376 | tf_op jit(solution)/shard_map/ppermute | solution.py:363

commit v8 on v7

--- a/solution.py
+++ b/solution.py
@@ -100,8 +100,8 @@
     second[...] = jnp.where(even, left, right)
 
 
-def unpack_columns(left, right, out):
-    packed = jnp.concatenate([left, right], axis=0).T
+def unpack_columns(columns, out):
+    packed = columns.T
     for f in range(6):
         w = WIDTH[f]
         matrix = place(
@@ -110,10 +110,24 @@
         out[:, f * 128 : (f + 1) * 128] = exact_dot(packed, matrix)
 
 
-def widen(field, sent_first, sent_second, from_second, from_first, wide, near, far, halo):
+def pack_rows(field, first_in, first, near, far):
+    first[...] = first_in[...]
+    upper = lax.axis_index("gx") % 2 == 0
+    for z in range(field.shape[1]):
+        own = []
+        for side in range(2):
+            rows = []
+            for f in (COND, RES1, MASK, RES2, POT1, POT2):
+                w = WIDTH[f]
+                start = 0 if side == 0 else 8 - w
+                rows.append(field[f, z, start : start + w])
+            own.append(jnp.concatenate(rows + [jnp.zeros((3, 128), jnp.float32)], axis=0))
+        near[z] = jnp.where(upper, own[1], own[0])
+        far[z] = jnp.where(upper, own[0], own[1])
+
+
+def close_columns(sent_first, sent_second, from_first, from_second, after, columns):
     even = lax.axis_index("gy") % 2 == 0
-    upper = lax.axis_index("gx") % 2 == 0
-    depth = field.shape[1]
     slot = lax.broadcasted_iota(jnp.int32, (GROUP, 128), 0)
     c = LANE[COND]
 
@@ -129,48 +143,37 @@
     outside = left[c + 2 : c + 3] == 0.0
     left = jnp.where(outside & (slot == c + 2), -roll(own_left, 2, 0), left)
     left = jnp.where(outside & pot, own_left, left)
-    near[depth] = left
-    near[depth + 1] = right
-    far[depth] = left
-    far[depth + 1] = right
-    unpack_columns(left, right, halo)
-    for z in range(depth):
-        fields = [field[f, z] for f in range(6)]
-        for f in range(6):
-            wide[f, z, :, 0:128] = fields[f]
-            wide[f, z, :, 128:256] = halo[8 * z : 8 * z + 8, f * 128 : (f + 1) * 128]
-        own = []
-        for side in range(2):
-            rows = []
-            for f in (COND, RES1, MASK, RES2, POT1, POT2):
-                w = WIDTH[f]
-                start = 0 if side == 0 else 8 - w
-                rows.append(fields[f][start : start + w])
-            own.append(jnp.concatenate(rows + [jnp.zeros((3, 128), jnp.float32)], axis=0))
-        near[z] = jnp.where(upper, own[1], own[0])
-        far[z] = jnp.where(upper, own[0], own[1])
-
-
-def moments(wide, from_near, from_far, sent, basis, pots, field, weight, flux, corner):
-    depth = wide.shape[1]
+    columns[0:GROUP] = left
+    columns[GROUP : 2 * GROUP] = right
+
+
+def widen(columns, halo):
+    unpack_columns(columns[...], halo)
+
+
+def moments(field_in, halo, near_rows, far_rows, near_columns, far_columns, sent, basis, pots, field, weight, flux, corner):
+    depth = field_in.shape[1]
     core = lax.axis_index("gx") % 2
     lane16 = lanes_of((16, 128))
     row8 = lax.broadcasted_iota(jnp.int32, (8, 256), 0)
 
-    def above(i):
-        return jnp.where(core == 0, from_far[i], from_near[1 - core, i])
-
-    def below(i):
-        return jnp.where(core == 0, from_near[1 - core, i], from_far[i])
-
-    for side, source in enumerate((above, below)):
-        unpack_columns(source(depth), source(depth + 1), corner.at[side])
+    def above(near, far):
+        return jnp.where(core == 0, far, near)
+
+    def below(near, far):
+        return jnp.where(core == 0, near, far)
+
+    for side, choose in enumerate((above, below)):
+        unpack_columns(choose(near_columns[1 - core], far_columns[...]), corner.at[side])
     for z in range(depth):
-        top, bottom = above(z), below(z)
+        pair = near_rows[1 - core, z], far_rows[z]
+        top, bottom = above(*pair), below(*pair)
         parts = []
         for f in range(6):
             w, s = WIDTH[f], SLOT[f]
-            own = wide[f, z]
+            own = jnp.concatenate(
+                [field_in[f, z], halo[8 * z : 8 * z + 8, f * 128 : (f + 1) * 128]], axis=1
+            )
             gap = jnp.zeros((8 - 2 * w, 128), jnp.float32)
             low = jnp.concatenate([bottom[s : s + w], gap, top[s : s + w]], axis=0)
             tips = [
@@ -375,19 +378,27 @@
         56 * 2**20,
     )(*args)
     from_second = trade(second, "gy", 1)
+    first, near, far = local(pack_rows, [(GROUP, depth * 8)] + [(depth, 16, 128)] * 2)(field, first)
     from_first = trade(first, "gy", 0)
-    wide, near, far = local(
-        widen,
-        [(6, depth, 8, 256)] + [(depth + 2, 16, 128)] * 2,
-        [scratch(depth * 8, 768)],
-    )(field, first, second, from_second, from_first)
-    far = trade(far, "gx", 1)
-    near = lax.all_gather(near, "gx", axis_index_groups=[[i, i + 1] for i in range(0, rows, 2)])
+    chips = [[i, i + 1] for i in range(0, rows, 2)]
+    far_rows = trade(far, "gx", 1)
+    near_rows = lax.all_gather(near, "gx", axis_index_groups=chips)
+    (columns,) = local(close_columns, [(2 * GROUP, depth * 8)])(
+        first, second, from_first, from_second, near_rows
+    )
+    far_columns = trade(columns, "gx", 1)
+    near_columns = lax.all_gather(columns, "gx", axis_index_groups=chips)
+    (halo,) = local(widen, [(depth * 8, 768)])(columns)
     sent, basis, pots = local(
         moments,
         [(rows, 128), (3, 2, depth, 16, 256), (2, depth, 16, 256)],
-        [scratch(1, depth, 16, 256), scratch(4, depth, 16, 256), scratch(2, depth, 16, 256), scratch(2, depth * 8, 768)],
-    )(wide, near, far)
+        [
+            scratch(1, depth, 16, 256),
+            scratch(4, depth, 16, 256),
+            scratch(2, depth, 16, 256),
+            scratch(2, depth * 8, 768),
+        ],
+    )(field, halo, near_rows, far_rows, near_columns, far_columns)
     received = lax.all_to_all(sent, "gx", 0, 0, tiled=True)
     (sent,) = local(relay, [(cols, 128)])(received)
     received = lax.all_to_all(sent, "gy", 0, 0, tiled=True)

time: 64.1 us -> 64.8 us (1.011)
  starting transfers between devices: 9.77 us -> 14.9 us
  blocking collectives: 47.3 us -> 43.2 us
    all_to_all x1, blocking collectives: 29.7 us -> 24.4 us  [per_device(): received = lax.all_to_all(sent, 'gy', 0, 0, tiled=True)]
    ppermute x3 -> x4, starting transfers between devices: 9.77 us -> 14.9 us  [trade(): return lax.ppermute(x, axis, pairs + [(j, i) for i, j in pairs])]
    all_to_all x1, blocking collectives: 13 us -> 15 us  [per_device(): received = lax.all_to_all(sent, 'gx', 0, 0, tiled=True)]
    all_gather x1 -> x2, blocking collectives: 4.6 us -> 3.83 us  [the longest x1 1.99 us: per_device(): near_rows = lax.all_gather(near, 'gx', axis_index_groups=chips)]
    pallas_call x5 -> x7, Pallas kernels: 5.66 us -> 5.66 us  [call(): pl.pallas_call(body, out_shape=shapes, in_specs=[pl.BlockSpec(memory_spac...]
  transfers between devices with their start and end apart: 3 -> 4, of which waited for: 1 -> 0; matrix products, arithmetic and copies ran while one was open for 0% -> 0% of each run, Pallas kernels for 0% -> 1%
where the time goes in v8:
time: 64.8 us; the launch traced here: 64.5 us
  blocking collectives  43.2 us (67%)
  starting transfers between devices  14.9 us (23%)
  Pallas kernels  5.66 us (9%)
  between operations  0.7 us (1%)
    all_to_all x1, blocking collectives, per_device(): received = lax.all_to_all(sent, 'gy', 0, 0, tiled=True)  24.4 us
    all_to_all x1, blocking collectives, per_device(): received = lax.all_to_all(sent, 'gx', 0, 0, tiled=True)  15 us
    ppermute x4, starting transfers between devices, trade(): return lax.ppermute(x, axis, pairs + [(j, i) for i, j in pairs])  14.9 us
    pallas_call x7, Pallas kernels, call(): pl.pallas_call(body, out_shape=shapes, in_specs=[pl.BlockSpec(memory_spac...  5.66 us
    all_gather x1, blocking collectives, per_device(): near_rows = lax.all_gather(near, 'gx', axis_index_groups=chips)  1.99 us
    all_gather x1, blocking collectives, per_device(): near_columns = lax.all_gather(columns, 'gx', axis_index_groups=chips)  1.83 us
  transfers between devices with their start and end apart: 4, of which 0 were waited for; matrix products, arithmetic and copies ran while one was open for 0% of the time, Pallas kernels for 1%

profile of v8, /device:TPU:1, one launch (start us, length us, event | category | flops | bytes accessed | tf_op | source)
XLA Modules:
  0.0 64.5 jit_solution(12401125586953025689)
XLA Ops:
  0.6 1.5 %shard_map.59 = (f32[16,128]{1,0:T(8,128)S(1)}, f32[16,128]{1,0:T(8,128)S(1)}, f32[6,16,8,128]{3,2,1,0:T(8,128)S(1)}) custom-call(f32[16,8,128]{2,1,0:T(8,128)} %cond_in.1, s32[16,8,128]{2,1,0:T(8,128)} %labels_in.1, f32[2,16,8,128]{3,2,1,0:T(8,128)} %cot_in.1, f32[2,16,8,128]{3,2,1,0:T(8,128)} %saved_in.1), custom_call_target="tpu_custom_call" | custom-call | tf_op jit(solution)/shard_map/pallas_call | solution.py:348
  2.1 0.1 shard_map.60
  2.2 4.6 %collective-permute-start.2 = (f32[16,16,128]{2,1,0:T(8,128)S(1)}, f32[16,16,128]{2,1,0:T(8,128)S(1)}, u32[]{:S(2)}, u32[]{:S(2)}) collective-permute-start(f32[16,16,128]{2,1,0:T(8,128)S(1)} %get-tuple-element.16), channel_id=1, source_target_pairs={{16,32},{48,64},{80,96},{112,128},{144,160},{176,192},{208,224},{2... | collective-permute-start | bytes 393224 | tf_op jit(solution)/shard_map/ppermute | solution.py:366
  6.8 0.7 %collective-permute-start.1 = (f32[16,128]{1,0:T(8,128)S(1)}, f32[16,128]{1,0:T(8,128)S(1)}, u32[]{:S(2)}, u32[]{:S(2)}) collective-permute-start(f32[16,128]{1,0:T(8,128)S(1)} %get-tuple-element.14.sent_second), channel_id=1, source_target_pairs={{1,2},{3,4},{5,6},{7,8},{9,10},{11,12},{13,14},{2,1},{4,3},{6,5},{... | collective-permute-start | bytes 24584 | tf_op jit(solution)/shard_map/ppermute | solution.py:366
  7.4 6.4 %collective-permute-start = (f32[16,128]{1,0:T(8,128)S(1)}, f32[16,128]{1,0:T(8,128)S(1)}, u32[]{:S(2)}, u32[]{:S(2)}) collective-permute-start(f32[16,128]{1,0:T(8,128)S(1)} %get-tuple-element.13.sent_first), channel_id=1, source_target_pairs={{0,1},{2,3},{4,5},{6,7},{8,9},{10,11},{12,13},{14,15},{1,0},{3,2},... | collective-permute-start | bytes 24584 | tf_op jit(solution)/shard_map/ppermute | solution.py:366
  13.9 2.0 %all-gather = f32[32,16,128]{2,1,0:T(8,128)S(1)} all-gather(f32[16,16,128]{2,1,0:T(8,128)S(1)} %get-tuple-element.15), channel_id=2, replica_groups={{0,16},{32,48},{64,80},{96,112},{128,144},{160,176},{192,208},{224,240}..., dimensions={0}, use_global_device_ids=true | all-gather | bytes 393216 | tf_op jit(solution)/shard_map/all_gather | solution.py:385
  15.9 0.0 collective-permute-done.1.from_second
  15.9 0.0 collective-permute-done.from_first
  15.9 3.2 %collective-permute-start.3 = (f32[32,128]{1,0:T(8,128)S(1)}, f32[32,128]{1,0:T(8,128)S(1)}, u32[]{:S(2)}, u32[]{:S(2)}) collective-permute-start(f32[32,128]{1,0:T(8,128)S(1)} %shard_map.61.columns), channel_id=1, source_target_pairs={{16,32},{48,64},{80,96},{112,128},{144,160},{176,192},{208,224},{2... | collective-permute-start | bytes 49160 | tf_op jit(solution)/shard_map/ppermute | solution.py:366
  19.1 0.4 shard_map.62.halo
  19.5 1.8 %all-gather.1 = f32[64,128]{1,0:T(8,128)S(1)} all-gather(f32[32,128]{1,0:T(8,128)S(1)} %shard_map.61.columns), channel_id=3, replica_groups={{0,16},{32,48},{64,80},{96,112},{128,144},{160,176},{192,208},{224,240}..., dimensions={0}, use_global_device_ids=true | all-gather | bytes 49152 | tf_op jit(solution)/shard_map/all_gather | solution.py:390
  21.3 0.0 collective-permute-done.3.far_columns
  21.3 0.0 collective-permute-done.2.far_rows
  21.3 2.6 %shard_map.63 = (f32[32,128]{1,0:T(8,128)S(1)}, f32[3,2,16,16,256]{4,3,2,1,0:T(8,128)S(1)}, f32[2,16,16,256]{3,2,1,0:T(8,128)S(1)}) custom-call(f32[6,16,8,128]{3,2,1,0:T(8,128)S(1)} %get-tuple-element.11.field.field_in, f32[128,768]{1,0:T(8,128)S(1)} %shard_map.62.halo, f32[2,16,16,128]{3,2,1,0:T(8,128)S(1)} %bitcast.11, ...), custom_call_target="tpu_custom_call" | custom-call | tf_op jit(solution)/shard_map/pallas_call | solution.py:348
  24.0 15.0 %all_to_all.22 = f32[32,1,128]{2,1,0:T(1,128)S(1)} all-to-all(f32[32,1,128]{2,1,0:T(1,128)S(1)} %bitcast.16), channel_id=1, replica_groups=mesh['gx'=32,'gy'=16] {'gx'}, dimensions={0} | all-to-all | bytes 32768 | tf_op jit(solution)/shard_map/all_to_all | solution.py:402
  39.0 24.4 %all_to_all.23 = f32[16,1,128]{2,1,0:T(1,128)S(1)} all-to-all(f32[16,1,128]{2,1,0:T(1,128)S(1)} %bitcast.15), channel_id=1, replica_groups=mesh['gx'=32,'gy'=16] {'gy'}, dimensions={0} | all-to-all | bytes 16384 | tf_op jit(solution)/shard_map/all_to_all | solution.py:404
  63.4 1.1 %shard_map.65 = (f32[2,16,8,128]{3,2,1,0:T(8,128)}, f32[16,8,128]{2,1,0:T(8,128)}) custom-call(f32[16,128]{1,0:T(8,128)S(1)} %bitcast.14, f32[3,2,16,16,256]{4,3,2,1,0:T(8,128)S(1)} %get-tuple-element.18.basis, f32[2,16,16,256]{3,2,1,0:T(8,128)S(1)} %get-tuple-element.19.pots), custom_call_target="tpu_custom_call" | custom-call | tf_op jit(solution)/shard_map/pallas_call | solution.py:348
  (2 shorter events, 0.0 us)
Async XLA Ops:
  2.2 19.2 %collective-permute-start.2 = (f32[16,16,128]{2,1,0:T(8,128)S(1)}, f32[16,16,128]{2,1,0:T(8,128)S(1)}, u32[]{:S(2)}, u32[]{:S(2)}) collective-permute-start(f32[16,16,128]{2,1,0:T(8,128)S(1)} %get-tuple-element.16), channel_id=1, source_target_pairs={{16,32},{48,64},{80,96},{112,128},{144,160},{176,192},{208,224},{2... | collective-permute-start | bytes 393224 | tf_op jit(solution)/shard_map/ppermute | solution.py:366
  6.8 9.1 %collective-permute-start.1 = (f32[16,128]{1,0:T(8,128)S(1)}, f32[16,128]{1,0:T(8,128)S(1)}, u32[]{:S(2)}, u32[]{:S(2)}) collective-permute-start(f32[16,128]{1,0:T(8,128)S(1)} %get-tuple-element.14.sent_second), channel_id=1, source_target_pairs={{1,2},{3,4},{5,6},{7,8},{9,10},{11,12},{13,14},{2,1},{4,3},{6,5},{... | collective-permute-start | bytes 24584 | tf_op jit(solution)/shard_map/ppermute | solution.py:366
  7.4 8.4 %collective-permute-start = (f32[16,128]{1,0:T(8,128)S(1)}, f32[16,128]{1,0:T(8,128)S(1)}, u32[]{:S(2)}, u32[]{:S(2)}) collective-permute-start(f32[16,128]{1,0:T(8,128)S(1)} %get-tuple-element.13.sent_first), channel_id=1, source_target_pairs={{0,1},{2,3},{4,5},{6,7},{8,9},{10,11},{12,13},{14,15},{1,0},{3,2},... | collective-permute-start | bytes 24584 | tf_op jit(solution)/shard_map/ppermute | solution.py:366
  15.9 5.4 %collective-permute-start.3 = (f32[32,128]{1,0:T(8,128)S(1)}, f32[32,128]{1,0:T(8,128)S(1)}, u32[]{:S(2)}, u32[]{:S(2)}) collective-permute-start(f32[32,128]{1,0:T(8,128)S(1)} %shard_map.61.columns), channel_id=1, source_target_pairs={{16,32},{48,64},{80,96},{112,128},{144,160},{176,192},{208,224},{2... | collective-permute-start | bytes 49160 | tf_op jit(solution)/shard_map/ppermute | solution.py:366

commit v9 on v7

--- a/solution.py
+++ b/solution.py
@@ -108,6 +108,10 @@
             (2 * GROUP, 128), 0, 1, [(LANE[f], 128 - w, w), (GROUP + LANE[f], 0, w)]
         )
         out[:, f * 128 : (f + 1) * 128] = exact_dot(packed, matrix)
+
+
+def hold(source, target):
+    target[...] = source[...]
 
 
 def widen(field, sent_first, sent_second, from_second, from_first, wide, near, far, halo):
@@ -375,6 +379,7 @@
         56 * 2**20,
     )(*args)
     from_second = trade(second, "gy", 1)
+    (from_second,) = local(hold, [(GROUP, depth * 8)])(from_second)
     from_first = trade(first, "gy", 0)
     wide, near, far = local(
         widen,

time: 64.1 us -> 62.4 us (0.973)
  blocking collectives: 47.3 us -> 41.2 us
  starting transfers between devices: 9.77 us -> 12.8 us
  waiting for transfers between devices: 0.36 us -> 1.8 us
    all_to_all x1, blocking collectives: 29.7 us -> 24.5 us  [per_device(): received = lax.all_to_all(sent, 'gy', 0, 0, tiled=True)]
    ppermute x3, starting transfers between devices: 9.77 us -> 12.8 us  [trade(): return lax.ppermute(x, axis, pairs + [(j, i) for i, j in pairs])]
    all_gather x1, blocking collectives: 4.6 us -> 2.02 us  [per_device(): lax.all_gather(near, 'gx', axis_index_groups=[[i, i + 1] for i in range(0...]
    all_to_all x1, blocking collectives: 13 us -> 14.6 us  [per_device(): received = lax.all_to_all(sent, 'gx', 0, 0, tiled=True)]
    ppermute x3, waiting for transfers between devices: 0.36 us -> 1.8 us  [trade(): return lax.ppermute(x, axis, pairs + [(j, i) for i, j in pairs])]
    pallas_call x5 -> x6, Pallas kernels: 5.66 us -> 5.68 us  [call(): pl.pallas_call(body, out_shape=shapes, in_specs=[pl.BlockSpec(memory_spac...]
  transfers between devices with their start and end apart: 3 -> 3, of which waited for: 1 -> 2; matrix products, arithmetic and copies ran while one was open for 0% -> 0% of each run, Pallas kernels for 0% -> 0%
where the time goes in v9:
time: 62.4 us; the launch traced here: 62.1 us
  blocking collectives  41.2 us (66%)
  starting transfers between devices  12.8 us (21%)
  Pallas kernels  5.68 us (9%)
  waiting for transfers between devices  1.8 us (3%)
  between operations  0.68 us (1%)
    all_to_all x1, blocking collectives, per_device(): received = lax.all_to_all(sent, 'gy', 0, 0, tiled=True)  24.5 us
    all_to_all x1, blocking collectives, per_device(): received = lax.all_to_all(sent, 'gx', 0, 0, tiled=True)  14.6 us
    ppermute x3, starting transfers between devices, trade(): return lax.ppermute(x, axis, pairs + [(j, i) for i, j in pairs])  12.8 us
    pallas_call x6, Pallas kernels, call(): pl.pallas_call(body, out_shape=shapes, in_specs=[pl.BlockSpec(memory_spac...  5.68 us
    all_gather x1, blocking collectives, per_device(): lax.all_gather(near, 'gx', axis_index_groups=[[i, i + 1] for i in range(0...  2.02 us
    ppermute x3, waiting for transfers between devices, trade(): return lax.ppermute(x, axis, pairs + [(j, i) for i, j in pairs])  1.8 us
  transfers between devices with their start and end apart: 3, of which 2 were waited for; matrix products, arithmetic and copies ran while one was open for 0% of the time, Pallas kernels for 0%

profile of v9, /device:TPU:1, one launch (start us, length us, event | category | flops | bytes accessed | tf_op | source)
XLA Modules:
  0.0 62.1 jit_solution(303741737508422973)
XLA Ops:
  0.6 1.5 %shard_map.59 = (f32[16,128]{1,0:T(8,128)S(1)}, f32[16,128]{1,0:T(8,128)S(1)}, f32[6,16,8,128]{3,2,1,0:T(8,128)S(1)}) custom-call(f32[16,8,128]{2,1,0:T(8,128)} %cond_in.1, s32[16,8,128]{2,1,0:T(8,128)} %labels_in.1, f32[2,16,8,128]{3,2,1,0:T(8,128)} %cot_in.1, f32[2,16,8,128]{3,2,1,0:T(8,128)} %saved_in.1), custom_call_target="tpu_custom_call" | custom-call | tf_op jit(solution)/shard_map/pallas_call | solution.py:349
  2.1 0.7 %collective-permute-start = (f32[16,128]{1,0:T(8,128)S(1)}, f32[16,128]{1,0:T(8,128)S(1)}, u32[]{:S(2)}, u32[]{:S(2)}) collective-permute-start(f32[16,128]{1,0:T(8,128)S(1)} %get-tuple-element.13.sent_second), channel_id=1, source_target_pairs={{1,2},{3,4},{5,6},{7,8},{9,10},{11,12},{13,14},{2,1},{4,3},{6,5},{... | collective-permute-start | bytes 24584 | tf_op jit(solution)/shard_map/ppermute | solution.py:367
  2.8 7.3 %collective-permute-start.1 = (f32[16,128]{1,0:T(8,128)S(1)}, f32[16,128]{1,0:T(8,128)S(1)}, u32[]{:S(2)}, u32[]{:S(2)}) collective-permute-start(f32[16,128]{1,0:T(8,128)S(1)} %get-tuple-element.12.sent_first), channel_id=1, source_target_pairs={{0,1},{2,3},{4,5},{6,7},{8,9},{10,11},{12,13},{14,15},{1,0},{3,2},... | collective-permute-start | bytes 24584 | tf_op jit(solution)/shard_map/ppermute | solution.py:367
  10.0 0.0 collective-permute-done.source
  10.0 1.0 %collective-permute-done.1.from_first = f32[16,128]{1,0:T(8,128)S(1)} collective-permute-done((f32[16,128]{1,0:T(8,128)S(1)}, f32[16,128]{1,0:T(8,128)S(1)}, u32[]{:S(2)}, u32[]{:S(2)}) %collective-permute-start.1) | collective-permute-done | bytes 8224 | tf_op jit(solution)/shard_map/ppermute | solution.py:367
  11.1 0.4 shard_map.61
  11.5 4.9 %collective-permute-start.2 = (f32[18,16,128]{2,1,0:T(8,128)S(1)}, f32[18,16,128]{2,1,0:T(8,128)S(1)}, u32[]{:S(2)}, u32[]{:S(2)}) collective-permute-start(f32[18,16,128]{2,1,0:T(8,128)S(1)} %get-tuple-element.16), channel_id=1, source_target_pairs={{16,32},{48,64},{80,96},{112,128},{144,160},{176,192},{208,224},{2... | collective-permute-start | bytes 442376 | tf_op jit(solution)/shard_map/ppermute | solution.py:367
  16.4 2.0 %all-gather = f32[36,16,128]{2,1,0:T(8,128)S(1)} all-gather(f32[18,16,128]{2,1,0:T(8,128)S(1)} %get-tuple-element.15), channel_id=2, replica_groups={{0,16},{32,48},{64,80},{96,112},{128,144},{160,176},{192,208},{224,240}..., dimensions={0}, use_global_device_ids=true | all-gather | bytes 442368 | tf_op jit(solution)/shard_map/all_gather | solution.py:390
  18.4 0.8 %collective-permute-done.2.from_far = f32[18,16,128]{2,1,0:T(8,128)S(1)} collective-permute-done((f32[18,16,128]{2,1,0:T(8,128)S(1)}, f32[18,16,128]{2,1,0:T(8,128)S(1)}, u32[]{:S(2)}, u32[]{:S(2)}) %collective-permute-start.2) | collective-permute-done | bytes 147488 | tf_op jit(solution)/shard_map/ppermute | solution.py:367
  19.2 2.6 %shard_map.62 = (f32[32,128]{1,0:T(8,128)S(1)}, f32[3,2,16,16,256]{4,3,2,1,0:T(8,128)S(1)}, f32[2,16,16,256]{3,2,1,0:T(8,128)S(1)}) custom-call(f32[6,16,8,256]{3,2,1,0:T(8,128)S(1)} %get-tuple-element.14.wide, f32[2,18,16,128]{3,2,1,0:T(8,128)S(1)} %bitcast.9, f32[18,16,128]{2,1,0:T(8,128)S(1)} %collective-permute-done.2.from_far), custom_call_target="tpu_custom_call" | custom-call | tf_op jit(solution)/shard_map/pallas_call | solution.py:349
  21.9 14.6 %all_to_all.22 = f32[32,1,128]{2,1,0:T(1,128)S(1)} all-to-all(f32[32,1,128]{2,1,0:T(1,128)S(1)} %bitcast.13), channel_id=1, replica_groups=mesh['gx'=32,'gy'=16] {'gx'}, dimensions={0} | all-to-all | bytes 32768 | tf_op jit(solution)/shard_map/all_to_all | solution.py:396
  36.5 24.5 %all_to_all.23 = f32[16,1,128]{2,1,0:T(1,128)S(1)} all-to-all(f32[16,1,128]{2,1,0:T(1,128)S(1)} %bitcast.12), channel_id=1, replica_groups=mesh['gx'=32,'gy'=16] {'gy'}, dimensions={0} | all-to-all | bytes 16384 | tf_op jit(solution)/shard_map/all_to_all | solution.py:398
  61.0 1.1 %shard_map.64 = (f32[2,16,8,128]{3,2,1,0:T(8,128)}, f32[16,8,128]{2,1,0:T(8,128)}) custom-call(f32[16,128]{1,0:T(8,128)S(1)} %bitcast.11, f32[3,2,16,16,256]{4,3,2,1,0:T(8,128)S(1)} %get-tuple-element.18.basis, f32[2,16,16,256]{3,2,1,0:T(8,128)S(1)} %get-tuple-element.19.pots), custom_call_target="tpu_custom_call" | custom-call | tf_op jit(solution)/shard_map/pallas_call | solution.py:349
  (2 shorter events, 0.0 us)
Async XLA Ops:
  2.1 7.9 %collective-permute-start = (f32[16,128]{1,0:T(8,128)S(1)}, f32[16,128]{1,0:T(8,128)S(1)}, u32[]{:S(2)}, u32[]{:S(2)}) collective-permute-start(f32[16,128]{1,0:T(8,128)S(1)} %get-tuple-element.13.sent_second), channel_id=1, source_target_pairs={{1,2},{3,4},{5,6},{7,8},{9,10},{11,12},{13,14},{2,1},{4,3},{6,5},{... | collective-permute-start | bytes 24584 | tf_op jit(solution)/shard_map/ppermute | solution.py:367
  2.8 8.3 %collective-permute-start.1 = (f32[16,128]{1,0:T(8,128)S(1)}, f32[16,128]{1,0:T(8,128)S(1)}, u32[]{:S(2)}, u32[]{:S(2)}) collective-permute-start(f32[16,128]{1,0:T(8,128)S(1)} %get-tuple-element.12.sent_first), channel_id=1, source_target_pairs={{0,1},{2,3},{4,5},{6,7},{8,9},{10,11},{12,13},{14,15},{1,0},{3,2},... | collective-permute-start | bytes 24584 | tf_op jit(solution)/shard_map/ppermute | solution.py:367
  11.5 7.7 %collective-permute-start.2 = (f32[18,16,128]{2,1,0:T(8,128)S(1)}, f32[18,16,128]{2,1,0:T(8,128)S(1)}, u32[]{:S(2)}, u32[]{:S(2)}) collective-permute-start(f32[18,16,128]{2,1,0:T(8,128)S(1)} %get-tuple-element.16), channel_id=1, source_target_pairs={{16,32},{48,64},{80,96},{112,128},{144,160},{176,192},{208,224},{2... | collective-permute-start | bytes 442376 | tf_op jit(solution)/shard_map/ppermute | solution.py:367

commit v10 on v9

--- a/solution.py
+++ b/solution.py
@@ -14,6 +14,7 @@
 LANE = (0, 9, 3, 6, 11, 12)
 SLOT = (0, 6, 3, 8, 11, 12)
 GROUP = 16
+ROWS = sum(WIDTH)
 
 
 def roll(x, amount, axis):
@@ -133,10 +134,12 @@
     outside = left[c + 2 : c + 3] == 0.0
     left = jnp.where(outside & (slot == c + 2), -roll(own_left, 2, 0), left)
     left = jnp.where(outside & pot, own_left, left)
-    near[depth] = left
-    near[depth + 1] = right
-    far[depth] = left
-    far[depth + 1] = right
+    columns = jnp.concatenate([left[0:ROWS], right[0:ROWS]], axis=0)
+    start, end = ROWS * depth, ROWS * (depth + 2)
+    for out in (near, far):
+        out[start:end] = columns
+        if out.shape[0] > end:
+            out[end:] = jnp.zeros((out.shape[0] - end, 128), jnp.float32)
     unpack_columns(left, right, halo)
     for z in range(depth):
         fields = [field[f, z] for f in range(6)]
@@ -150,9 +153,9 @@
                 w = WIDTH[f]
                 start = 0 if side == 0 else 8 - w
                 rows.append(fields[f][start : start + w])
-            own.append(jnp.concatenate(rows + [jnp.zeros((3, 128), jnp.float32)], axis=0))
-        near[z] = jnp.where(upper, own[1], own[0])
-        far[z] = jnp.where(upper, own[0], own[1])
+            own.append(jnp.concatenate(rows, axis=0))
+        near[ROWS * z : ROWS * (z + 1)] = jnp.where(upper, own[1], own[0])
+        far[ROWS * z : ROWS * (z + 1)] = jnp.where(upper, own[0], own[1])
 
 
 def moments(wide, from_near, from_far, sent, basis, pots, field, weight, flux, corner):
@@ -162,13 +165,17 @@
     row8 = lax.broadcasted_iota(jnp.int32, (8, 256), 0)
 
     def above(i):
-        return jnp.where(core == 0, from_far[i], from_near[1 - core, i])
+        rows = slice(ROWS * i, ROWS * (i + 1))
+        return jnp.where(core == 0, from_far[rows], from_near[1 - core, rows])
 
     def below(i):
-        return jnp.where(core == 0, from_near[1 - core, i], from_far[i])
-
+        rows = slice(ROWS * i, ROWS * (i + 1))
+        return jnp.where(core == 0, from_near[1 - core, rows], from_far[rows])
+
+    blank = jnp.zeros((GROUP - ROWS, 128), jnp.float32)
     for side, source in enumerate((above, below)):
-        unpack_columns(source(depth), source(depth + 1), corner.at[side])
+        tips = [jnp.concatenate([source(depth + i), blank], axis=0) for i in range(2)]
+        unpack_columns(*tips, corner.at[side])
     for z in range(depth):
         top, bottom = above(z), below(z)
         parts = []
@@ -383,7 +390,7 @@
     from_first = trade(first, "gy", 0)
     wide, near, far = local(
         widen,
-        [(6, depth, 8, 256)] + [(depth + 2, 16, 128)] * 2,
+        [(6, depth, 8, 256)] + [(-(-ROWS * (depth + 2) // 8) * 8, 128)] * 2,
         [scratch(depth * 8, 768)],
     )(field, first, second, from_second, from_first)
     far = trade(far, "gx", 1)

time: 62.4 us -> 62.2 us (level)
  no operation moved by 1% of the time
where the time goes in v10:
time: 62.2 us; the launch traced here: 62 us
  blocking collectives  41.1 us (66%)
  starting transfers between devices  12.8 us (21%)
  Pallas kernels  5.76 us (9%)
  waiting for transfers between devices  1.57 us (3%)
  between operations  0.68 us (1%)
    all_to_all x1, blocking collectives, per_device(): received = lax.all_to_all(sent, 'gy', 0, 0, tiled=True)  24.5 us
    all_to_all x1, blocking collectives, per_device(): received = lax.all_to_all(sent, 'gx', 0, 0, tiled=True)  14.6 us
    ppermute x3, starting transfers between devices, trade(): return lax.ppermute(x, axis, pairs + [(j, i) for i, j in pairs])  12.8 us
    pallas_call x6, Pallas kernels, call(): pl.pallas_call(body, out_shape=shapes, in_specs=[pl.BlockSpec(memory_spac...  5.76 us
    all_gather x1, blocking collectives, per_device(): lax.all_gather(near, 'gx', axis_index_groups=[[i, i + 1] for i in range(0...  1.98 us
    ppermute x3, waiting for transfers between devices, trade(): return lax.ppermute(x, axis, pairs + [(j, i) for i, j in pairs])  1.57 us
  transfers between devices with their start and end apart: 3, of which 2 were waited for; matrix products, arithmetic and copies ran while one was open for 0% of the time, Pallas kernels for 0%

profile of v10, /device:TPU:1, one launch (start us, length us, event | category | flops | bytes accessed | tf_op | source)
XLA Modules:
  0.0 62.0 jit_solution(16862811310261154551)
XLA Ops:
  0.6 1.5 %shard_map.59 = (f32[16,128]{1,0:T(8,128)S(1)}, f32[16,128]{1,0:T(8,128)S(1)}, f32[6,16,8,128]{3,2,1,0:T(8,128)S(1)}) custom-call(f32[16,8,128]{2,1,0:T(8,128)} %cond_in.1, s32[16,8,128]{2,1,0:T(8,128)} %labels_in.1, f32[2,16,8,128]{3,2,1,0:T(8,128)} %cot_in.1, f32[2,16,8,128]{3,2,1,0:T(8,128)} %saved_in.1), custom_call_target="tpu_custom_call" | custom-call | tf_op jit(solution)/shard_map/pallas_call | solution.py:356
  2.1 0.7 %collective-permute-start = (f32[16,128]{1,0:T(8,128)S(1)}, f32[16,128]{1,0:T(8,128)S(1)}, u32[]{:S(2)}, u32[]{:S(2)}) collective-permute-start(f32[16,128]{1,0:T(8,128)S(1)} %get-tuple-element.13.sent_second), channel_id=1, source_target_pairs={{1,2},{3,4},{5,6},{7,8},{9,10},{11,12},{13,14},{2,1},{4,3},{6,5},{... | collective-permute-start | bytes 24584 | tf_op jit(solution)/shard_map/ppermute | solution.py:374
  2.8 7.3 %collective-permute-start.1 = (f32[16,128]{1,0:T(8,128)S(1)}, f32[16,128]{1,0:T(8,128)S(1)}, u32[]{:S(2)}, u32[]{:S(2)}) collective-permute-start(f32[16,128]{1,0:T(8,128)S(1)} %get-tuple-element.12.sent_first), channel_id=1, source_target_pairs={{0,1},{2,3},{4,5},{6,7},{8,9},{10,11},{12,13},{14,15},{1,0},{3,2},... | collective-permute-start | bytes 24584 | tf_op jit(solution)/shard_map/ppermute | solution.py:374
  10.0 0.0 collective-permute-done.source
  10.0 1.0 %collective-permute-done.1.from_first = f32[16,128]{1,0:T(8,128)S(1)} collective-permute-done((f32[16,128]{1,0:T(8,128)S(1)}, f32[16,128]{1,0:T(8,128)S(1)}, u32[]{:S(2)}, u32[]{:S(2)}) %collective-permute-start.1) | collective-permute-done | bytes 8224 | tf_op jit(solution)/shard_map/ppermute | solution.py:374
  11.1 0.4 shard_map.61
  11.5 4.9 %collective-permute-start.2 = (f32[240,128]{1,0:T(8,128)S(1)}, f32[240,128]{1,0:T(8,128)S(1)}, u32[]{:S(2)}, u32[]{:S(2)}) collective-permute-start(f32[240,128]{1,0:T(8,128)S(1)} %get-tuple-element.16), channel_id=1, source_target_pairs={{16,32},{48,64},{80,96},{112,128},{144,160},{176,192},{208,224},{2... | collective-permute-start | bytes 368648 | tf_op jit(solution)/shard_map/ppermute | solution.py:374
  16.4 2.0 %all-gather = f32[480,128]{1,0:T(8,128)S(1)} all-gather(f32[240,128]{1,0:T(8,128)S(1)} %get-tuple-element.15), channel_id=2, replica_groups={{0,16},{32,48},{64,80},{96,112},{128,144},{160,176},{192,208},{224,240}..., dimensions={0}, use_global_device_ids=true | all-gather | bytes 368640 | tf_op jit(solution)/shard_map/all_gather | solution.py:397
  18.4 0.6 collective-permute-done.2.from_far
  19.0 2.7 %shard_map.62 = (f32[32,128]{1,0:T(8,128)S(1)}, f32[3,2,16,16,256]{4,3,2,1,0:T(8,128)S(1)}, f32[2,16,16,256]{3,2,1,0:T(8,128)S(1)}) custom-call(f32[6,16,8,256]{3,2,1,0:T(8,128)S(1)} %get-tuple-element.14.wide, f32[2,240,128]{2,1,0:T(8,128)S(1)} %bitcast.9, f32[240,128]{1,0:T(8,128)S(1)} %collective-permute-done.2.from_far), custom_call_target="tpu_custom_call" | custom-call | tf_op jit(solution)/shard_map/pallas_call | solution.py:356
  21.7 14.6 %all_to_all.22 = f32[32,1,128]{2,1,0:T(1,128)S(1)} all-to-all(f32[32,1,128]{2,1,0:T(1,128)S(1)} %bitcast.13), channel_id=1, replica_groups=mesh['gx'=32,'gy'=16] {'gx'}, dimensions={0} | all-to-all | bytes 32768 | tf_op jit(solution)/shard_map/all_to_all | solution.py:403
  36.3 24.5 %all_to_all.23 = f32[16,1,128]{2,1,0:T(1,128)S(1)} all-to-all(f32[16,1,128]{2,1,0:T(1,128)S(1)} %bitcast.12), channel_id=1, replica_groups=mesh['gx'=32,'gy'=16] {'gy'}, dimensions={0} | all-to-all | bytes 16384 | tf_op jit(solution)/shard_map/all_to_all | solution.py:405
  60.8 1.1 %shard_map.64 = (f32[2,16,8,128]{3,2,1,0:T(8,128)}, f32[16,8,128]{2,1,0:T(8,128)}) custom-call(f32[16,128]{1,0:T(8,128)S(1)} %bitcast.11, f32[3,2,16,16,256]{4,3,2,1,0:T(8,128)S(1)} %get-tuple-element.18.basis, f32[2,16,16,256]{3,2,1,0:T(8,128)S(1)} %get-tuple-element.19.pots), custom_call_target="tpu_custom_call" | custom-call | tf_op jit(solution)/shard_map/pallas_call | solution.py:356
  (2 shorter events, 0.0 us)
Async XLA Ops:
  2.1 7.9 %collective-permute-start = (f32[16,128]{1,0:T(8,128)S(1)}, f32[16,128]{1,0:T(8,128)S(1)}, u32[]{:S(2)}, u32[]{:S(2)}) collective-permute-start(f32[16,128]{1,0:T(8,128)S(1)} %get-tuple-element.13.sent_second), channel_id=1, source_target_pairs={{1,2},{3,4},{5,6},{7,8},{9,10},{11,12},{13,14},{2,1},{4,3},{6,5},{... | collective-permute-start | bytes 24584 | tf_op jit(solution)/shard_map/ppermute | solution.py:374
  2.8 8.3 %collective-permute-start.1 = (f32[16,128]{1,0:T(8,128)S(1)}, f32[16,128]{1,0:T(8,128)S(1)}, u32[]{:S(2)}, u32[]{:S(2)}) collective-permute-start(f32[16,128]{1,0:T(8,128)S(1)} %get-tuple-element.12.sent_first), channel_id=1, source_target_pairs={{0,1},{2,3},{4,5},{6,7},{8,9},{10,11},{12,13},{14,15},{1,0},{3,2},... | collective-permute-start | bytes 24584 | tf_op jit(solution)/shard_map/ppermute | solution.py:374
  11.5 7.5 %collective-permute-start.2 = (f32[240,128]{1,0:T(8,128)S(1)}, f32[240,128]{1,0:T(8,128)S(1)}, u32[]{:S(2)}, u32[]{:S(2)}) collective-permute-start(f32[240,128]{1,0:T(8,128)S(1)} %get-tuple-element.16), channel_id=1, source_target_pairs={{16,32},{48,64},{80,96},{112,128},{144,160},{176,192},{208,224},{2... | collective-permute-start | bytes 368648 | tf_op jit(solution)/shard_map/ppermute | solution.py:374

commit v11 on v10

--- a/solution.py
+++ b/solution.py
@@ -115,7 +115,7 @@
     target[...] = source[...]
 
 
-def widen(field, sent_first, sent_second, from_second, from_first, wide, near, far, halo):
+def pack_rows(field, sent_first, sent_second, from_second, from_first, near, far, closed):
     even = lax.axis_index("gy") % 2 == 0
     upper = lax.axis_index("gx") % 2 == 0
     depth = field.shape[1]
@@ -140,12 +140,10 @@
         out[start:end] = columns
         if out.shape[0] > end:
             out[end:] = jnp.zeros((out.shape[0] - end, 128), jnp.float32)
-    unpack_columns(left, right, halo)
+    closed[0] = left
+    closed[1] = right
     for z in range(depth):
         fields = [field[f, z] for f in range(6)]
-        for f in range(6):
-            wide[f, z, :, 0:128] = fields[f]
-            wide[f, z, :, 128:256] = halo[8 * z : 8 * z + 8, f * 128 : (f + 1) * 128]
         own = []
         for side in range(2):
             rows = []
@@ -156,6 +154,14 @@
             own.append(jnp.concatenate(rows, axis=0))
         near[ROWS * z : ROWS * (z + 1)] = jnp.where(upper, own[1], own[0])
         far[ROWS * z : ROWS * (z + 1)] = jnp.where(upper, own[0], own[1])
+
+
+def widen(field, closed, wide, halo):
+    unpack_columns(closed[0], closed[1], halo)
+    for z in range(field.shape[1]):
+        for f in range(6):
+            wide[f, z, :, 0:128] = field[f, z]
+            wide[f, z, :, 128:256] = halo[8 * z : 8 * z + 8, f * 128 : (f + 1) * 128]
 
 
 def moments(wide, from_near, from_far, sent, basis, pots, field, weight, flux, corner):
@@ -388,11 +394,11 @@
     from_second = trade(second, "gy", 1)
     (from_second,) = local(hold, [(GROUP, depth * 8)])(from_second)
     from_first = trade(first, "gy", 0)
-    wide, near, far = local(
-        widen,
-        [(6, depth, 8, 256)] + [(-(-ROWS * (depth + 2) // 8) * 8, 128)] * 2,
-        [scratch(depth * 8, 768)],
-    )(field, first, second, from_second, from_first)
+    packed = (-(-ROWS * (depth + 2) // 8) * 8, 128)
+    near, far, closed = local(pack_rows, [packed, packed, (2, GROUP, depth * 8)])(
+        field, first, second, from_second, from_first
+    )
+    (wide,) = local(widen, [(6, depth, 8, 256)], [scratch(depth * 8, 768)])(field, closed)
     far = trade(far, "gx", 1)
     near = lax.all_gather(near, "gx", axis_index_groups=[[i, i + 1] for i in range(0, rows, 2)])
     sent, basis, pots = local(

time: 62.2 us -> 61.9 us (level)
    pallas_call x6 -> x7, Pallas kernels: 5.76 us -> 5.76 us  [call(): pl.pallas_call(body, out_shape=shapes, in_specs=[pl.BlockSpec(memory_spac...]
  transfers between devices with their start and end apart: 3 -> 3, of which waited for: 2 -> 2; matrix products, arithmetic and copies ran while one was open for 0% -> 0% of each run, Pallas kernels for 0% -> 1%
where the time goes in v11:
time: 61.9 us; the launch traced here: 61.6 us
  blocking collectives  41.1 us (66%)
  starting transfers between devices  12.8 us (21%)
  Pallas kernels  5.76 us (9%)
  waiting for transfers between devices  1.2 us (2%)
  between operations  0.69 us (1%)
    all_to_all x1, blocking collectives, per_device(): received = lax.all_to_all(sent, 'gy', 0, 0, tiled=True)  24.5 us
    all_to_all x1, blocking collectives, per_device(): received = lax.all_to_all(sent, 'gx', 0, 0, tiled=True)  14.6 us
    ppermute x3, starting transfers between devices, trade(): return lax.ppermute(x, axis, pairs + [(j, i) for i, j in pairs])  12.8 us
    pallas_call x7, Pallas kernels, call(): pl.pallas_call(body, out_shape=shapes, in_specs=[pl.BlockSpec(memory_spac...  5.76 us
    all_gather x1, blocking collectives, per_device(): lax.all_gather(near, 'gx', axis_index_groups=[[i, i + 1] for i in range(0...  1.98 us
  transfers between devices with their start and end apart: 3, of which 2 were waited for; matrix products, arithmetic and copies ran while one was open for 0% of the time, Pallas kernels for 1%

profile of v11, /device:TPU:1, one launch (start us, length us, event | category | flops | bytes accessed | tf_op | source)
XLA Modules:
  0.0 61.6 jit_solution(12906838611598089224)
XLA Ops:
  0.6 1.5 %shard_map.59 = (f32[16,128]{1,0:T(8,128)S(1)}, f32[16,128]{1,0:T(8,128)S(1)}, f32[6,16,8,128]{3,2,1,0:T(8,128)S(1)}) custom-call(f32[16,8,128]{2,1,0:T(8,128)} %cond_in.1, s32[16,8,128]{2,1,0:T(8,128)} %labels_in.1, f32[2,16,8,128]{3,2,1,0:T(8,128)} %cot_in.1, f32[2,16,8,128]{3,2,1,0:T(8,128)} %saved_in.1), custom_call_target="tpu_custom_call" | custom-call | tf_op jit(solution)/shard_map/pallas_call | solution.py:362
  2.1 0.7 %collective-permute-start = (f32[16,128]{1,0:T(8,128)S(1)}, f32[16,128]{1,0:T(8,128)S(1)}, u32[]{:S(2)}, u32[]{:S(2)}) collective-permute-start(f32[16,128]{1,0:T(8,128)S(1)} %get-tuple-element.13.sent_second), channel_id=1, source_target_pairs={{1,2},{3,4},{5,6},{7,8},{9,10},{11,12},{13,14},{2,1},{4,3},{6,5},{... | collective-permute-start | bytes 24584 | tf_op jit(solution)/shard_map/ppermute | solution.py:380
  2.8 7.3 %collective-permute-start.1 = (f32[16,128]{1,0:T(8,128)S(1)}, f32[16,128]{1,0:T(8,128)S(1)}, u32[]{:S(2)}, u32[]{:S(2)}) collective-permute-start(f32[16,128]{1,0:T(8,128)S(1)} %get-tuple-element.12.sent_first), channel_id=1, source_target_pairs={{0,1},{2,3},{4,5},{6,7},{8,9},{10,11},{12,13},{14,15},{1,0},{3,2},... | collective-permute-start | bytes 24584 | tf_op jit(solution)/shard_map/ppermute | solution.py:380
  10.0 0.0 collective-permute-done.source
  10.0 1.0 %collective-permute-done.1.from_first = f32[16,128]{1,0:T(8,128)S(1)} collective-permute-done((f32[16,128]{1,0:T(8,128)S(1)}, f32[16,128]{1,0:T(8,128)S(1)}, u32[]{:S(2)}, u32[]{:S(2)}) %collective-permute-start.1) | collective-permute-done | bytes 8224 | tf_op jit(solution)/shard_map/ppermute | solution.py:380
  11.1 0.1 shard_map.61
  11.1 4.9 %collective-permute-start.2 = (f32[240,128]{1,0:T(8,128)S(1)}, f32[240,128]{1,0:T(8,128)S(1)}, u32[]{:S(2)}, u32[]{:S(2)}) collective-permute-start(f32[240,128]{1,0:T(8,128)S(1)} %get-tuple-element.16), channel_id=1, source_target_pairs={{16,32},{48,64},{80,96},{112,128},{144,160},{176,192},{208,224},{2... | collective-permute-start | bytes 368648 | tf_op jit(solution)/shard_map/ppermute | solution.py:380
  16.0 0.4 shard_map.62.wide
  16.4 2.0 %all-gather = f32[480,128]{1,0:T(8,128)S(1)} all-gather(f32[240,128]{1,0:T(8,128)S(1)} %get-tuple-element.15), channel_id=2, replica_groups={{0,16},{32,48},{64,80},{96,112},{128,144},{160,176},{192,208},{224,240}..., dimensions={0}, use_global_device_ids=true | all-gather | bytes 368640 | tf_op jit(solution)/shard_map/all_gather | solution.py:403
  18.4 0.2 collective-permute-done.2.from_far
  18.6 2.7 %shard_map.63 = (f32[32,128]{1,0:T(8,128)S(1)}, f32[3,2,16,16,256]{4,3,2,1,0:T(8,128)S(1)}, f32[2,16,16,256]{3,2,1,0:T(8,128)S(1)}) custom-call(f32[6,16,8,256]{3,2,1,0:T(8,128)S(1)} %shard_map.62.wide, f32[2,240,128]{2,1,0:T(8,128)S(1)} %bitcast.9, f32[240,128]{1,0:T(8,128)S(1)} %collective-permute-done.2.from_far), custom_call_target="tpu_custom_call" | custom-call | tf_op jit(solution)/shard_map/pallas_call | solution.py:362
  21.3 14.6 %all_to_all.22 = f32[32,1,128]{2,1,0:T(1,128)S(1)} all-to-all(f32[32,1,128]{2,1,0:T(1,128)S(1)} %bitcast.13), channel_id=1, replica_groups=mesh['gx'=32,'gy'=16] {'gx'}, dimensions={0} | all-to-all | bytes 32768 | tf_op jit(solution)/shard_map/all_to_all | solution.py:409
  35.9 24.5 %all_to_all.23 = f32[16,1,128]{2,1,0:T(1,128)S(1)} all-to-all(f32[16,1,128]{2,1,0:T(1,128)S(1)} %bitcast.12), channel_id=1, replica_groups=mesh['gx'=32,'gy'=16] {'gy'}, dimensions={0} | all-to-all | bytes 16384 | tf_op jit(solution)/shard_map/all_to_all | solution.py:411
  60.5 1.1 %shard_map.65 = (f32[2,16,8,128]{3,2,1,0:T(8,128)}, f32[16,8,128]{2,1,0:T(8,128)}) custom-call(f32[16,128]{1,0:T(8,128)S(1)} %bitcast.11, f32[3,2,16,16,256]{4,3,2,1,0:T(8,128)S(1)} %get-tuple-element.18.basis, f32[2,16,16,256]{3,2,1,0:T(8,128)S(1)} %get-tuple-element.19.pots), custom_call_target="tpu_custom_call" | custom-call | tf_op jit(solution)/shard_map/pallas_call | solution.py:362
  (2 shorter events, 0.0 us)
Async XLA Ops:
  2.1 7.9 %collective-permute-start = (f32[16,128]{1,0:T(8,128)S(1)}, f32[16,128]{1,0:T(8,128)S(1)}, u32[]{:S(2)}, u32[]{:S(2)}) collective-permute-start(f32[16,128]{1,0:T(8,128)S(1)} %get-tuple-element.13.sent_second), channel_id=1, source_target_pairs={{1,2},{3,4},{5,6},{7,8},{9,10},{11,12},{13,14},{2,1},{4,3},{6,5},{... | collective-permute-start | bytes 24584 | tf_op jit(solution)/shard_map/ppermute | solution.py:380
  2.8 8.3 %collective-permute-start.1 = (f32[16,128]{1,0:T(8,128)S(1)}, f32[16,128]{1,0:T(8,128)S(1)}, u32[]{:S(2)}, u32[]{:S(2)}) collective-permute-start(f32[16,128]{1,0:T(8,128)S(1)} %get-tuple-element.12.sent_first), channel_id=1, source_target_pairs={{0,1},{2,3},{4,5},{6,7},{8,9},{10,11},{12,13},{14,15},{1,0},{3,2},... | collective-permute-start | bytes 24584 | tf_op jit(solution)/shard_map/ppermute | solution.py:380
  11.1 7.5 %collective-permute-start.2 = (f32[240,128]{1,0:T(8,128)S(1)}, f32[240,128]{1,0:T(8,128)S(1)}, u32[]{:S(2)}, u32[]{:S(2)}) collective-permute-start(f32[240,128]{1,0:T(8,128)S(1)} %get-tuple-element.16), channel_id=1, source_target_pairs={{16,32},{48,64},{80,96},{112,128},{144,160},{176,192},{208,224},{2... | collective-permute-start | bytes 368648 | tf_op jit(solution)/shard_map/ppermute | solution.py:380

commit v12 on v11

--- a/solution.py
+++ b/solution.py
@@ -336,16 +336,17 @@
         gx = gy = gz = None
         for k in range(2):
             a, p = field[k, z], pots[k, z]
+            ty = (a[0:8] - roll(a[0:8], -1, 1)) * (p[0:8] - roll(p[0:8], -1, 1))
+            a, p = a[:, 0:128], p[:, 0:128]
             tx = (a - roll(a, -1, 0)) * (p - roll(p, -1, 0))
-            ty = (a - roll(a, -1, 1)) * (p - roll(p, -1, 1))
             gx = tx if gx is None else gx + tx
             gy = ty if gy is None else gy + ty
             if z + 1 < depth:
-                tz = (a[0:8, 0:128] - field[k, z + 1, 0:8, 0:128]) * (
-                    p[0:8, 0:128] - pots[k, z + 1, 0:8, 0:128]
+                tz = (a[0:8] - field[k, z + 1, 0:8, 0:128]) * (
+                    p[0:8] - pots[k, z + 1, 0:8, 0:128]
                 )
                 gz = tz if gz is None else gz + tz
-        total = (gx + roll(gx, 1, 0) + gy + roll(gy, 1, 1))[0:8, 0:128]
+        total = (gx + roll(gx, 1, 0))[0:8] + (gy + roll(gy, 1, 1))[:, 0:128]
         if carry is not None:
             total = total + carry
         if gz is not None:

time: 61.9 us -> 61.9 us (level)
  no operation moved by 1% of the time
where the time goes in v12:
time: 61.9 us; the launch traced here: 61.6 us
  blocking collectives  41.1 us (66%)
  starting transfers between devices  12.8 us (21%)
  Pallas kernels  5.76 us (9%)
  waiting for transfers between devices  1.2 us (2%)
  between operations  0.69 us (1%)
    all_to_all x1, blocking collectives, per_device(): received = lax.all_to_all(sent, 'gy', 0, 0, tiled=True)  24.5 us
    all_to_all x1, blocking collectives, per_device(): received = lax.all_to_all(sent, 'gx', 0, 0, tiled=True)  14.6 us
    ppermute x3, starting transfers between devices, trade(): return lax.ppermute(x, axis, pairs + [(j, i) for i, j in pairs])  12.8 us
    pallas_call x7, Pallas kernels, call(): pl.pallas_call(body, out_shape=shapes, in_specs=[pl.BlockSpec(memory_spac...  5.76 us
    all_gather x1, blocking collectives, per_device(): lax.all_gather(near, 'gx', axis_index_groups=[[i, i + 1] for i in range(0...  1.98 us
  transfers between devices with their start and end apart: 3, of which 2 were waited for; matrix products, arithmetic and copies ran while one was open for 0% of the time, Pallas kernels for 1%

profile of v12, /device:TPU:1, one launch (start us, length us, event | category | flops | bytes accessed | tf_op | source)
XLA Modules:
  0.0 61.6 jit_solution(12280317518569345177)
XLA Ops:
  0.6 1.5 %shard_map.59 = (f32[16,128]{1,0:T(8,128)S(1)}, f32[16,128]{1,0:T(8,128)S(1)}, f32[6,16,8,128]{3,2,1,0:T(8,128)S(1)}) custom-call(f32[16,8,128]{2,1,0:T(8,128)} %cond_in.1, s32[16,8,128]{2,1,0:T(8,128)} %labels_in.1, f32[2,16,8,128]{3,2,1,0:T(8,128)} %cot_in.1, f32[2,16,8,128]{3,2,1,0:T(8,128)} %saved_in.1), custom_call_target="tpu_custom_call" | custom-call | tf_op jit(solution)/shard_map/pallas_call | solution.py:363
  2.1 0.7 %collective-permute-start = (f32[16,128]{1,0:T(8,128)S(1)}, f32[16,128]{1,0:T(8,128)S(1)}, u32[]{:S(2)}, u32[]{:S(2)}) collective-permute-start(f32[16,128]{1,0:T(8,128)S(1)} %get-tuple-element.13.sent_second), channel_id=1, source_target_pairs={{1,2},{3,4},{5,6},{7,8},{9,10},{11,12},{13,14},{2,1},{4,3},{6,5},{... | collective-permute-start | bytes 24584 | tf_op jit(solution)/shard_map/ppermute | solution.py:381
  2.8 7.3 %collective-permute-start.1 = (f32[16,128]{1,0:T(8,128)S(1)}, f32[16,128]{1,0:T(8,128)S(1)}, u32[]{:S(2)}, u32[]{:S(2)}) collective-permute-start(f32[16,128]{1,0:T(8,128)S(1)} %get-tuple-element.12.sent_first), channel_id=1, source_target_pairs={{0,1},{2,3},{4,5},{6,7},{8,9},{10,11},{12,13},{14,15},{1,0},{3,2},... | collective-permute-start | bytes 24584 | tf_op jit(solution)/shard_map/ppermute | solution.py:381
  10.0 0.0 collective-permute-done.source
  10.0 1.0 %collective-permute-done.1.from_first = f32[16,128]{1,0:T(8,128)S(1)} collective-permute-done((f32[16,128]{1,0:T(8,128)S(1)}, f32[16,128]{1,0:T(8,128)S(1)}, u32[]{:S(2)}, u32[]{:S(2)}) %collective-permute-start.1) | collective-permute-done | bytes 8224 | tf_op jit(solution)/shard_map/ppermute | solution.py:381
  11.1 0.1 shard_map.61
  11.1 4.9 %collective-permute-start.2 = (f32[240,128]{1,0:T(8,128)S(1)}, f32[240,128]{1,0:T(8,128)S(1)}, u32[]{:S(2)}, u32[]{:S(2)}) collective-permute-start(f32[240,128]{1,0:T(8,128)S(1)} %get-tuple-element.16), channel_id=1, source_target_pairs={{16,32},{48,64},{80,96},{112,128},{144,160},{176,192},{208,224},{2... | collective-permute-start | bytes 368648 | tf_op jit(solution)/shard_map/ppermute | solution.py:381
  16.0 0.4 shard_map.62.wide
  16.4 2.0 %all-gather = f32[480,128]{1,0:T(8,128)S(1)} all-gather(f32[240,128]{1,0:T(8,128)S(1)} %get-tuple-element.15), channel_id=2, replica_groups={{0,16},{32,48},{64,80},{96,112},{128,144},{160,176},{192,208},{224,240}..., dimensions={0}, use_global_device_ids=true | all-gather | bytes 368640 | tf_op jit(solution)/shard_map/all_gather | solution.py:404
  18.4 0.2 collective-permute-done.2.from_far
  18.6 2.7 %shard_map.63 = (f32[32,128]{1,0:T(8,128)S(1)}, f32[3,2,16,16,256]{4,3,2,1,0:T(8,128)S(1)}, f32[2,16,16,256]{3,2,1,0:T(8,128)S(1)}) custom-call(f32[6,16,8,256]{3,2,1,0:T(8,128)S(1)} %shard_map.62.wide, f32[2,240,128]{2,1,0:T(8,128)S(1)} %bitcast.9, f32[240,128]{1,0:T(8,128)S(1)} %collective-permute-done.2.from_far), custom_call_target="tpu_custom_call" | custom-call | tf_op jit(solution)/shard_map/pallas_call | solution.py:363
  21.3 14.6 %all_to_all.22 = f32[32,1,128]{2,1,0:T(1,128)S(1)} all-to-all(f32[32,1,128]{2,1,0:T(1,128)S(1)} %bitcast.13), channel_id=1, replica_groups=mesh['gx'=32,'gy'=16] {'gx'}, dimensions={0} | all-to-all | bytes 32768 | tf_op jit(solution)/shard_map/all_to_all | solution.py:410
  35.9 24.5 %all_to_all.23 = f32[16,1,128]{2,1,0:T(1,128)S(1)} all-to-all(f32[16,1,128]{2,1,0:T(1,128)S(1)} %bitcast.12), channel_id=1, replica_groups=mesh['gx'=32,'gy'=16] {'gy'}, dimensions={0} | all-to-all | bytes 16384 | tf_op jit(solution)/shard_map/all_to_all | solution.py:412
  60.5 1.1 %shard_map.65 = (f32[2,16,8,128]{3,2,1,0:T(8,128)}, f32[16,8,128]{2,1,0:T(8,128)}) custom-call(f32[16,128]{1,0:T(8,128)S(1)} %bitcast.11, f32[3,2,16,16,256]{4,3,2,1,0:T(8,128)S(1)} %get-tuple-element.18.basis, f32[2,16,16,256]{3,2,1,0:T(8,128)S(1)} %get-tuple-element.19.pots), custom_call_target="tpu_custom_call" | custom-call | tf_op jit(solution)/shard_map/pallas_call | solution.py:363
  (2 shorter events, 0.0 us)
Async XLA Ops:
  2.1 7.9 %collective-permute-start = (f32[16,128]{1,0:T(8,128)S(1)}, f32[16,128]{1,0:T(8,128)S(1)}, u32[]{:S(2)}, u32[]{:S(2)}) collective-permute-start(f32[16,128]{1,0:T(8,128)S(1)} %get-tuple-element.13.sent_second), channel_id=1, source_target_pairs={{1,2},{3,4},{5,6},{7,8},{9,10},{11,12},{13,14},{2,1},{4,3},{6,5},{... | collective-permute-start | bytes 24584 | tf_op jit(solution)/shard_map/ppermute | solution.py:381
  2.8 8.3 %collective-permute-start.1 = (f32[16,128]{1,0:T(8,128)S(1)}, f32[16,128]{1,0:T(8,128)S(1)}, u32[]{:S(2)}, u32[]{:S(2)}) collective-permute-start(f32[16,128]{1,0:T(8,128)S(1)} %get-tuple-element.12.sent_first), channel_id=1, source_target_pairs={{0,1},{2,3},{4,5},{6,7},{8,9},{10,11},{12,13},{14,15},{1,0},{3,2},... | collective-permute-start | bytes 24584 | tf_op jit(solution)/shard_map/ppermute | solution.py:381
  11.1 7.5 %collective-permute-start.2 = (f32[240,128]{1,0:T(8,128)S(1)}, f32[240,128]{1,0:T(8,128)S(1)}, u32[]{:S(2)}, u32[]{:S(2)}) collective-permute-start(f32[240,128]{1,0:T(8,128)S(1)} %get-tuple-element.16), channel_id=1, source_target_pairs={{16,32},{48,64},{80,96},{112,128},{144,160},{176,192},{208,224},{2... | collective-permute-start | bytes 368648 | tf_op jit(solution)/shard_map/ppermute | solution.py:381
